TPU v7x, 128 devices: a whole 4x4x4 slice. The times are simulated.
128 devices in a mesh: seq: 4 (over x), req: 32 (over z, y, core).
Axes of the slice: x: 4, y: 4, z: 4, core: 2. Of those that a mesh axis runs over, the one named last changes fastest.
Arguments:
- stream_tokens: bfloat16 [65536, 2048], P(('seq', 'req')), may hold values from -6 to 6
- xbc_weight: bfloat16 [2048, 5120], P(None, ('seq', 'req')), may hold values from -0.125 to 0.125
- step_weight: bfloat16 [2048, 64], replicated, may hold values from -0.125 to 0.125
- conv_weight: float32 [4, 5120], replicated, may hold values from -3 to 3
- conv_bias: float32 [5120], replicated, may hold values from -3 to 3
- step_bias: float32 [64], replicated, may hold values from -6 to -4
- decay_rate: float32 [64], replicated, may hold values from 0.02 to 3
- skip_gain: float32 [64], replicated, may hold values from 0.1 to 0.5
- norm_gain: float32 [4096], replicated, may hold values from 0.5 to 1.5
- segment_ids: int32 [32, 2048], P('req'), may hold values from 0 to 1, never falling along the last dimension, each value on 1 to 1536 neighbouring positions
- page_target: int32 [128, 32], P(('seq', 'req')), may hold values from 0 to 31, each once within a row
Outputs:
- mixer_out: bfloat16 [65536, 4096], P(('seq', 'req'))
Inputs may be any that keep to these rules, and one draw needn't show every extreme that they name: `segment_ids`: along each row the ids never fall; each request holds 512 to 1536 consecutive tokens. `page_target`: each row holds every request group's index once.
All inputs are finite; a program needn't handle non-finite values.
Results may differ from a plain program's by a relative error of at most 0.0066.
Values may be sent and summed in bfloat16 or wider, within the bound.
No kernel may reach another device: no remote copies, remote signals or barrier semaphores. Data moves between devices by JAX's collectives and lax.ppermute only.
A program may use at most 128 MiB of HBM per device.

v0:
```python
from functools import partial

import jax
import jax.numpy as jnp
from jax import lax
from jax.sharding import PartitionSpec as P

HEADS = 64
HEAD_DIM = 64
GROUPS = 4
STATE = 128
KCONV = 4
SPAN = 256
INNER = 4096
XBC = 5120


def shifted(shard, axis, by):
    peers = lax.axis_size(axis)
    pairs = [(i, i + by) for i in range(peers) if 0 <= i + by < peers]
    return lax.ppermute(shard, axis, pairs)


def conv_rows(raw_rows, seg_rows, prev_raw, prev_seg, conv_weight, conv_bias):
    conv_taps = conv_weight.shape[0]
    row_count = raw_rows.shape[0]
    stacked = jnp.concatenate([prev_raw, raw_rows], axis=0).astype(jnp.float32)
    labels = jnp.concatenate([prev_seg, seg_rows], axis=0)
    summed = conv_bias[None, :] + conv_weight[conv_taps - 1][None, :] * stacked[conv_taps - 1 :]
    for offset in range(conv_taps - 1):
        matching = (labels[offset : offset + row_count] == seg_rows).astype(jnp.float32)
        summed = (
            summed
            + conv_weight[offset][None, :]
            * stacked[offset : offset + row_count]
            * matching[:, None]
        )
    return jax.nn.silu(summed).astype(jnp.bfloat16)


def state_readout(c_mat, state_four):
    upper = state_four.astype(jnp.bfloat16)
    lower = (state_four - upper.astype(jnp.float32)).astype(jnp.bfloat16)
    first = jnp.einsum("tgn,ghpn->tghp", c_mat, upper, preferred_element_type=jnp.float32)
    second = jnp.einsum("tgn,ghpn->tghp", c_mat, lower, preferred_element_type=jnp.float32)
    return first + second


def span_step(decay_rate, state, pieces):
    x_heads, b_mat, c_mat, step_size, seg_rows, seg_before = pieces
    span_len, head_count, head_dim = x_heads.shape
    group_count, state_dim = (b_mat.shape[1], b_mat.shape[2])
    per_group = head_count // group_count
    log_decay = jnp.cumsum(-step_size * decay_rate[None, :], axis=0)
    places = jnp.arange(span_len)
    allowed = (seg_rows[:, None] == seg_rows[None, :]) & (places[:, None] >= places[None, :])
    scores = jnp.einsum("tgn,ugn->gtu", c_mat, b_mat, preferred_element_type=jnp.float32)
    spread = log_decay.T[:, :, None] - log_decay.T[:, None, :]
    decays = jnp.where(allowed[None], jnp.exp(jnp.where(allowed[None], spread, 0.0)), 0.0)
    mixing = (
        scores.reshape(group_count, 1, span_len, span_len)
        * decays.reshape(group_count, per_group, span_len, span_len)
        * step_size.T.reshape(group_count, per_group, 1, span_len)
    ).astype(jnp.bfloat16)
    inside = jnp.einsum(
        "ghtu,ughp->tghp",
        mixing,
        x_heads.reshape(span_len, group_count, per_group, head_dim),
        preferred_element_type=jnp.float32,
    )
    keeping = (seg_rows == seg_before).astype(jnp.float32)
    readout = state_readout(c_mat, state.reshape(group_count, per_group, head_dim, state_dim))
    carried = readout * (keeping[:, None] * jnp.exp(log_decay)).reshape(
        span_len, group_count, per_group, 1
    )
    final_seg = seg_rows[span_len - 1]
    tail_weight = (
        jnp.where(
            seg_rows[:, None] == final_seg,
            jnp.exp(log_decay[span_len - 1][None, :] - log_decay),
            0.0,
        )
        * step_size
    )
    weighted = (x_heads.astype(jnp.float32) * tail_weight[:, :, None]).astype(jnp.bfloat16)
    gained = jnp.einsum(
        "ughp,ugn->ghpn",
        weighted.reshape(span_len, group_count, per_group, head_dim),
        b_mat,
        preferred_element_type=jnp.float32,
    )
    passing = jnp.where(final_seg == seg_before, jnp.exp(log_decay[span_len - 1]), 0.0)
    new_state = passing[:, None, None] * state + gained.reshape(head_count, head_dim, state_dim)
    return (new_state, (inside + carried).reshape(span_len, head_count * head_dim))


def normalize(mixed_rows, x_heads, skip_gain, norm_gain):
    combined = mixed_rows + (x_heads.astype(jnp.float32) * skip_gain[None, :, None]).reshape(
        mixed_rows.shape
    )
    power = jnp.mean(combined * combined, axis=-1, keepdims=True)
    return (combined * lax.rsqrt(power + 1e-05) * norm_gain[None, :]).astype(jnp.bfloat16)


def per_device(
    stream_tokens,
    xbc_weight,
    step_weight,
    conv_weight,
    conv_bias,
    step_bias,
    decay_rate,
    skip_gain,
    norm_gain,
    segment_ids,
    page_target,
):
    req_count = lax.axis_size("req")
    tok_rows = stream_tokens.shape[0]
    page_rows = tok_rows // req_count
    targets = page_target[0]
    page_order = jnp.argsort(targets)
    per_group = HEADS // GROUPS

    def outgoing(values):
        return jnp.take(values.reshape(req_count, page_rows, values.shape[1]), page_order, axis=0)

    raw_rows = jnp.dot(
        stream_tokens,
        lax.all_gather(xbc_weight, ("seq", "req"), axis=1, tiled=True),
        preferred_element_type=jnp.float32,
    ).astype(jnp.bfloat16)
    step_raw = jnp.dot(stream_tokens, step_weight, preferred_element_type=jnp.float32).astype(
        jnp.bfloat16
    )
    raw_rows, step_raw = (raw_rows, step_raw)
    raw_in, step_in = (
        lax.all_to_all(outgoing(raw_rows), "req", split_axis=0, concat_axis=0, tiled=True),
        lax.all_to_all(outgoing(step_raw), "req", split_axis=0, concat_axis=0, tiled=True),
    )
    raw_rows = raw_in.reshape(tok_rows, XBC)
    step_raw = step_in.reshape(tok_rows, HEADS)
    seq_at = lax.axis_index("seq")
    full_ids = segment_ids[0]
    padded_ids = jnp.concatenate([jnp.full((KCONV - 1,), -1, jnp.int32), full_ids])
    seg_rows = lax.dynamic_slice_in_dim(full_ids, seq_at * tok_rows, tok_rows)
    prev_ids = lax.dynamic_slice_in_dim(padded_ids, seq_at * tok_rows, KCONV - 1)
    seg_before = prev_ids[KCONV - 2]
    prev_raw = shifted(raw_rows[tok_rows - (KCONV - 1) :], "seq", 1)
    conv_out = conv_rows(raw_rows, seg_rows, prev_raw, prev_ids, conv_weight, conv_bias)
    step_size = jax.nn.softplus(step_raw.astype(jnp.float32) + step_bias[None, :])
    x_heads = conv_out[:, :INNER].reshape(tok_rows, HEADS, HEAD_DIM)
    b_mat = conv_out[:, INNER : INNER + GROUPS * STATE].reshape(tok_rows, GROUPS, STATE)
    c_mat = conv_out[:, INNER + GROUPS * STATE :].reshape(tok_rows, GROUPS, STATE)
    blocks = tok_rows // SPAN
    block_ends = seg_rows.reshape(blocks, SPAN)[:, SPAN - 1]
    before = jnp.concatenate([seg_before[None], block_ends[:-1]])
    pieces = (
        x_heads.reshape(blocks, SPAN, HEADS, HEAD_DIM),
        b_mat.reshape(blocks, SPAN, GROUPS, STATE),
        c_mat.reshape(blocks, SPAN, GROUPS, STATE),
        step_size.reshape(blocks, SPAN, HEADS),
        seg_rows.reshape(blocks, SPAN),
        before,
    )
    local_state, outputs = lax.scan(
        partial(span_step, decay_rate), jnp.zeros((HEADS, HEAD_DIM, STATE), jnp.float32), pieces
    )
    log_decay = jnp.cumsum(-step_size * decay_rate[None, :], axis=0)
    through = jnp.where(seg_rows[tok_rows - 1] == seg_before, jnp.exp(log_decay[tok_rows - 1]), 0.0)
    incoming = jnp.zeros((HEADS, HEAD_DIM, STATE), jnp.float32)
    for relay_turn in range(lax.axis_size("seq") - 1):
        incoming = shifted(
            (through[:, None, None] * incoming + local_state).astype(jnp.bfloat16), "seq", 1
        ).astype(jnp.float32)
    readout = state_readout(c_mat, incoming.reshape(GROUPS, per_group, HEAD_DIM, STATE))
    keeping = (seg_rows == seg_before).astype(jnp.float32)
    factor = keeping[:, None] * jnp.exp(log_decay)
    mixed_rows = outputs.reshape(tok_rows, INNER) + (
        readout * factor.reshape(tok_rows, GROUPS, per_group, 1)
    ).reshape(tok_rows, INNER)
    normed = normalize(mixed_rows, x_heads, skip_gain, norm_gain)
    returned = lax.all_to_all(
        normed.reshape(req_count, page_rows, INNER), "req", split_axis=0, concat_axis=0, tiled=True
    )
    return jnp.take(returned, targets, axis=0).reshape(tok_rows, INNER)


def solution(mesh):
    in_specs = (
        P(("seq", "req"), None),
        P(None, ("seq", "req")),
        P(),
        P(),
        P(),
        P(),
        P(),
        P(),
        P(),
        P("req", None),
        P(("seq", "req"), None),
    )
    out_specs = P(("seq", "req"), None)
    return jax.shard_map(
        per_device, mesh=mesh, in_specs=in_specs, out_specs=out_specs, check_vma=False
    )
```

profile of v0, /device:TPU:1, one launch (start us, length us, event | category | flops | bytes accessed | tf_op | source)
XLA Modules:
  0.0 508.5 jit_solution(1334981604789869834)
XLA Ops:
  15.0 9.6 %all-to-all-start = ((bf16[32,2,512]{2,1,0:T(2,128)(2,1)}), bf16[32,2,512]{2,1,0:T(2,128)(2,1)S(1)}, u32[]{:S(2)}, u32[]{:S(2)}) async-start(bf16[32,2,512]{2,1,0:T(2,128)(2,1)} %reshape.325), calls=%async_computation | async-start | bytes 131072 | tf_op jit(solution)/shard_map/all_to_all | solution.py:139
  24.6 76.2 %all-gather.2.cloned.1.call-done = bf16[2048,5120]{0,1:T(8,128)(2,1)} async-done(((bf16[2048,40]{0,1:T(8,128)(2,1)}), bf16[2048,5120]{0,1:T(8,128)(2,1)}) %all-gather.2.cloned.1.call-update) | async-done | bytes 20971536 | tf_op jit(solution)/shard_map/all_gather | solution.py:130
  100.8 16.7 %convolution_convert_fusion = bf16[512,5120]{1,0:T(8,128)(2,1)} fusion(bf16[512,2048]{1,0:T(8,128)(2,1)S(1)} %copy-done, bf16[2048,5120]{0,1:T(8,128)(2,1)} %all-gather.2.cloned.1.call-done), kind=kOutput, calls=%fused_computation.74 | convolution fusion | flops 10740039680 | bytes 28311552 | tf_op jit(solution)/shard_map/dot_general | solution.py:128
  117.5 5.7 %gather_fusion.1 = bf16[32,16,5120]{2,1,0:T(8,128)(2,1)} fusion(bf16[32,16,5120]{2,1,0:T(8,128)(2,1)} %bitcast.212, s32[1024]{0:T(1024)S(1)} %pad_clamp_fusion.1), kind=kCustom, calls=%fused_computation.1 | custom fusion | bytes 10485888 | tf_op jit(solution)/shard_map/jit(_take)/gather | solution.py:126
  123.1 5.3 %broadcast_select_fusion.2 = bf16[32,16,5120]{2,1,0:T(8,128)(2,1)} fusion(bf16[32,16,5120]{2,1,0:T(8,128)(2,1)} %gather_fusion.1, pred[32]{0:T(512)(128)(4,1)S(1)} %get-tuple-element.157), kind=kLoop, calls=%fused_computation.76 | loop fusion | flops 2621440 | bytes 10485792 | tf_op jit(solution)/shard_map/jit(_take)/select_n | solution.py:126
  128.5 6.4 %all-to-all-start.1 = ((bf16[32,16,5120]{2,1,0:T(8,128)(2,1)}), bf16[32,16,5120]{2,1,0:T(8,128)(2,1)}, u32[]{:S(2)}, u32[]{:S(2)}) async-start(bf16[32,16,5120]{2,1,0:T(8,128)(2,1)} %broadcast_select_fusion.2), calls=%async_computation.1 | async-start | bytes 10485760 | tf_op jit(solution)/shard_map/all_to_all | solution.py:138
  144.4 52.4 %all-to-all-done.1 = bf16[32,16,5120]{2,1,0:T(8,128)(2,1)} async-done(((bf16[32,16,5120]{2,1,0:T(8,128)(2,1)}), bf16[32,16,5120]{2,1,0:T(8,128)(2,1)}, u32[]{:S(2)}, u32[]{:S(2)}) %all-to-all-start.1) | async-done | bytes 5242912 | tf_op jit(solution)/shard_map/all_to_all | solution.py:138
  201.1 4.0 maximum_convert_fusion
  205.2 8.3 %multiply_convert_fusion.6 = bf16[512,5120]{1,0:T(8,128)(2,1)S(1)} fusion(f32[515,5120]{1,0:T(8,128)S(1)} %maximum_convert_fusion, f32[512]{0:T(512)S(1)} %get-tuple-element.154, f32[5120]{0:T(1024)S(1)} %bitcast.222, f32[512]{0:T(512)S(1)} %get-tuple-element.155, f32[5120]{0:T(1024)S(1)} %bitcast.223, f32[512]{0:T(512)S(1)} %get-tuple-element.153, ...), kind=kLoop, calls=%fused_computation.68 | loop fusion | flops 41943040 | bytes 47294464 | tf_op jit(solution)/shard_map/convert_element_type | solution.py:38
  217.2 12.8 %reshape.309 = bf16[2,256,64,64]{3,2,1,0:T(8,128)(2,1)} reshape(bf16[512,4096]{1,0:T(8,128)(2,1)} %slice.123) | data formatting | bytes 8388608 | tf_op jit(solution)/shard_map/reshape;reshape | solution.py:159
  230.0 10.5 %copy.43 = bf16[2,256,64,64]{1,3,2,0:T(8,128)(2,1)} copy(bf16[2,256,64,64]{3,2,1,0:T(8,128)(2,1)} %reshape.309) | data formatting | bytes 8388608
  240.7 76.9 %while.13 = (s32[]{:T(128)}, f32[64,64,128]{2,1,0:T(8,128)}, f32[2,256,4096]{2,1,0:T(8,128)}, s32[2,256]{1,0:T(2,128)S(1)}, s32[2]{0:T(128)S(1)}, /*index=5*/f32...) while((s32[]{:T(128)}, f32[64,64,128]{2,1,0:T(8,128)}, ...), condition=%wide.region_4.5_spmd.clone, body=%wide.region_1.0_spmd.clone.sunk | while | flops 1447363584 | bytes 79509296 | solution.py:166
  259.3 9.3 %fusion.92 = f32[256,4,16,64]{0,3,2,1:T(8,128)} fusion(f32[4,16,64,256]{3,2,1,0:T(8,128)} %fusion.88, f32[4,256,16,64]{1,3,2,0:T(8,128)} %fusion.89, bf16[256,4,16,64]{0,3,2,1:T(8,128)(2,1)} %bitcast.199, f32[4,16,256]{2,1,0:T(8,128)S(1)} %bitcast.206, f32[4,16,256]{2,1,0:T(8,128)S(1)} %reduce_window_sum.61, f32[4,256,256]{2,1,0:T(8,128)S(1)} %fusion.90, ...), kind=kOutput, calls=%fused_computation.13.clone.1 | convolution fusion | flops 565182464 | bytes 15990784 | tf_op jit(solution)/shard_map/while/body/eval_jaxpr/ghtu,ughp->tghp/dot_general | solution.py:65
  268.6 5.6 %copy.125 = f32[1,256,4096]{2,1,0:T(8,128)} copy(f32[1,256,4096]{1,2,0:T(8,128)} %bitcast.200) | data formatting | bytes 8388608 | tf_op jit(solution)/shard_map/while/body/jit(dynamic_update_index_in_dim)/dynamic_update_slice | solution.py:166
  274.2 4.7 constant_dynamic-update-slice_fusion.2
  298.0 9.3 %fusion.92 = f32[256,4,16,64]{0,3,2,1:T(8,128)} fusion(f32[4,16,64,256]{3,2,1,0:T(8,128)} %fusion.88, f32[4,256,16,64]{1,3,2,0:T(8,128)} %fusion.89, bf16[256,4,16,64]{0,3,2,1:T(8,128)(2,1)} %bitcast.199, f32[4,16,256]{2,1,0:T(8,128)S(1)} %bitcast.206, f32[4,16,256]{2,1,0:T(8,128)S(1)} %reduce_window_sum.61, f32[4,256,256]{2,1,0:T(8,128)S(1)} %fusion.90, ...), kind=kOutput, calls=%fused_computation.13.clone.1 | convolution fusion | flops 565182464 | bytes 15990784 | tf_op jit(solution)/shard_map/while/body/eval_jaxpr/ghtu,ughp->tghp/dot_general | solution.py:65
  307.3 5.6 %copy.125 = f32[1,256,4096]{2,1,0:T(8,128)} copy(f32[1,256,4096]{1,2,0:T(8,128)} %bitcast.200) | data formatting | bytes 8388608 | tf_op jit(solution)/shard_map/while/body/jit(dynamic_update_index_in_dim)/dynamic_update_slice | solution.py:166
  313.0 4.7 constant_dynamic-update-slice_fusion.2
  319.7 3.9 collective-permute-start.1
  323.6 16.8 %collective-permute-done.1 = bf16[64,64,128]{2,1,0:T(8,128)(2,1)S(1)} collective-permute-done((bf16[64,64,128]{2,1,0:T(8,128)(2,1)S(1)}, bf16[64,64,128]{2,1,0:T(8,128)(2,1)S(1)}, u32[]{:S(2)}, u32[]{:S(2)}) %collective-permute-start.1) | collective-permute-done | bytes 1048608 | tf_op jit(solution)/shard_map/ppermute | solution.py:21
  342.4 4.2 collective-permute-start.2
  346.5 16.1 %collective-permute-done.2 = bf16[64,64,128]{2,1,0:T(8,128)(2,1)S(1)} collective-permute-done((bf16[64,64,128]{2,1,0:T(8,128)(2,1)S(1)}, bf16[64,64,128]{2,1,0:T(8,128)(2,1)S(1)}, u32[]{:S(2)}, u32[]{:S(2)}) %collective-permute-start.2) | collective-permute-done | bytes 1048608 | tf_op jit(solution)/shard_map/ppermute | solution.py:21
  364.0 4.2 collective-permute-start.3
  368.7 15.7 %collective-permute-done.3 = bf16[64,64,128]{2,1,0:T(8,128)(2,1)S(1)} collective-permute-done((bf16[64,64,128]{2,1,0:T(8,128)(2,1)}, bf16[64,64,128]{2,1,0:T(8,128)(2,1)S(1)}, u32[]{:S(2)}, u32[]{:S(2)}) %collective-permute-start.3) | collective-permute-done | bytes 1048608 | tf_op jit(solution)/shard_map/ppermute | solution.py:21
  385.6 4.6 bitcast_multiply_fusion.1
  390.2 9.1 %copy.53 = f32[512,4096]{1,0:T(8,128)} copy(f32[512,4096]{0,1:T(8,128)} %bitcast.203) | data formatting | bytes 16777216 | tf_op jit(solution)/shard_map/reshape | solution.py:181
  399.2 8.1 %multiply_reduce_fusion = f32[512]{0:T(512)S(1)} fusion(f32[4096]{0:T(1024)S(1)} %mul.252, f32[512,4096]{1,0:T(8,128)} %copy.53, f32[2,256,4096]{2,1,0:T(8,128)} %get-tuple-element.60, bf16[512,5120]{1,0:T(8,128)(2,1)} %copy-done.5), kind=kLoop, calls=%fused_computation.73 | loop fusion | flops 12582400 | bytes 20989952 | tf_op jit(solution)/shard_map/reduce_sum | solution.py:101
  409.9 6.1 %multiply_convert_fusion.7 = bf16[512,4096]{1,0:T(8,128)(2,1)} fusion(f32[4096]{0:T(1024)S(1)} %copy-done.17, f32[512]{0:T(512)S(1)} %add_rsqrt_fusion, f32[4096]{0:T(1024)S(1)} %mul.252, f32[512,4096]{1,0:T(8,128)S(1)} %copy-done.4, f32[2,256,4096]{2,1,0:T(8,128)} %get-tuple-element.60, bf16[512,5120]{1,0:T(8,128)(2,1)S(1)} %bitcast.202), kind=kLoop, calls=%fused_computation.72 | loop fusion | flops 14680064 | bytes 25200640 | tf_op jit(solution)/shard_map/convert_element_type | solution.py:102
  416.0 25.2 %all-to-all-start.2 = ((bf16[32,16,4096]{2,1,0:T(8,128)(2,1)}), bf16[32,16,4096]{2,1,0:T(8,128)(2,1)}, u32[]{:S(2)}, u32[]{:S(2)}) async-start(bf16[32,16,4096]{2,1,0:T(8,128)(2,1)} %bitcast.204), calls=%async_computation.2 | async-start | bytes 8388608 | tf_op jit(solution)/shard_map/all_to_all | solution.py:183
  441.4 50.5 %all-to-all-done.2 = bf16[32,16,4096]{2,1,0:T(8,128)(2,1)} async-done(((bf16[32,16,4096]{2,1,0:T(8,128)(2,1)}), bf16[32,16,4096]{2,1,0:T(8,128)(2,1)}, u32[]{:S(2)}, u32[]{:S(2)}) %all-to-all-start.2) | async-done | bytes 4194336 | tf_op jit(solution)/shard_map/all_to_all | solution.py:183
  491.9 5.1 %gather_fusion.2 = bf16[32,16,4096]{2,1,0:T(8,128)(2,1)} fusion(bf16[32,16,4096]{2,1,0:T(8,128)(2,1)} %all-to-all-done.2, s32[1024]{0:T(1024)S(1)} %pad_clamp_fusion), kind=kCustom, calls=%fused_computation.2 | custom fusion | bytes 8388736 | tf_op jit(solution)/shard_map/jit(_take)/gather | solution.py:186
  497.0 4.6 bitcast_select_fusion
  (173 shorter events, 69.4 us)
Async XLA Ops:
  6.5 94.2 %all-gather.2.cloned.1.call-start = ((), (), s32[]{:S(2)}) async-start(), calls=%async_computation.3 | async-start | bytes 21135360 | tf_op jit(solution)/shard_map/all_gather | solution.py:130
  15.0 113.5 %all-to-all-start = ((bf16[32,2,512]{2,1,0:T(2,128)(2,1)}), bf16[32,2,512]{2,1,0:T(2,128)(2,1)S(1)}, u32[]{:S(2)}, u32[]{:S(2)}) async-start(bf16[32,2,512]{2,1,0:T(2,128)(2,1)} %reshape.325), calls=%async_computation | async-start | bytes 131072 | tf_op jit(solution)/shard_map/all_to_all | solution.py:139
  128.5 6.5 %copy-start.18 = (s32[1,2048]{1,0:T(1,128)S(1)}, s32[1,2048]{1,0:T(1,128)}, u32[]{:S(2)}) copy-start(s32[1,2048]{1,0:T(1,128)} %param.22) | copy-start | bytes 24580
  128.5 13.4 %copy-start.12 = (f32[4,5120]{1,0:T(4,128)S(1)}, f32[4,5120]{1,0:T(4,128)}, u32[]{:S(2)}) copy-start(f32[4,5120]{1,0:T(4,128)} %param.16) | copy-start | bytes 245764
  128.5 13.7 %copy-start.14 = (f32[64]{0:T(128)S(1)}, f32[64]{0:T(128)}, u32[]{:S(2)}) copy-start(f32[64]{0:T(128)} %param.19) | copy-start | bytes 772
  128.5 13.7 %copy-start.22 = (f32[64]{0:T(128)S(1)}, f32[64]{0:T(128)}, u32[]{:S(2)}) copy-start(f32[64]{0:T(128)} %param.18) | copy-start | bytes 772
  128.5 68.3 %all-to-all-start.1 = ((bf16[32,16,5120]{2,1,0:T(8,128)(2,1)}), bf16[32,16,5120]{2,1,0:T(8,128)(2,1)}, u32[]{:S(2)}, u32[]{:S(2)}) async-start(bf16[32,16,5120]{2,1,0:T(8,128)(2,1)} %broadcast_select_fusion.2), calls=%async_computation.1 | async-start | bytes 10485760 | tf_op jit(solution)/shard_map/all_to_all | solution.py:138
  143.7 61.5 %copy-start.10 = (f32[64,4,128]{2,0,1:T(8,128)}, f32[64,4,128]{2,0,1:T(8,128)S(1)}, u32[]{:S(2)}) copy-start(f32[64,4,128]{2,0,1:T(8,128)S(1)} %reduce-window.16) | copy-start | bytes 393220
  143.9 52.9 %copy-start.15 = (f32[64,4]{0,1:T(4,128)}, f32[64,4]{0,1:T(4,128)S(1)}, u32[]{:S(2)}) copy-start(f32[64,4]{0,1:T(4,128)S(1)} %slice.103) | copy-start | bytes 3076
  144.2 56.0 %copy-start.20 = (f32[64]{0:T(128)}, f32[64]{0:T(128)S(1)}, u32[]{:S(2)}) copy-start(f32[64]{0:T(128)S(1)} %fusion.42) | copy-start | bytes 772
  197.7 3.4 collective-permute-start
  217.2 23.4 %copy-start.8 = (bf16[512,512]{1,0:T(8,128)(2,1)}, bf16[512,512]{1,0:T(8,128)(2,1)S(1)}, u32[]{:S(2)}) copy-start(bf16[512,512]{1,0:T(8,128)(2,1)S(1)} %get-tuple-element.148) | copy-start | bytes 1572868
  240.7 77.0 %copy-start.26 = (f32[64]{0:T(128)S(1)}, f32[64]{0:T(128)}, u32[]{:S(2)}) copy-start(f32[64]{0:T(128)} %broadcast_multiply_fusion) | copy-start | bytes 772
  240.7 99.7 %copy-start.21 = (f32[64]{0:T(128)S(1)}, f32[64]{0:T(128)}, u32[]{:S(2)}) copy-start(f32[64]{0:T(128)} %copy-done.20) | copy-start | bytes 772
  313.0 4.7 copy-start.7
  317.7 45.0 %copy-start.3 = (f32[64,64,128]{2,1,0:T(8,128)S(1)}, f32[64,64,128]{2,1,0:T(8,128)}, u32[]{:S(2)}) copy-start(f32[64,64,128]{2,1,0:T(8,128)} %get-tuple-element.61) | copy-start | bytes 6291460
  317.7 50.5 %copy-start.24 = (f32[64]{0:T(128)S(1)}, f32[64]{0:T(128)}, u32[]{:S(2)}) copy-start(f32[64]{0:T(128)} %param.20) | copy-start | bytes 772
  317.7 50.6 %copy-start.11 = (f32[64,4,128]{2,0,1:T(8,128)S(1)}, f32[64,4,128]{2,0,1:T(8,128)}, u32[]{:S(2)}) copy-start(f32[64,4,128]{2,0,1:T(8,128)} %copy-done.10) | copy-start | bytes 393220
  317.7 50.6 %copy-start.16 = (f32[64,4]{0,1:T(4,128)S(1)}, f32[64,4]{0,1:T(4,128)}, u32[]{:S(2)}) copy-start(f32[64,4]{0,1:T(4,128)} %copy-done.15) | copy-start | bytes 3076
  317.7 50.6 %copy-start.19 = (f32[512]{0:T(512)S(1)}, f32[512]{0:T(512)}, u32[]{:S(2)}) copy-start(f32[512]{0:T(512)} %get-tuple-element.156) | copy-start | bytes 6148
  317.7 50.7 %copy-start.9 = (bf16[512,512]{1,0:T(8,128)(2,1)S(1)}, bf16[512,512]{1,0:T(8,128)(2,1)}, u32[]{:S(2)}) copy-start(bf16[512,512]{1,0:T(8,128)(2,1)} %copy-done.8) | copy-start | bytes 1572868
  319.7 20.7 %collective-permute-start.1 = (bf16[64,64,128]{2,1,0:T(8,128)(2,1)S(1)}, bf16[64,64,128]{2,1,0:T(8,128)(2,1)S(1)}, u32[]{:S(2)}, u32[]{:S(2)}) collective-permute-start(bf16[64,64,128]{2,1,0:T(8,128)(2,1)S(1)} %add_convert_fusion.2), channel_id=1, source_target_pairs={{0,32},{32,64},{64,96},{1,33},{33,65},{65,97},{2,34},{34,66},{66,9... | collective-permute-start | bytes 3145736 | tf_op jit(solution)/shard_map/ppermute | solution.py:21
  342.4 20.3 %collective-permute-start.2 = (bf16[64,64,128]{2,1,0:T(8,128)(2,1)S(1)}, bf16[64,64,128]{2,1,0:T(8,128)(2,1)S(1)}, u32[]{:S(2)}, u32[]{:S(2)}) collective-permute-start(bf16[64,64,128]{2,1,0:T(8,128)(2,1)S(1)} %add_convert_fusion.1), channel_id=1, source_target_pairs={{0,32},{32,64},{64,96},{1,33},{33,65},{65,97},{2,34},{34,66},{66,9... | collective-permute-start | bytes 3145736 | tf_op jit(solution)/shard_map/ppermute | solution.py:21
  364.0 20.4 %collective-permute-start.3 = (bf16[64,64,128]{2,1,0:T(8,128)(2,1)}, bf16[64,64,128]{2,1,0:T(8,128)(2,1)S(1)}, u32[]{:S(2)}, u32[]{:S(2)}) collective-permute-start(bf16[64,64,128]{2,1,0:T(8,128)(2,1)} %add_convert_fusion), channel_id=1, source_target_pairs={{0,32},{32,64},{64,96},{1,33},{33,65},{65,97},{2,34},{34,66},{66,9... | collective-permute-start | bytes 3145736 | tf_op jit(solution)/shard_map/ppermute | solution.py:21
  390.2 17.2 %slice-start = ((s8[5242880]{0:T(1024)(128)(4,1)}), s8[1048576]{0:T(1024)(128)(4,1)S(1)}, s32[]{:S(2)}) async-start(s8[5242880]{0:T(1024)(128)(4,1)} %bitcast.201), calls=%async_computation.4 | async-start | bytes 2097152
  399.2 9.4 %copy-start.4 = (f32[512,4096]{1,0:T(8,128)S(1)}, f32[512,4096]{1,0:T(8,128)}, u32[]{:S(2)}) copy-start(f32[512,4096]{1,0:T(8,128)} %copy.53) | copy-start | bytes 25165828
  399.2 10.6 %slice-start.1 = ((s8[5242880]{0:T(1024)(128)(4,1)}), s8[4194304]{0:T(1024)(128)(4,1)S(1)}, s32[]{:S(2)}) async-start(s8[5242880]{0:T(1024)(128)(4,1)} %bitcast.201), calls=%async_computation.5 | async-start | bytes 8388608
  399.2 10.6 %copy-start.17 = (f32[4096]{0:T(1024)S(1)}, f32[4096]{0:T(1024)}, u32[]{:S(2)}) copy-start(f32[4096]{0:T(1024)} %param.21) | copy-start | bytes 49156
  416.0 25.2 %copy-start.23 = (pred[32]{0:T(512)(128)(4,1)S(1)}, pred[32]{0:T(512)(128)(4,1)}, u32[]{:S(2)}) copy-start(pred[32]{0:T(512)(128)(4,1)} %get-tuple-element.158) | copy-start | bytes 100
  416.0 25.3 %copy-start.25 = (s32[1,32]{1,0:T(1,128)S(1)}, s32[1,32]{1,0:T(1,128)}, u32[]{:S(2)}) copy-start(s32[1,32]{1,0:T(1,128)} %param.23) | copy-start | bytes 388
  416.0 75.8 %all-to-all-start.2 = ((bf16[32,16,4096]{2,1,0:T(8,128)(2,1)}), bf16[32,16,4096]{2,1,0:T(8,128)(2,1)}, u32[]{:S(2)}, u32[]{:S(2)}) async-start(bf16[32,16,4096]{2,1,0:T(8,128)(2,1)} %bitcast.204), calls=%async_computation.2 | async-start | bytes 8388608 | tf_op jit(solution)/shard_map/all_to_all | solution.py:183
  491.9 9.8 %copy-start.1 = (bf16[512,2048]{1,0:T(8,128)(2,1)S(1)}, bf16[512,2048]{1,0:T(8,128)(2,1)}, u32[]{:S(2)}) copy-start(bf16[512,2048]{1,0:T(8,128)(2,1)} %param.13) | copy-start | bytes 6291460
  (8 other events, 29.3 us)
Sparse Core Ops, SparseCore 0:
  10.2 90.5 all-gather.1
where the time goes:
time: 513 us; the launch traced here: 508 us
  waiting for transfers between devices  229 us (45%)
  local copies, waits for them, and re-layouts  85.3 us (17%)
  other arithmetic  62.4 us (12%)
  matrix products  58.2 us (11%)
  starting transfers between devices  55.9 us (11%)
  between operations  15.1 us (3%)
    all_gather x1, waiting for transfers between devices, per_device(): lax.all_gather(xbc_weight, ('seq', 'req'), axis=1, tiled=True)  76.2 us
    all_to_all x1, waiting for transfers between devices, per_device(): lax.all_to_all(outgoing(raw_rows), 'req', split_axis=0, concat_axis=0, ti...  52.4 us
    all_to_all x1, waiting for transfers between devices, per_device(): lax.all_to_all(normed.reshape(req_count, page_rows, INNER), 'req', split_...  50.5 us
    ppermute x4, waiting for transfers between devices, shifted(): return lax.ppermute(shard, axis, pairs)  48.9 us
    all_to_all x1, starting transfers between devices, per_device(): lax.all_to_all(normed.reshape(req_count, page_rows, INNER), 'req', split_...  25.2 us
    dynamic_update_slice x4, local copies, waits for them, and re-layouts, per_device(): lax.scan(partial(span_step, decay_rate), jnp.zeros((HEADS, HEAD_DIM, STAT...  20.6 us
    dot_general x2, matrix products, span_step(): jnp.einsum('ghtu,ughp->tghp', mixing, x_heads.reshape(span_len, group_cou...  18.6 us
    dot_general x1, matrix products, per_device(): jnp.dot(stream_tokens, lax.all_gather(xbc_weight, ('seq', 'req'), axis=1,...  16.7 us
  transfers between devices with their start and end apart: 8, of which 7 were waited for; matrix products, arithmetic and copies ran while one was open for 9% of the time, Pallas kernels for 0%

commit v1 on v0

v1 whole, which is shorter than its diff:
```python
from functools import partial

import jax
import jax.numpy as jnp
import numpy as np
from jax import lax
from jax.experimental import pallas as pl
from jax.experimental.pallas import tpu as pltpu
from jax.sharding import Mesh, PartitionSpec as P

HEAD_DIM = 64
STATE = 128
KCONV = 4
SPAN = 256
INNER = 4096
XBC = 5120
D = 2048
CORES = 2
HEADS = 32
GROUPS = 2
HALF = 2048
BC = GROUPS * STATE
OWN = HALF + 2 * BC
UNIT = 8
PIECE = 5
DEVICES = 128


def unit_of(core, at):
    x_units, bc_units = HALF // UNIT, BC // UNIT
    if at < x_units:
        return x_units * core + at
    if at < x_units + bc_units:
        return INNER // UNIT + bc_units * core + (at - x_units)
    return (INNER + 2 * BC) // UNIT + bc_units * core + (at - x_units - bc_units)


def weight_moves():
    wanted = [
        [divmod(unit_of(d % 2, PIECE * (d // 2) + k), PIECE) for k in range(PIECE)]
        for d in range(DEVICES)
    ]
    edges = sorted({(source, d) for d in range(DEVICES) for source, _ in wanted[d]})
    sent = [{} for _ in range(DEVICES)]
    got = [{} for _ in range(DEVICES)]

    def free(table):
        return next(k for k in range(DEVICES) if k not in table)

    for source, d in edges:
        a, b = free(sent[source]), free(got[d])
        if a != b:
            path, at, tables, other, colour = [], d, got, sent, a
            while colour in tables[at]:
                nxt = tables[at][colour]
                path.append((nxt, at, colour) if tables is got else (at, nxt, colour))
                at, tables, other = nxt, other, tables
                colour = b if colour == a else a
            for s, t, colour in path:
                del sent[s][colour]
                del got[t][colour]
            for s, t, colour in path:
                sent[s][a + b - colour] = t
                got[t][a + b - colour] = s
        sent[source][a] = d
        got[d][a] = source
    rounds = 1 + max(k for table in got for k in table)
    pairs = [[(got[d][k], d) for d in range(DEVICES) if k in got[d]] for k in range(rounds)]
    picks = np.zeros((DEVICES, PIECE), np.int32)
    for d in range(DEVICES):
        where = {source: k for k, source in got[d].items()}
        picks[d] = [where[source] * PIECE + slot for source, slot in wanted[d]]
    return pairs, picks


ALL = ("seq", "chip", "core")
REQ = ("chip", "core")


def move(index_ref, source_ref, out_ref, sems, *, places):
    copies = []
    for k, (source, target) in enumerate(places(index_ref)):
        copies.append(
            pltpu.make_async_copy(source_ref.at[source], out_ref.at[target], sems.at[k])
        )
    for copy in copies:
        copy.start()
    for copy in copies:
        copy.wait()


def scatter_pages(pages, targets):
    count = pages.shape[0]
    return pl.pallas_call(
        partial(move, places=lambda index: [(k, index[k]) for k in range(count)]),
        out_shape=jax.ShapeDtypeStruct(pages.shape, pages.dtype),
        in_specs=[pl.BlockSpec(memory_space=pltpu.SMEM), pl.BlockSpec(memory_space=pl.ANY)],
        out_specs=pl.BlockSpec(memory_space=pl.ANY),
        scratch_shapes=[pltpu.SemaphoreType.DMA((count,))],
        name="scatter_pages",
    )(targets, pages)


def pick_units(units, picks):
    count = picks.shape[0]
    return pl.pallas_call(
        partial(move, places=lambda index: [(index[k], k) for k in range(count)]),
        out_shape=jax.ShapeDtypeStruct((count,) + units.shape[1:], units.dtype),
        in_specs=[pl.BlockSpec(memory_space=pltpu.SMEM), pl.BlockSpec(memory_space=pl.ANY)],
        out_specs=pl.BlockSpec(memory_space=pl.ANY),
        scratch_shapes=[pltpu.SemaphoreType.DMA((count,))],
        name="pick_units",
    )(picks, units)


def join_kernel(target_ref, own_ref, other_ref, out_ref, sems):
    copies = []
    for k in range(own_ref.shape[0]):
        group = target_ref[k]
        for part, (pages, page) in enumerate(((own_ref, group), (other_ref, group ^ 1))):
            half = (group & 1) ^ part
            copies.append(
                pltpu.make_async_copy(
                    pages.at[page],
                    out_ref.at[k, :, pl.ds(pl.multiple_of(half * HALF, HALF), HALF)],
                    sems.at[2 * k + part],
                )
            )
    for copy in copies:
        copy.start()
    for copy in copies:
        copy.wait()


def join_pages(own, other, targets):
    count, rows, width = own.shape
    return pl.pallas_call(
        join_kernel,
        out_shape=jax.ShapeDtypeStruct((count, rows, 2 * width), own.dtype),
        in_specs=[pl.BlockSpec(memory_space=pltpu.SMEM)] + [pl.BlockSpec(memory_space=pl.ANY)] * 2,
        out_specs=pl.BlockSpec(memory_space=pl.ANY),
        scratch_shapes=[pltpu.SemaphoreType.DMA((2 * count,))],
        name="join_pages",
    )(targets, own, other)


def conv_rows(stacked, labels, conv_weight, conv_bias):
    row_count = stacked.shape[0] - (KCONV - 1)
    stacked = stacked.astype(jnp.float32)
    seg_rows = labels[KCONV - 1 :]
    summed = conv_bias[None, :] + conv_weight[KCONV - 1][None, :] * stacked[KCONV - 1 :]
    for offset in range(KCONV - 1):
        matching = (labels[offset : offset + row_count] == seg_rows).astype(jnp.float32)
        summed = (
            summed
            + conv_weight[offset][None, :]
            * stacked[offset : offset + row_count]
            * matching[:, None]
        )
    return jax.nn.silu(summed).astype(jnp.bfloat16)


def state_readout(c_mat, state_four):
    upper = state_four.astype(jnp.bfloat16)
    lower = (state_four - upper.astype(jnp.float32)).astype(jnp.bfloat16)
    first = jnp.einsum("tgn,ghpn->tghp", c_mat, upper, preferred_element_type=jnp.float32)
    second = jnp.einsum("tgn,ghpn->tghp", c_mat, lower, preferred_element_type=jnp.float32)
    return first + second


def span_step(decay_rate, state, pieces):
    x_heads, b_mat, c_mat, step_size, seg_rows, seg_before = pieces
    span_len, head_count, head_dim = x_heads.shape
    group_count, state_dim = (b_mat.shape[1], b_mat.shape[2])
    per_group = head_count // group_count
    log_decay = jnp.cumsum(-step_size * decay_rate[None, :], axis=0)
    places = jnp.arange(span_len)
    allowed = (seg_rows[:, None] == seg_rows[None, :]) & (places[:, None] >= places[None, :])
    scores = jnp.einsum("tgn,ugn->gtu", c_mat, b_mat, preferred_element_type=jnp.float32)
    spread = log_decay.T[:, :, None] - log_decay.T[:, None, :]
    decays = jnp.where(allowed[None], jnp.exp(jnp.where(allowed[None], spread, 0.0)), 0.0)
    mixing = (
        scores.reshape(group_count, 1, span_len, span_len)
        * decays.reshape(group_count, per_group, span_len, span_len)
        * step_size.T.reshape(group_count, per_group, 1, span_len)
    ).astype(jnp.bfloat16)
    inside = jnp.einsum(
        "ghtu,ughp->tghp",
        mixing,
        x_heads.reshape(span_len, group_count, per_group, head_dim),
        preferred_element_type=jnp.float32,
    )
    keeping = (seg_rows == seg_before).astype(jnp.float32)
    readout = state_readout(c_mat, state.reshape(group_count, per_group, head_dim, state_dim))
    carried = readout * (keeping[:, None] * jnp.exp(log_decay)).reshape(
        span_len, group_count, per_group, 1
    )
    final_seg = seg_rows[span_len - 1]
    tail_weight = (
        jnp.where(
            seg_rows[:, None] == final_seg,
            jnp.exp(log_decay[span_len - 1][None, :] - log_decay),
            0.0,
        )
        * step_size
    )
    weighted = (x_heads.astype(jnp.float32) * tail_weight[:, :, None]).astype(jnp.bfloat16)
    gained = jnp.einsum(
        "ughp,ugn->ghpn",
        weighted.reshape(span_len, group_count, per_group, head_dim),
        b_mat,
        preferred_element_type=jnp.float32,
    )
    passing = jnp.where(final_seg == seg_before, jnp.exp(log_decay[span_len - 1]), 0.0)
    new_state = passing[:, None, None] * state + gained.reshape(head_count, head_dim, state_dim)
    return (new_state, (inside + carried).reshape(span_len, head_count * head_dim))


def request(tokens, halo, labels, weight, step_weight, conv_weight, conv_bias, step_bias, decay_rate, skip_gain):
    tok_rows = tokens.shape[0]
    rows = jnp.concatenate([halo[halo.shape[0] - (KCONV - 1) :], tokens], axis=0)
    raw_rows = lax.dot_general(
        rows, weight, (((1,), (1,)), ((), ())), preferred_element_type=jnp.float32
    ).astype(jnp.bfloat16)
    step_raw = jnp.dot(tokens, step_weight, preferred_element_type=jnp.float32).astype(jnp.bfloat16)
    seg_rows = labels[KCONV - 1 :]
    seg_before = labels[KCONV - 2]
    conv_out = conv_rows(raw_rows, labels, conv_weight, conv_bias)
    step_size = jax.nn.softplus(step_raw.astype(jnp.float32) + step_bias[None, :])
    x_heads = conv_out[:, :HALF].reshape(tok_rows, HEADS, HEAD_DIM)
    b_mat = conv_out[:, HALF : HALF + BC].reshape(tok_rows, GROUPS, STATE)
    c_mat = conv_out[:, HALF + BC :].reshape(tok_rows, GROUPS, STATE)
    blocks = tok_rows // SPAN
    block_ends = seg_rows.reshape(blocks, SPAN)[:, SPAN - 1]
    before = jnp.concatenate([seg_before[None], block_ends[:-1]])
    pieces = (
        x_heads.reshape(blocks, SPAN, HEADS, HEAD_DIM),
        b_mat.reshape(blocks, SPAN, GROUPS, STATE),
        c_mat.reshape(blocks, SPAN, GROUPS, STATE),
        step_size.reshape(blocks, SPAN, HEADS),
        seg_rows.reshape(blocks, SPAN),
        before,
    )
    local_state, outputs = lax.scan(
        partial(span_step, decay_rate), jnp.zeros((HEADS, HEAD_DIM, STATE), jnp.float32), pieces
    )
    log_decay = jnp.cumsum(-step_size * decay_rate[None, :], axis=0)
    through = jnp.where(seg_rows[tok_rows - 1] == seg_before, jnp.exp(log_decay[tok_rows - 1]), 0.0)
    states = lax.all_gather(local_state.astype(jnp.bfloat16), "seq")
    throughs = lax.all_gather(jnp.broadcast_to(through[None, :], (8, HEADS)), "seq")[:, 0]
    here = lax.axis_index("seq")
    incoming = jnp.zeros((HEADS, HEAD_DIM, STATE), jnp.float32)
    for at in range(lax.axis_size("seq") - 1):
        after = throughs[at][:, None, None] * incoming + states[at].astype(jnp.float32)
        incoming = jnp.where(at < here, after, incoming)
    readout = state_readout(c_mat, incoming.reshape(GROUPS, HEADS // GROUPS, HEAD_DIM, STATE))
    keeping = (seg_rows == seg_before).astype(jnp.float32)
    factor = keeping[:, None] * jnp.exp(log_decay)
    mixed_rows = outputs.reshape(tok_rows, HALF) + (
        readout * factor.reshape(tok_rows, GROUPS, HEADS // GROUPS, 1)
    ).reshape(tok_rows, HALF)
    combined = mixed_rows + (x_heads.astype(jnp.float32) * skip_gain[None, :, None]).reshape(
        mixed_rows.shape
    )
    return combined, jnp.sum(combined * combined, axis=-1)


def per_device(
    stream_tokens,
    xbc_weight,
    step_weight,
    conv_weight,
    conv_bias,
    step_bias,
    decay_rate,
    skip_gain,
    norm_gain,
    segment_ids,
    page_target,
):
    groups_of_requests = lax.axis_size("chip") * CORES
    tok_rows = stream_tokens.shape[0]
    page_rows = tok_rows // groups_of_requests
    seq_at, core = lax.axis_index("seq"), lax.axis_index("core")
    flat = (seq_at * lax.axis_size("chip") + lax.axis_index("chip")) * CORES + core
    swap = [(0, 1), (1, 0)]
    peers = lax.axis_size("seq")
    onward = [(i, i + 1) for i in range(peers - 1)]
    onward_swap = [(2 * i + k, 2 * (i + 1) + 1 - k) for i in range(peers - 1) for k in range(2)]

    targets = page_target[0]
    pages = scatter_pages(stream_tokens.reshape(groups_of_requests, page_rows, D), targets)
    own = lax.all_to_all(pages, REQ, split_axis=0, concat_axis=0, tiled=True)
    other = lax.ppermute(own, "core", swap)
    last_page = own[groups_of_requests - 1]
    own_halo = lax.ppermute(last_page, "seq", onward)
    other_halo = lax.ppermute(last_page, ("seq", "core"), onward_swap)
    other_ids = lax.ppermute(segment_ids, "core", swap)

    pairs, picks = weight_moves()
    piece = xbc_weight.T.reshape(PIECE, UNIT, D)
    arrived = jnp.concatenate([lax.ppermute(piece, ALL, moves) for moves in pairs], axis=0)
    units = pick_units(arrived, jnp.asarray(picks)[flat])
    weight = lax.all_gather(units.reshape(PIECE * UNIT, D), ("seq", "chip"), axis=0, tiled=True)

    def columns(values):
        return jnp.concatenate(
            [
                lax.dynamic_slice_in_dim(values, core * HALF, HALF, axis=-1),
                lax.dynamic_slice_in_dim(values, INNER + core * BC, BC, axis=-1),
                lax.dynamic_slice_in_dim(values, INNER + 2 * BC + core * BC, BC, axis=-1),
            ],
            axis=-1,
        )

    def heads(values):
        return lax.dynamic_slice_in_dim(values, core * HEADS, HEADS, axis=-1)

    def labels(ids):
        padded = jnp.concatenate([jnp.full((KCONV - 1,), -1, jnp.int32), ids[0]])
        return lax.dynamic_slice_in_dim(padded, seq_at * tok_rows, tok_rows + KCONV - 1)

    shared = (
        weight,
        heads(step_weight),
        columns(conv_weight),
        columns(conv_bias),
        heads(step_bias),
        heads(decay_rate),
        heads(skip_gain),
    )
    gain = lax.dynamic_slice_in_dim(norm_gain, core * HALF, HALF)
    own_rows, own_power = request(own.reshape(tok_rows, D), own_halo, labels(segment_ids), *shared)
    other_rows, other_power = request(
        other.reshape(tok_rows, D), other_halo, labels(other_ids), *shared
    )
    swapped = lax.ppermute(jnp.stack([own_power, other_power]), "core", swap)

    def sent_back(rows, power):
        mean = power / INNER
        normed = (rows * lax.rsqrt(mean[:, None] + 1e-05) * gain[None, :]).astype(jnp.bfloat16)
        return lax.all_to_all(
            normed.reshape(groups_of_requests, page_rows, HALF),
            REQ,
            split_axis=0,
            concat_axis=0,
            tiled=True,
        )

    own_back = sent_back(own_rows, own_power + swapped[1])
    other_back = sent_back(other_rows, other_power + swapped[0])
    return join_pages(own_back, other_back, targets).reshape(tok_rows, INNER)


def solution(mesh):
    chips = mesh.shape["req"] // CORES
    by_core = Mesh(
        mesh.devices.reshape(mesh.shape["seq"], chips, CORES), ("seq", "chip", "core")
    )
    in_specs = (
        P(ALL, None),
        P(None, ALL),
        P(),
        P(),
        P(),
        P(),
        P(),
        P(),
        P(),
        P(REQ, None),
        P(ALL, None),
    )
    return jax.shard_map(
        per_device, mesh=by_core, in_specs=in_specs, out_specs=P(ALL, None), check_vma=False
    )
```

time: 513 us -> 589 us (1.15)
  Pallas kernels: 0 us -> 202 us
  waiting for transfers between devices: 229 us -> 43.7 us
  blocking collectives: 0 us -> 78.5 us
  starting transfers between devices: 55.9 us -> 26.7 us
  local copies, waits for them, and re-layouts: 85.3 us -> 104 us
  other arithmetic: 62.4 us -> 48.6 us
    pallas_call x0 -> x3, Pallas kernels: none -> 202 us  [the longest x1 129 us: join_pages(): pl.pallas_call(join_kernel, out_shape=jax.ShapeDtypeStruct((count, rows,...]
    all_gather x1 -> x3, waiting for transfers between devices: 76.2 us -> 0.02 us  [the longest x2 0.02 us: request(): states = lax.all_gather(local_state.astype(jnp.bfloat16), 'seq')]
    all_to_all x3 -> x1, waiting for transfers between devices: 103 us -> 32.8 us  [per_device(): own = lax.all_to_all(pages, REQ, split_axis=0, concat_axis=0, tiled=True)]
    all_to_all x0 -> x2, blocking collectives: none -> 64.3 us  [sent_back(): lax.all_to_all(normed.reshape(groups_of_requests, page_rows, HALF), REQ,...]
    ppermute x4 -> x8, waiting for transfers between devices: 48.9 us -> 10.8 us  [the longest x3 10 us: per_device(): lax.ppermute(piece, ALL, moves)]
    all_to_all x3 -> x1, starting transfers between devices: 41.2 us -> 8.48 us  [per_device(): own = lax.all_to_all(pages, REQ, split_axis=0, concat_axis=0, tiled=True)]
    all_gather x0 -> x2, blocking collectives: none -> 14.2 us  [request(): lax.all_gather(jnp.broadcast_to(through[None, :], (8, HEADS)), 'seq')[:, 0]]
    gather x3 -> x0, local copies, waits for them, and re-layouts: 11.4 us -> none  [the longest x2 6.24 us: outgoing(): jnp.take(values.reshape(req_count, page_rows, values.shape[1]), page_orde...]
  transfers between devices with their start and end apart: 8 -> 12, of which waited for: 7 -> 4; matrix products, arithmetic and copies ran while one was open for 9% -> 17% of each run, Pallas kernels for 0% -> 11%
where the time goes in v1:
time: 589 us; the launch traced here: 587 us
  Pallas kernels  202 us (34%)
  local copies, waits for them, and re-layouts  104 us (18%)
  blocking collectives  78.5 us (13%)
  matrix products  61.8 us (10%)
  other arithmetic  48.6 us (8%)
  waiting for transfers between devices  43.7 us (7%)
  starting transfers between devices  26.7 us (5%)
  between operations  16.1 us (3%)
    pallas_call x1, Pallas kernels, join_pages(): pl.pallas_call(join_kernel, out_shape=jax.ShapeDtypeStruct((count, rows,...  129 us
    pallas_call x1, Pallas kernels, scatter_pages(): pl.pallas_call(partial(move, places=lambda index: [(k, index[k]) for k in...  65.7 us
    all_to_all x2, blocking collectives, sent_back(): lax.all_to_all(normed.reshape(groups_of_requests, page_rows, HALF), REQ,...  64.3 us
    all_to_all x1, waiting for transfers between devices, per_device(): own = lax.all_to_all(pages, REQ, split_axis=0, concat_axis=0, tiled=True)  32.8 us
    dot_general x4, matrix products, span_step(): jnp.einsum('ghtu,ughp->tghp', mixing, x_heads.reshape(span_len, group_cou...  23.2 us
    dynamic_slice x24, local copies, waits for them, and re-layouts, request(): lax.scan(partial(span_step, decay_rate), jnp.zeros((HEADS, HEAD_DIM, STAT...  16.7 us
    dot_general x2, matrix products, request(): lax.dot_general(rows, weight, (((1,), (1,)), ((), ())), preferred_element...  15.4 us
    all_gather x2, blocking collectives, request(): lax.all_gather(jnp.broadcast_to(through[None, :], (8, HEADS)), 'seq')[:, 0]  14.2 us
  transfers between devices with their start and end apart: 12, of which 4 were waited for; matrix products, arithmetic and copies ran while one was open for 17% of the time, Pallas kernels for 11%

profile of v1, /device:TPU:1, one launch (start us, length us, event | category | flops | bytes accessed | tf_op | source)
XLA Modules:
  0.0 586.5 jit_solution(16651240193601078481)
XLA Ops:
  6.5 4.7 collective-permute-start.1
  14.5 3.3 collective-permute-done.1
  17.8 6.7 %collective-permute-done.2 = bf16[5,8,2048]{2,1,0:T(8,128)(2,1)S(1)} collective-permute-done((bf16[5,8,2048]{2,1,0:T(8,128)(2,1)}, bf16[5,8,2048]{2,1,0:T(8,128)(2,1)S(1)}, u32[]{:S(2)}, u32[]{:S(2)}) %collective-permute-start.2) | collective-permute-done | bytes 163872 | tf_op jit(solution)/shard_map/ppermute | solution.py:302
  25.4 6.8 %pick_units.1 = bf16[5,8,2048]{2,1,0:T(8,128)(2,1)} custom-call(s32[5]{0:T(128)} %fusion.138.index_ref, bf16[15,8,2048]{2,1,0:T(8,128)(2,1)} %pad_maximum_fusion.source_ref), custom_call_target="tpu_custom_call" | custom-call | tf_op jit(solution)/shard_map/pick_units/pallas_call | solution.py:106
  32.2 65.7 %scatter_pages.1 = bf16[32,16,2048]{2,1,0:T(8,128)(2,1)} custom-call(s32[32]{0:T(128)} %bitcast.455, bf16[32,16,2048]{2,1,0:T(8,128)(2,1)} %bitcast.435), custom_call_target="tpu_custom_call" | custom-call | tf_op jit(solution)/shard_map/scatter_pages/pallas_call | solution.py:94
  98.0 8.5 %all-to-all-start = ((bf16[32,16,2048]{2,1,0:T(8,128)(2,1)}), bf16[32,16,2048]{2,1,0:T(8,128)(2,1)S(1)}, u32[]{:S(2)}, u32[]{:S(2)}) async-start(bf16[32,16,2048]{2,1,0:T(8,128)(2,1)} %scatter_pages.1), calls=%async_computation | async-start | bytes 4194304 | tf_op jit(solution)/shard_map/all_to_all | solution.py:293
  107.5 32.8 %all-to-all-done = bf16[32,16,2048]{2,1,0:T(8,128)(2,1)S(1)} async-done(((bf16[32,16,2048]{2,1,0:T(8,128)(2,1)}), bf16[32,16,2048]{2,1,0:T(8,128)(2,1)S(1)}, u32[]{:S(2)}, u32[]{:S(2)}) %all-to-all-start) | async-done | bytes 2097184 | tf_op jit(solution)/shard_map/all_to_all | solution.py:293
  147.6 3.2 pad_add_fusion
  152.8 3.5 collective-permute-start.6
  167.3 9.7 %fusion.74 = f32[515,2560]{1,0:T(8,128)S(1)} fusion(bf16[2560,2048]{1,0:T(8,128)(2,1)} %all-gather.10.cloned.1.call-done, bf16[512,2048]{1,0:T(8,128)(2,1)} %bitcast.27, bf16[3,2048]{1,0:T(4,128)(2,1)} %slice.335), kind=kOutput, calls=%fused_computation.133 | convolution fusion | flops 5407022080 | bytes 17868800 | tf_op jit(solution)/shard_map/dot_general | solution.py:222
  177.1 5.7 fusion.75
  182.9 8.7 %multiply_convert_fusion.13 = (bf16[512,2560]{1,0:T(8,128)(2,1)S(1)}, bf16[512,2560]{1,0:T(8,128)(2,1)S(1)}) fusion(f32[515,2560]{1,0:T(8,128)S(1)} %fusion.75, f32[512]{0:T(512)S(1)} %get-tuple-element.350, f32[2560]{0:T(1024)S(1)} %copy-done.19, f32[512]{0:T(512)S(1)} %get-tuple-element.351, f32[2560]{0:T(1024)S(1)} %copy-done.20, ...), kind=kLoop, calls=%fused_computation.131 | loop fusion | flops 41943040 | bytes 47249408 | tf_op jit(solution)/shard_map/convert_element_type | solution.py:160
  195.8 5.3 reshape.541
  201.1 5.8 copy.105
  210.9 46.3 %while.26 = (s32[]{:T(128)}, f32[32,64,128]{2,1,0:T(8,128)S(1)}, f32[2,256,2048]{2,1,0:T(8,128)}, s32[2,256]{1,0:T(2,128)}, s32[2]{0:T(128)}, /*index=5*/f32[2,2...) while((s32[]{:T(128)}, f32[32,64,128]{2,1,0:T(8,128)S(1)}, ...), condition=%wide.region_3.4_spmd.clone, body=%wide.region_0.3_spmd.clone.sunk | while | flops 723780480 | bytes 42478156 | solution.py:244
  224.7 5.8 fusion.216
  247.9 5.8 fusion.216
  258.1 7.1 %reshape.542 = bf16[2,256,32,64]{3,2,1,0:T(8,128)(2,1)} reshape(bf16[512,2048]{1,0:T(8,128)(2,1)} %slice.340) | data formatting | bytes 4194304 | tf_op jit(solution)/shard_map/reshape;reshape | solution.py:237
  265.2 6.0 %copy.116 = bf16[2,256,32,64]{1,3,2,0:T(8,128)(2,1)} copy(bf16[2,256,32,64]{3,2,1,0:T(8,128)(2,1)} %reshape.542) | data formatting | bytes 4194304
  275.3 44.1 %while.27 = (s32[]{:T(128)}, f32[32,64,128]{2,1,0:T(8,128)S(1)}, f32[2,256,2048]{2,1,0:T(8,128)}, s32[2,256]{1,0:T(2,128)S(1)}, s32[2]{0:T(128)S(1)}, /*index=5*...) while((s32[]{:T(128)}, f32[32,64,128]{2,1,0:T(8,128)S(1)}, ...), condition=%wide.region_10.11_spmd.clone, body=%wide.region_7.10_spmd.clone.sunk | while | flops 723780480 | bytes 41953880 | solution.py:244
  288.1 5.8 fusion.232
  310.1 5.8 fusion.232
  327.8 6.4 %all-gather.5 = f32[4,1,32]{2,1,0:T(1,128)S(1)} all-gather(f32[1,1,32]{2,1,0:T(1,128)S(1)} %bitcast.457), channel_id=6, replica_groups=mesh['seq'=4,'chip'=16,'core'=2] {'seq'}, dimensions={0}, use_global_device_ids=true | all-gather | bytes 640 | tf_op jit(solution)/shard_map/all_gather | solution.py:250
  334.5 7.8 %all-gather.4 = f32[4,1,32]{2,1,0:T(1,128)S(1)} all-gather(f32[1,1,32]{2,1,0:T(1,128)S(1)} %bitcast.458), channel_id=4, replica_groups=mesh['seq'=4,'chip'=16,'core'=2] {'seq'}, dimensions={0}, use_global_device_ids=true | all-gather | bytes 640 | tf_op jit(solution)/shard_map/all_gather | solution.py:250
  350.6 5.4 copy.113
  361.1 5.6 copy.124
  366.7 7.4 %multiply_reduce_fusion = (f32[512]{0:T(512)S(1)}, f32[512]{0:T(512)S(1)}) fusion(f32[2048]{0:T(1024)S(1)} %mul.498, f32[512,2048]{1,0:T(8,128)} %copy.124, f32[2,256,2048]{2,1,0:T(8,128)} %get-tuple-element.638, bf16[512,2560]{1,0:T(8,128)(2,1)} %copy-done.9, bf16[512,2560]{1,0:T(8,128)(2,1)S(1)} %copy-done.8, f32[512,2048]{1,0:T(8,128)} %copy.113, ...), kind=kLoop, calls=%fused_computation.144 | loop fusion | flops 12581888 | bytes 20983808 | tf_op jit(solution)/shard_map/reduce_sum | solution.py:265
  374.1 3.4 collective-permute-start.7
  378.3 7.9 %multiply_convert_fusion.14 = (bf16[512,2048]{1,0:T(8,128)(2,1)S(1)}, bf16[512,2048]{1,0:T(8,128)(2,1)S(1)}) fusion(f32[512]{0:T(512)S(1)} %add_rsqrt_fusion, f32[2048]{0:T(1024)S(1)} %dynamic_slice.96, f32[2048]{0:T(1024)S(1)} %mul.498, f32[512,2048]{1,0:T(8,128)} %copy.124, f32[2,256,2048]{2,1,0:T(8,128)} %get-tuple-element.638, ...), kind=kLoop, calls=%fused_computation.142 | loop fusion | flops 14680064 | bytes 25186304 | tf_op jit(solution)/shard_map/convert_element_type | solution.py:341
  386.2 32.1 %all_to_all.15.own_ref = bf16[32,16,2048]{2,1,0:T(8,128)(2,1)} all-to-all(bf16[32,16,2048]{2,1,0:T(8,128)(2,1)S(1)} %bitcast.416), channel_id=1, replica_groups=mesh['seq'=4,'chip'=16,'core'=2] {'chip','core'}, dimensions={0} | all-to-all | bytes 4194304 | tf_op jit(solution)/shard_map/all_to_all | solution.py:342
  418.3 32.3 %all_to_all.16.other_ref = bf16[32,16,2048]{2,1,0:T(8,128)(2,1)} all-to-all(bf16[32,16,2048]{2,1,0:T(8,128)(2,1)S(1)} %bitcast.415), channel_id=1, replica_groups=mesh['seq'=4,'chip'=16,'core'=2] {'chip','core'}, dimensions={0} | all-to-all | bytes 4194304 | tf_op jit(solution)/shard_map/all_to_all | solution.py:342
  450.5 129.4 %join_pages.1 = bf16[32,16,4096]{2,1,0:T(8,128)(2,1)} custom-call(s32[32]{0:T(128)} %bitcast.456, bf16[32,16,2048]{2,1,0:T(8,128)(2,1)} %all_to_all.15.own_ref, bf16[32,16,2048]{2,1,0:T(8,128)(2,1)} %all_to_all.16.other_ref), custom_call_target="tpu_custom_call" | custom-call | tf_op jit(solution)/shard_map/join_pages/pallas_call | solution.py:137
  (305 shorter events, 120.4 us)
Async XLA Ops:
  6.5 152.9 %copy-start = (bf16[2048,64]{0,1:T(8,128)(2,1)S(1)}, bf16[2048,64]{0,1:T(8,128)(2,1)}, u32[]{:S(2)}) copy-start(bf16[2048,64]{0,1:T(8,128)(2,1)} %param.18) | copy-start | bytes 786436
  6.5 160.8 %all-gather.10.cloned.1.call-start = ((), (), s32[]{:S(2)}) async-start(), calls=%async_computation.3 | async-start | bytes 10649600 | tf_op jit(solution)/shard_map/all_gather | solution.py:304
  6.5 11.3 %collective-permute-start.1 = (bf16[5,8,2048]{2,1,0:T(8,128)(2,1)}, bf16[5,8,2048]{2,1,0:T(8,128)(2,1)S(1)}, u32[]{:S(2)}, u32[]{:S(2)}) collective-permute-start(bf16[5,8,2048]{2,1,0:T(8,128)(2,1)} %bitcast.459), channel_id=1, source_target_pairs={{0,0},{51,1},{1,2},{52,3},{2,4},{53,5},{3,6},{54,7},{4,8},{55,9},{... | collective-permute-start | bytes 491528 | tf_op jit(solution)/shard_map/ppermute | solution.py:302
  11.2 13.3 %collective-permute-start.2 = (bf16[5,8,2048]{2,1,0:T(8,128)(2,1)}, bf16[5,8,2048]{2,1,0:T(8,128)(2,1)S(1)}, u32[]{:S(2)}, u32[]{:S(2)}) collective-permute-start(bf16[5,8,2048]{2,1,0:T(8,128)(2,1)} %bitcast.460), channel_id=1, source_target_pairs={{52,1},{53,3},{54,5},{55,7},{56,9},{57,11},{58,13},{59,15},{60,17}... | collective-permute-start | bytes 491528 | tf_op jit(solution)/shard_map/ppermute | solution.py:302
  12.6 12.0 %collective-permute-start.3 = (bf16[5,8,2048]{2,1,0:T(8,128)(2,1)}, bf16[5,8,2048]{2,1,0:T(8,128)(2,1)S(1)}, u32[]{:S(2)}, u32[]{:S(2)}) collective-permute-start(bf16[5,8,2048]{2,1,0:T(8,128)(2,1)} %bitcast.461), channel_id=1, source_target_pairs={{51,102},{102,103},{108,114},{114,115},{115,116}} | collective-permute-start | bytes 491528 | tf_op jit(solution)/shard_map/ppermute | solution.py:302
  32.2 74.3 %copy-start.29 = (s32[1,2048]{1,0:T(1,128)S(1)}, s32[1,2048]{1,0:T(1,128)}, u32[]{:S(2)}) copy-start(s32[1,2048]{1,0:T(1,128)} %param.25) | copy-start | bytes 24580
  32.2 75.4 %copy-start.24 = (f32[4,5120]{1,0:T(4,128)S(1)}, f32[4,5120]{1,0:T(4,128)}, u32[]{:S(2)}) copy-start(f32[4,5120]{1,0:T(4,128)} %param.19) | copy-start | bytes 245764
  32.2 109.2 %copy-start.30 = (f32[5120]{0:T(1024)S(1)}, f32[5120]{0:T(1024)}, u32[]{:S(2)}) copy-start(f32[5120]{0:T(1024)} %param.20) | copy-start | bytes 61444
  32.2 113.7 %copy-start.36 = (f32[64]{0:T(128)S(1)}, f32[64]{0:T(128)}, u32[]{:S(2)}) copy-start(f32[64]{0:T(128)} %param.21) | copy-start | bytes 772
  32.2 113.8 %copy-start.37 = (f32[64]{0:T(128)S(1)}, f32[64]{0:T(128)}, u32[]{:S(2)}) copy-start(f32[64]{0:T(128)} %param.22) | copy-start | bytes 772
  98.0 42.4 %all-to-all-start = ((bf16[32,16,2048]{2,1,0:T(8,128)(2,1)}), bf16[32,16,2048]{2,1,0:T(8,128)(2,1)S(1)}, u32[]{:S(2)}, u32[]{:S(2)}) async-start(bf16[32,16,2048]{2,1,0:T(8,128)(2,1)} %scatter_pages.1), calls=%async_computation | async-start | bytes 4194304 | tf_op jit(solution)/shard_map/all_to_all | solution.py:293
  106.4 239.0 %all-gather.12.cloned.1.call-start = ((), (), s32[]{:S(2)}) async-start(), calls=%async_computation.4 | async-start | bytes 2621440 | tf_op jit(solution)/shard_map/all_gather | solution.py:249
  106.5 39.6 %collective-permute-start.4 = (s32[1,2048]{1,0:T(1,128)S(1)}, s32[1,2048]{1,0:T(1,128)S(1)}, u32[]{:S(2)}, u32[]{:S(2)}) collective-permute-start(s32[1,2048]{1,0:T(1,128)S(1)} %copy-done.29), channel_id=1, source_target_pairs={{0,1},{1,0},{2,3},{3,2},{4,5},{5,4},{6,7},{7,6},{8,9},{9,8},{10,11... | collective-permute-start | bytes 24584 | tf_op jit(solution)/shard_map/ppermute | solution.py:298
  140.3 23.3 %collective-permute-start.5 = (bf16[32,16,2048]{2,1,0:T(8,128)(2,1)S(1)}, bf16[32,16,2048]{2,1,0:T(8,128)(2,1)}, u32[]{:S(2)}, u32[]{:S(2)}) collective-permute-start(bf16[32,16,2048]{2,1,0:T(8,128)(2,1)S(1)} %all-to-all-done), channel_id=1, source_target_pairs={{0,1},{1,0},{2,3},{3,2},{4,5},{5,4},{6,7},{7,6},{8,9},{9,8},{10,11... | collective-permute-start | bytes 6291464 | tf_op jit(solution)/shard_map/ppermute | solution.py:294
  146.0 14.8 %copy-start.32 = (f32[32]{0:T(128)}, f32[32]{0:T(128)S(1)}, u32[]{:S(2)}) copy-start(f32[32]{0:T(128)S(1)} %dynamic_slice.85) | copy-start | bytes 388
  146.3 13.2 %copy-start.22 = (s32[2,256]{1,0:T(2,128)}, s32[2,256]{1,0:T(2,128)S(1)}, u32[]{:S(2)}) copy-start(s32[2,256]{1,0:T(2,128)S(1)} %reshape.446) | copy-start | bytes 6148
  152.8 8.1 %collective-permute-start.6 = (bf16[16,2048]{1,0:T(8,128)(2,1)}, bf16[16,2048]{1,0:T(8,128)(2,1)}, u32[]{:S(2)}, u32[]{:S(2)}) collective-permute-start(bf16[16,2048]{1,0:T(8,128)(2,1)} %slice_bitcast_fusion), channel_id=1, source_target_pairs={{0,33},{1,32},{32,65},{33,64},{64,97},{65,96},{2,35},{3,34},{34,67... | collective-permute-start | bytes 196616 | tf_op jit(solution)/shard_map/ppermute | solution.py:297
  156.3 5.9 %collective-permute-start = (bf16[16,2048]{1,0:T(8,128)(2,1)}, bf16[16,2048]{1,0:T(8,128)(2,1)}, u32[]{:S(2)}, u32[]{:S(2)}) collective-permute-start(bf16[16,2048]{1,0:T(8,128)(2,1)} %slice_bitcast_fusion), channel_id=1, source_target_pairs={{0,32},{32,64},{64,96},{1,33},{33,65},{65,97},{2,34},{34,66},{66,9... | collective-permute-start | bytes 196616 | tf_op jit(solution)/shard_map/ppermute | solution.py:296
  167.3 9.7 %copy-start.25 = (bf16[3,2048]{1,0:T(4,128)(2,1)S(1)}, bf16[3,2048]{1,0:T(4,128)(2,1)}, u32[]{:S(2)}) copy-start(bf16[3,2048]{1,0:T(4,128)(2,1)} %slice.315) | copy-start | bytes 36868
  167.3 9.7 %copy-start.35 = (bf16[2560,2048]{1,0:T(8,128)(2,1)S(1)}, bf16[2560,2048]{1,0:T(8,128)(2,1)}, u32[]{:S(2)}) copy-start(bf16[2560,2048]{1,0:T(8,128)(2,1)} %all-gather.10.cloned.1.call-done) | copy-start | bytes 31457284
  177.1 5.8 copy-start.17
  177.1 5.8 copy-start.18
  177.1 5.8 copy-start.19
  194.1 13.6 %copy-start.12 = (bf16[512,256]{1,0:T(8,128)(2,1)}, bf16[512,256]{1,0:T(8,128)(2,1)S(1)}, u32[]{:S(2)}) copy-start(bf16[512,256]{1,0:T(8,128)(2,1)S(1)} %get-tuple-element.330) | copy-start | bytes 786436
  201.1 5.9 copy-start.14
  258.1 97.9 %all-gather.14.cloned.1.call-start = ((), (), s32[]{:S(2)}) async-start(), calls=%async_computation.5 | async-start | bytes 2621440 | tf_op jit(solution)/shard_map/all_gather | solution.py:249
  265.2 6.0 %copy-start.13 = (bf16[512,256]{1,0:T(8,128)(2,1)S(1)}, bf16[512,256]{1,0:T(8,128)(2,1)}, u32[]{:S(2)}) copy-start(bf16[512,256]{1,0:T(8,128)(2,1)} %get-tuple-element.370) | copy-start | bytes 786436
  265.2 6.8 %copy-start.10 = (bf16[512,256]{1,0:T(8,128)(2,1)S(1)}, bf16[512,256]{1,0:T(8,128)(2,1)}, u32[]{:S(2)}) copy-start(bf16[512,256]{1,0:T(8,128)(2,1)} %get-tuple-element.369) | copy-start | bytes 786436
  319.4 25.9 %copy-start.11 = (bf16[512,256]{1,0:T(8,128)(2,1)S(1)}, bf16[512,256]{1,0:T(8,128)(2,1)}, u32[]{:S(2)}) copy-start(bf16[512,256]{1,0:T(8,128)(2,1)} %get-tuple-element.369) | copy-start | bytes 786436
  366.7 10.8 %copy-start.31 = (f32[4096]{0:T(1024)S(1)}, f32[4096]{0:T(1024)}, u32[]{:S(2)}) copy-start(f32[4096]{0:T(1024)} %param.24) | copy-start | bytes 49156
  374.1 4.2 collective-permute-start.7
  418.3 161.7 %copy-start.1 = (bf16[2048,64]{0,1:T(8,128)(2,1)S(1)}, bf16[2048,64]{0,1:T(8,128)(2,1)}, u32[]{:S(2)}) copy-start(bf16[2048,64]{0,1:T(8,128)(2,1)} %param.18) | copy-start | bytes 786436
  (25 other events, 93.9 us)
Sparse Core Ops, SparseCore 0:
  32.3 103.4 all-gather.9
  258.2 27.1 all-gather.11
  320.5 27.1 all-gather.13

commit v2 on v1

v2 whole, which is shorter than its diff:
```python
from functools import partial

import jax
import jax.numpy as jnp
import numpy as np
from jax import lax
from jax.experimental import pallas as pl
from jax.experimental.pallas import tpu as pltpu
from jax.sharding import Mesh, PartitionSpec as P

HEAD_DIM = 64
STATE = 128
KCONV = 4
SPAN = 256
INNER = 4096
XBC = 5120
D = 2048
CORES = 2
HEADS = 32
GROUPS = 2
HALF = 2048
BC = GROUPS * STATE
OWN = HALF + 2 * BC
UNIT = 8
PIECE = 5
DEVICES = 128


def unit_of(core, at):
    x_units, bc_units = HALF // UNIT, BC // UNIT
    if at < x_units:
        return x_units * core + at
    if at < x_units + bc_units:
        return INNER // UNIT + bc_units * core + (at - x_units)
    return (INNER + 2 * BC) // UNIT + bc_units * core + (at - x_units - bc_units)


def weight_moves():
    wanted = [
        [divmod(unit_of(d % 2, PIECE * (d // 2) + k), PIECE) for k in range(PIECE)]
        for d in range(DEVICES)
    ]
    edges = sorted({(source, d) for d in range(DEVICES) for source, _ in wanted[d]})
    sent = [{} for _ in range(DEVICES)]
    got = [{} for _ in range(DEVICES)]

    def free(table):
        return next(k for k in range(DEVICES) if k not in table)

    for source, d in edges:
        a, b = free(sent[source]), free(got[d])
        if a != b:
            path, at, tables, other, colour = [], d, got, sent, a
            while colour in tables[at]:
                nxt = tables[at][colour]
                path.append((nxt, at, colour) if tables is got else (at, nxt, colour))
                at, tables, other = nxt, other, tables
                colour = b if colour == a else a
            for s, t, colour in path:
                del sent[s][colour]
                del got[t][colour]
            for s, t, colour in path:
                sent[s][a + b - colour] = t
                got[t][a + b - colour] = s
        sent[source][a] = d
        got[d][a] = source
    rounds = 1 + max(k for table in got for k in table)
    pairs = [[(got[d][k], d) for d in range(DEVICES) if k in got[d]] for k in range(rounds)]
    picks = np.zeros((DEVICES, PIECE), np.int32)
    for d in range(DEVICES):
        where = {source: k for k, source in got[d].items()}
        picks[d] = [where[source] * PIECE + slot for source, slot in wanted[d]]
    return pairs, picks


ALL = ("seq", "chip", "core")
REQ = ("chip", "core")


def move(index_ref, source_ref, out_ref, sems, *, places):
    copies = []
    for k, (source, target) in enumerate(places(index_ref)):
        copies.append(
            pltpu.make_async_copy(source_ref.at[source], out_ref.at[target], sems.at[k])
        )
    for copy in copies:
        copy.start()
    for copy in copies:
        copy.wait()


def scatter_pages(pages, targets):
    count = pages.shape[0]
    return pl.pallas_call(
        partial(move, places=lambda index: [(k, index[k]) for k in range(count)]),
        out_shape=jax.ShapeDtypeStruct(pages.shape, pages.dtype),
        in_specs=[pl.BlockSpec(memory_space=pltpu.SMEM), pl.BlockSpec(memory_space=pl.ANY)],
        out_specs=pl.BlockSpec(memory_space=pltpu.VMEM),
        scratch_shapes=[pltpu.SemaphoreType.DMA((count,))],
        name="scatter_pages",
    )(targets, pages)


def pick_units(units, picks):
    count = picks.shape[0]
    return pl.pallas_call(
        partial(move, places=lambda index: [(index[k], k) for k in range(count)]),
        out_shape=jax.ShapeDtypeStruct((count,) + units.shape[1:], units.dtype),
        in_specs=[pl.BlockSpec(memory_space=pltpu.SMEM), pl.BlockSpec(memory_space=pl.ANY)],
        out_specs=pl.BlockSpec(memory_space=pltpu.VMEM),
        scratch_shapes=[pltpu.SemaphoreType.DMA((count,))],
        name="pick_units",
    )(picks, units)


def join_kernel(target_ref, own_ref, other_ref, out_ref, sems):
    copies = []
    for k in range(own_ref.shape[0]):
        group = target_ref[k]
        for part, (pages, page) in enumerate(((own_ref, group), (other_ref, group ^ 1))):
            half = (group & 1) ^ part
            copies.append(
                pltpu.make_async_copy(
                    pages.at[page],
                    out_ref.at[k, :, pl.ds(pl.multiple_of(half * HALF, HALF), HALF)],
                    sems.at[2 * k + part],
                )
            )
    for copy in copies:
        copy.start()
    for copy in copies:
        copy.wait()


def join_pages(own, other, targets):
    count, rows, width = own.shape
    return pl.pallas_call(
        join_kernel,
        out_shape=jax.ShapeDtypeStruct((count, rows, 2 * width), own.dtype),
        in_specs=[pl.BlockSpec(memory_space=pltpu.SMEM)] + [pl.BlockSpec(memory_space=pl.ANY)] * 2,
        out_specs=pl.BlockSpec(memory_space=pltpu.VMEM),
        scratch_shapes=[pltpu.SemaphoreType.DMA((2 * count,))],
        name="join_pages",
    )(targets, own, other)


INTERPRET = False
LOG2E = 1.4426950408889634
ROWS = 512
BLOCKS = ROWS // SPAN
CONV_COLS = 512
CHUNK = 256
HALO = 16
TERMS = 3
SENT = STATE + 16
HEADS_STEP = 4
STEP_COLS = HEADS_STEP * HEAD_DIM
PER_GROUP = HEADS // GROUPS
GROUP_COLS = PER_GROUP * HEAD_DIM


def conv_kernel(halo_ref, tok_ref, weight_ref, taps_ref, bias_ref, mask_ref, out_ref, raw_ref):
    masks = [mask_ref[:, k : k + 1] for k in range(KCONV - 1)]
    for part in range(CONV_COLS // CHUNK):
        cols = slice(part * CHUNK, (part + 1) * CHUNK)
        weight = weight_ref[cols, :]
        dims = (((1,), (1,)), ((), ()))
        raw_ref[part, :HALO, :] = (
            lax.dot_general(halo_ref[...], weight, dims, preferred_element_type=jnp.float32)
            .astype(jnp.bfloat16)
            .astype(jnp.float32)
        )
        raw_ref[part, HALO:, :] = (
            lax.dot_general(tok_ref[...], weight, dims, preferred_element_type=jnp.float32)
            .astype(jnp.bfloat16)
            .astype(jnp.float32)
        )
    for part in range(CONV_COLS // CHUNK):
        cols = slice(part * CHUNK, (part + 1) * CHUNK)
        summed = bias_ref[:, cols] + taps_ref[KCONV - 1 : KCONV, cols] * raw_ref[part, HALO:, :]
        for k in range(KCONV - 1):
            start = HALO - (KCONV - 1) + k
            summed = (
                summed
                + (taps_ref[k : k + 1, cols] * raw_ref[part, start : start + ROWS, :]) * masks[k]
            )
        out_ref[:, cols] = (summed * (0.5 + 0.5 * jnp.tanh(0.5 * summed))).astype(jnp.bfloat16)


def project_conv(halo, tokens, weight, taps, bias, masks):
    return pl.pallas_call(
        conv_kernel,
        grid=(OWN // CONV_COLS,),
        out_shape=jax.ShapeDtypeStruct((ROWS, OWN), jnp.bfloat16),
        in_specs=[
            pl.BlockSpec((HALO, D), lambda n: (0, 0)),
            pl.BlockSpec((ROWS, D), lambda n: (0, 0)),
            pl.BlockSpec((CONV_COLS, D), lambda n: (n, 0)),
            pl.BlockSpec((KCONV, CONV_COLS), lambda n: (0, n)),
            pl.BlockSpec((1, CONV_COLS), lambda n: (0, n)),
            pl.BlockSpec((ROWS, KCONV - 1), lambda n: (0, 0)),
        ],
        out_specs=pl.BlockSpec((ROWS, CONV_COLS), lambda n: (0, n)),
        scratch_shapes=[pltpu.VMEM((CONV_COLS // CHUNK, HALO + ROWS, CHUNK), jnp.float32)],
        cost_estimate=pl.CostEstimate(
            flops=2 * (ROWS + HALO) * D * OWN, transcendentals=ROWS * OWN, bytes_accessed=15 << 20
        ),
        name="project_conv",
        interpret=INTERPRET,
    )(halo, tokens, weight, taps, bias, masks)


def spread_heads(values, first_head, columns):
    upper = values.astype(jnp.bfloat16)
    lower = (values - upper.astype(jnp.float32)).astype(jnp.bfloat16)
    head = lax.broadcasted_iota(jnp.int32, (HEADS, columns), 0)
    column = lax.broadcasted_iota(jnp.int32, (HEADS, columns), 1)
    chosen = (head == first_head + column // HEAD_DIM).astype(jnp.bfloat16)
    return jnp.dot(upper, chosen, preferred_element_type=jnp.float32) + jnp.dot(
        lower, chosen, preferred_element_type=jnp.float32
    )


def state_kernel(x_ref, b_ref, tail_ref, row_ref, gained_ref, local_ref):
    tail = spread_heads(tail_ref[...], pl.program_id(0) * PER_GROUP, GROUP_COLS)
    weighted = (x_ref[...].astype(jnp.float32) * tail).astype(jnp.bfloat16)
    gained = [
        lax.dot_general(
            b_ref[b * SPAN : (b + 1) * SPAN, :],
            weighted[b * SPAN : (b + 1) * SPAN],
            (((0,), (0,)), ((), ())),
            preferred_element_type=jnp.float32,
        )
        for b in range(BLOCKS)
    ]
    gained_ref[...] = gained[0]
    local_ref[:STATE, :] = (row_ref[1:2, :] * gained[0] + gained[1]).astype(jnp.bfloat16)
    left = row_ref[0:1, :] * row_ref[1:2, :]
    row = lax.broadcasted_iota(jnp.int32, (SENT - STATE, GROUP_COLS), 0)
    terms = jnp.zeros((SENT - STATE, GROUP_COLS), jnp.float32)
    for at in range(TERMS):
        term = left.astype(jnp.bfloat16).astype(jnp.float32)
        terms = jnp.where(row == at, term, terms)
        left = left - term
    local_ref[STATE:, :] = terms.astype(jnp.bfloat16)


def block_states(conv_out, tail, rows):
    return pl.pallas_call(
        state_kernel,
        grid=(GROUPS,),
        out_shape=[
            jax.ShapeDtypeStruct((STATE, HALF), jnp.float32),
            jax.ShapeDtypeStruct((SENT, HALF), jnp.bfloat16),
        ],
        in_specs=[
            pl.BlockSpec((ROWS, GROUP_COLS), lambda g: (0, g)),
            pl.BlockSpec((ROWS, STATE), lambda g: (0, HALF // STATE + g)),
            pl.BlockSpec((ROWS, HEADS), lambda g: (0, 0)),
            pl.BlockSpec((8, GROUP_COLS), lambda g: (0, g)),
        ],
        out_specs=[
            pl.BlockSpec((STATE, GROUP_COLS), lambda g: (0, g)),
            pl.BlockSpec((SENT, GROUP_COLS), lambda g: (0, g)),
        ],
        cost_estimate=pl.CostEstimate(
            flops=2 * ROWS * HALF * STATE, transcendentals=0, bytes_accessed=4 << 20
        ),
        name="block_states",
        interpret=INTERPRET,
    )(conv_out, conv_out, tail, rows)


def mixing_kernel(x_ref, b_ref, c_ref, decay_ref, seg_ref, out_ref, scores_ref, bias_ref):
    @pl.when(pl.program_id(1) == 0)
    def _():
        at = lax.broadcasted_iota(jnp.int32, (SPAN, SPAN), 0)
        source = lax.broadcasted_iota(jnp.int32, (SPAN, SPAN), 1)
        for b in range(BLOCKS):
            rows = slice(b * SPAN, (b + 1) * SPAN)
            scores_ref[b] = lax.dot_general(
                c_ref[rows, :],
                b_ref[rows, :],
                (((1,), (1,)), ((), ())),
                preferred_element_type=jnp.float32,
            )
            across = seg_ref[:, rows]
            down = across.T[:, 0:1]
            allowed = (down == across[0:1, :]) & (at >= source)
            bias_ref[b] = jnp.where(allowed, 0.0, -1e30)

    half = SPAN // 2
    lane = lax.broadcasted_iota(jnp.int32, (half, 2 * HEAD_DIM), 1)
    for b in range(BLOCKS):
        decay = decay_ref[0, :, b * SPAN : (b + 1) * SPAN]
        down = decay.T
        for pair in range(HEADS_STEP // 2):
            cols = slice(pair * 2 * HEAD_DIM, (pair + 1) * 2 * HEAD_DIM)
            for part in range(2):
                reach = (part + 1) * half
                rows = slice(part * half, reach)
                found = []
                for head in (2 * pair, 2 * pair + 1):
                    spread = (
                        down[rows, head : head + 1]
                        - decay[HEADS_STEP + head : HEADS_STEP + head + 1, :reach]
                    )
                    mixing = (
                        jnp.exp2(spread + bias_ref[b, rows, :reach]) * scores_ref[b, rows, :reach]
                    ).astype(jnp.bfloat16)
                    found.append(
                        jnp.dot(
                            mixing,
                            x_ref[b * SPAN : b * SPAN + reach, cols],
                            preferred_element_type=jnp.float32,
                        )
                    )
                out_ref[b * SPAN + part * half : b * SPAN + reach, cols] = jnp.where(
                    lane < HEAD_DIM, found[0], found[1]
                )


def mix_blocks(conv_out, decay, seg):
    steps = PER_GROUP // HEADS_STEP
    return pl.pallas_call(
        mixing_kernel,
        grid=(GROUPS, steps),
        out_shape=jax.ShapeDtypeStruct((ROWS, HALF), jnp.float32),
        in_specs=[
            pl.BlockSpec((ROWS, STEP_COLS), lambda g, p: (0, g * steps + p)),
            pl.BlockSpec((ROWS, STATE), lambda g, p: (0, HALF // STATE + g)),
            pl.BlockSpec((ROWS, STATE), lambda g, p: (0, HALF // STATE + GROUPS + g)),
            pl.BlockSpec((1, 8, ROWS), lambda g, p: (g * steps + p, 0, 0)),
            pl.BlockSpec((8, ROWS), lambda g, p: (0, 0)),
        ],
        out_specs=pl.BlockSpec((ROWS, STEP_COLS), lambda g, p: (0, g * steps + p)),
        scratch_shapes=[pltpu.VMEM((BLOCKS, SPAN, SPAN), jnp.float32)] * 2,
        cost_estimate=pl.CostEstimate(
            flops=2 * ROWS * SPAN * HALF,
            transcendentals=ROWS * SPAN * HEADS,
            bytes_accessed=7 << 20,
        ),
        name="mix_blocks",
        interpret=INTERPRET,
    )(conv_out, conv_out, conv_out, decay, seg)


def readout_kernel(
    y_ref, x_ref, c_ref, gained_ref, states_ref, factor_ref, row_ref, out_ref, power_ref, part_ref
):
    steps = PER_GROUP // HEADS_STEP
    at = pl.program_id(0) * steps + pl.program_id(1)
    incoming = jnp.zeros((STATE, STEP_COLS), jnp.float32)
    for peer in range(states_ref.shape[0] - 1):
        terms = states_ref[peer, STATE:, :].astype(jnp.float32)
        through = (terms[0:1] + terms[1:2]) + terms[2:3]
        after = through * incoming + states_ref[peer, :STATE, :].astype(jnp.float32)
        incoming = jnp.where(row_ref[4 + peer : 5 + peer, :] > 0.5, after, incoming)
    second = row_ref[0:1, :] * incoming + gained_ref[...]
    factor = spread_heads(factor_ref[...], at * HEADS_STEP, STEP_COLS)

    @pl.when(at == 0)
    def _():
        part_ref[...] = jnp.zeros_like(part_ref)

    for b, state in enumerate((incoming, second)):
        rows = slice(b * SPAN, (b + 1) * SPAN)
        readout = jnp.dot(
            c_ref[rows, :], state.astype(jnp.bfloat16), preferred_element_type=jnp.float32
        )
        combined = (
            y_ref[rows, :]
            + readout * factor[rows]
            + row_ref[2:3, :] * x_ref[rows, :].astype(jnp.float32)
        )
        out_ref[rows, :] = combined
        squared = combined * combined
        part_ref[rows, :] += squared[:, :128] + squared[:, 128:]

    @pl.when(at == GROUPS * steps - 1)
    def _():
        power_ref[...] = jnp.sum(part_ref[...].T, axis=0, keepdims=True)


def read_states(mixed, conv_out, gained, states, factor, rows):
    steps = PER_GROUP // HEADS_STEP
    peers = states.shape[0]
    return pl.pallas_call(
        readout_kernel,
        grid=(GROUPS, steps),
        out_shape=[
            jax.ShapeDtypeStruct((ROWS, HALF), jnp.float32),
            jax.ShapeDtypeStruct((1, ROWS), jnp.float32),
        ],
        in_specs=[
            pl.BlockSpec((ROWS, STEP_COLS), lambda g, p: (0, g * steps + p)),
            pl.BlockSpec((ROWS, STEP_COLS), lambda g, p: (0, g * steps + p)),
            pl.BlockSpec((ROWS, STATE), lambda g, p: (0, HALF // STATE + GROUPS + g)),
            pl.BlockSpec((STATE, STEP_COLS), lambda g, p: (0, g * steps + p)),
            pl.BlockSpec((peers, SENT, STEP_COLS), lambda g, p: (0, 0, g * steps + p)),
            pl.BlockSpec((ROWS, HEADS), lambda g, p: (0, 0)),
            pl.BlockSpec((8, STEP_COLS), lambda g, p: (0, g * steps + p)),
        ],
        out_specs=[
            pl.BlockSpec((ROWS, STEP_COLS), lambda g, p: (0, g * steps + p)),
            pl.BlockSpec((1, ROWS), lambda g, p: (0, 0)),
        ],
        scratch_shapes=[pltpu.VMEM((ROWS, 128), jnp.float32)],
        cost_estimate=pl.CostEstimate(
            flops=2 * ROWS * STATE * HALF, transcendentals=0, bytes_accessed=14 << 20
        ),
        name="read_states",
        interpret=INTERPRET,
    )(mixed, conv_out, conv_out, gained, states, factor, rows)


def prepare(tokens, labels, step_weight, step_bias, decay_rate):
    step_raw = jnp.dot(tokens, step_weight, preferred_element_type=jnp.float32).astype(jnp.bfloat16)
    step_size = jax.nn.softplus(step_raw.astype(jnp.float32) + step_bias[None, :])
    seg = labels[KCONV - 1 :]
    change = (-step_size * decay_rate[None, :]).reshape(BLOCKS, SPAN, HEADS)
    log_decay = jnp.cumsum(change, axis=1)
    last = log_decay[:, SPAN - 1]
    seg_blocks = seg.reshape(BLOCKS, SPAN)
    final = seg_blocks[:, SPAN - 1]
    before = jnp.concatenate([labels[KCONV - 2][None], final[:-1]])
    tail = jnp.where(
        (seg_blocks == final[:, None])[:, :, None], jnp.exp(last[:, None] - log_decay), 0.0
    ) * step_size.reshape(BLOCKS, SPAN, HEADS)
    factor = jnp.where((seg_blocks == before[:, None])[:, :, None], jnp.exp(log_decay), 0.0)
    passing = jnp.where((final == before)[:, None], jnp.exp(last), 0.0)
    masks = jnp.stack(
        [(labels[k : k + ROWS] == seg).astype(jnp.float32) for k in range(KCONV - 1)], axis=1
    )
    scaled = (log_decay * LOG2E).reshape(ROWS, HEADS).T
    sized = scaled - jnp.log2(step_size).T
    decay = jnp.concatenate(
        [
            scaled.reshape(HEADS // HEADS_STEP, HEADS_STEP, ROWS),
            sized.reshape(HEADS // HEADS_STEP, HEADS_STEP, ROWS),
        ],
        axis=1,
    )
    seg_rows = jnp.broadcast_to(seg.astype(jnp.float32)[None, :], (8, ROWS))
    return dict(
        tail=tail.reshape(ROWS, HEADS),
        factor=factor.reshape(ROWS, HEADS),
        passing=passing,
        masks=masks,
        decay=decay,
        seg=seg_rows,
    )


def over_columns(values):
    return jnp.repeat(values, HEAD_DIM, axis=-1)


def per_device(
    stream_tokens,
    xbc_weight,
    step_weight,
    conv_weight,
    conv_bias,
    step_bias,
    decay_rate,
    skip_gain,
    norm_gain,
    segment_ids,
    page_target,
):
    request_groups = lax.axis_size("chip") * CORES
    tok_rows = stream_tokens.shape[0]
    page_rows = tok_rows // request_groups
    seq_at, core = lax.axis_index("seq"), lax.axis_index("core")
    flat = (seq_at * lax.axis_size("chip") + lax.axis_index("chip")) * CORES + core
    swap = [(0, 1), (1, 0)]
    peers = lax.axis_size("seq")
    onward = [(i, i + 1) for i in range(peers - 1)]
    onward_swap = [(2 * i + k, 2 * (i + 1) + 1 - k) for i in range(peers - 1) for k in range(2)]

    targets = page_target[0]
    pages = scatter_pages(stream_tokens.reshape(request_groups, page_rows, D), targets)
    own = lax.all_to_all(pages, REQ, split_axis=0, concat_axis=0, tiled=True)
    other = lax.ppermute(own, "core", swap)
    last_page = own[request_groups - 1]
    own_halo = lax.ppermute(last_page, "seq", onward)
    other_halo = lax.ppermute(last_page, ("seq", "core"), onward_swap)
    other_ids = lax.ppermute(segment_ids, "core", swap)

    pairs, picks = weight_moves()
    piece = xbc_weight.T.reshape(PIECE, UNIT, D)
    arrived = jnp.concatenate([lax.ppermute(piece, ALL, moves) for moves in pairs], axis=0)
    units = pick_units(arrived, jnp.asarray(picks)[flat])
    weight = lax.all_gather(units.reshape(PIECE * UNIT, D), ("seq", "chip"), axis=0, tiled=True)

    def columns(values):
        return jnp.concatenate(
            [
                lax.dynamic_slice_in_dim(values, core * HALF, HALF, axis=-1),
                lax.dynamic_slice_in_dim(values, INNER + core * BC, BC, axis=-1),
                lax.dynamic_slice_in_dim(values, INNER + 2 * BC + core * BC, BC, axis=-1),
            ],
            axis=-1,
        )

    def heads(values):
        return lax.dynamic_slice_in_dim(values, core * HEADS, HEADS, axis=-1)

    def labels(ids):
        padded = jnp.concatenate([jnp.full((KCONV - 1,), -1, jnp.int32), ids[0]])
        return lax.dynamic_slice_in_dim(padded, seq_at * tok_rows, tok_rows + KCONV - 1)

    taps, bias = columns(conv_weight), columns(conv_bias[None, :])
    step_half, step_shift, rate = heads(step_weight), heads(step_bias), heads(decay_rate)
    gain = lax.dynamic_slice_in_dim(norm_gain, core * HALF, HALF)
    ahead = (jnp.arange(peers) < seq_at).astype(jnp.float32)
    fixed_rows = jnp.concatenate(
        [
            over_columns(heads(skip_gain)[None, :]),
            jnp.zeros((1, HALF), jnp.float32),
            jnp.broadcast_to(ahead[:, None], (peers, HALF)),
        ],
        axis=0,
    )

    def states(tokens, halo, ids):
        tokens = tokens.reshape(tok_rows, D)
        ready = prepare(tokens, labels(ids), step_half, step_shift, rate)
        rows = jnp.concatenate([over_columns(ready["passing"]), fixed_rows], axis=0)
        conv_out = project_conv(halo, tokens, weight, taps, bias, ready["masks"])
        gained, local = block_states(conv_out, ready["tail"], rows)
        every = lax.all_gather(local, "seq")
        return ready, rows, conv_out, gained, every

    def outputs(ready, rows, conv_out, gained, every):
        mixed = mix_blocks(conv_out, ready["decay"], ready["seg"])
        combined, power = read_states(mixed, conv_out, gained, every, ready["factor"], rows)
        return combined, power, lax.ppermute(power, "core", swap)

    def sent_back(combined, power):
        scale = lax.rsqrt(power[0] / INNER + 1e-05)
        normed = (combined * scale[:, None] * gain[None, :]).astype(jnp.bfloat16)
        return lax.all_to_all(
            normed.reshape(request_groups, page_rows, HALF),
            REQ,
            split_axis=0,
            concat_axis=0,
            tiled=True,
        )

    own_states = states(own, own_halo, segment_ids)
    other_states = states(other, other_halo, other_ids)
    own_rows, own_power, own_swapped = outputs(*own_states)
    other_rows, other_power, other_swapped = outputs(*other_states)
    own_back = sent_back(own_rows, own_power + other_swapped)
    other_back = sent_back(other_rows, other_power + own_swapped)
    return join_pages(own_back, other_back, targets).reshape(tok_rows, INNER)


def solution(mesh):
    chips = mesh.shape["req"] // CORES
    by_core = Mesh(
        mesh.devices.reshape(mesh.shape["seq"], chips, CORES), ("seq", "chip", "core")
    )
    in_specs = (
        P(ALL, None),
        P(None, ALL),
        P(),
        P(),
        P(),
        P(),
        P(),
        P(),
        P(),
        P(REQ, None),
        P(ALL, None),
    )
    return jax.shard_map(
        per_device, mesh=by_core, in_specs=in_specs, out_specs=P(ALL, None), check_vma=False
    )
```

time: 589 us -> 315 us (0.53)
  Pallas kernels: 202 us -> 92.5 us
  local copies, waits for them, and re-layouts: 104 us -> 12.9 us
  matrix products: 61.8 us -> 3.2 us
  waiting for transfers between devices: 43.7 us -> 83 us
  other arithmetic: 48.6 us -> 17.8 us
  blocking collectives: 78.5 us -> 67.8 us
    pallas_call x1, Pallas kernels: 129 us -> 5.46 us  [join_pages(): pl.pallas_call(join_kernel, out_shape=jax.ShapeDtypeStruct((count, rows,...]
    pallas_call x0 -> x8, Pallas kernels: none -> 81 us  [the longest x2 31.7 us: project_conv(): pl.pallas_call(conv_kernel, grid=(OWN // CONV_COLS,), out_shape=jax.Shape...]
    pallas_call x1, Pallas kernels: 65.7 us -> 3.82 us  [scatter_pages(): pl.pallas_call(partial(move, places=lambda index: [(k, index[k]) for k in...]
    dot_general x28 -> x2, matrix products: 61.8 us -> 3.2 us  [prepare(): jnp.dot(tokens, step_weight, preferred_element_type=jnp.float32)]
    all_gather x1, waiting for transfers between devices: 0.01 us -> 44.4 us  [per_device(): lax.all_gather(units.reshape(PIECE * UNIT, D), ('seq', 'chip'), axis=0, t...]
    convert_element_type x10 -> x2, other arithmetic: 26.1 us -> 4.22 us  [the longest x1 4.22 us: sent_back(): normed = (combined * scale[:, None] * gain[None, :]).astype(jnp.bfloat16)]
    another operation x28 -> x14, local copies, waits for them, and re-layouts: 21.4 us -> 2.03 us  [the longest x8 1.76 us: prepare(): jnp.stack([(labels[k:k + ROWS] == seg).astype(jnp.float32) for k in range...]
    dynamic_slice x24 -> x0, local copies, waits for them, and re-layouts: 16.7 us -> none  [request(): lax.scan(partial(span_step, decay_rate), jnp.zeros((HEADS, HEAD_DIM, STAT...]
  transfers between devices with their start and end apart: 12 -> 13, of which waited for: 4 -> 7; matrix products, arithmetic and copies ran while one was open for 17% -> 9% of each run, Pallas kernels for 11% -> 21%
where the time goes in v2:
time: 315 us; the launch traced here: 313 us
  Pallas kernels  92.5 us (29%)
  waiting for transfers between devices  83 us (26%)
  blocking collectives  67.8 us (22%)
  starting transfers between devices  22.3 us (7%)
  other arithmetic  17.8 us (6%)
  between operations  13.5 us (4%)
  local copies, waits for them, and re-layouts  12.9 us (4%)
  matrix products  3.2 us (1%)
    all_to_all x2, blocking collectives, sent_back(): lax.all_to_all(normed.reshape(request_groups, page_rows, HALF), REQ, spli...  67.8 us
    all_gather x1, waiting for transfers between devices, per_device(): lax.all_gather(units.reshape(PIECE * UNIT, D), ('seq', 'chip'), axis=0, t...  44.4 us
    pallas_call x2, Pallas kernels, project_conv(): pl.pallas_call(conv_kernel, grid=(OWN // CONV_COLS,), out_shape=jax.Shape...  31.7 us
    pallas_call x2, Pallas kernels, read_states(): pl.pallas_call(readout_kernel, grid=(GROUPS, steps), out_shape=[jax.Shape...  21.8 us
    all_to_all x1, waiting for transfers between devices, per_device(): own = lax.all_to_all(pages, REQ, split_axis=0, concat_axis=0, tiled=True)  21.4 us
    pallas_call x2, Pallas kernels, mix_blocks(): pl.pallas_call(mixing_kernel, grid=(GROUPS, steps), out_shape=jax.ShapeDt...  19.5 us
    ppermute x3, waiting for transfers between devices, per_device(): lax.ppermute(piece, ALL, moves)  11.1 us
    pallas_call x2, Pallas kernels, block_states(): pl.pallas_call(state_kernel, grid=(GROUPS,), out_shape=[jax.ShapeDtypeStr...  7.99 us
  transfers between devices with their start and end apart: 13, of which 7 were waited for; matrix products, arithmetic and copies ran while one was open for 9% of the time, Pallas kernels for 21%

profile of v2, /device:TPU:1, one launch (start us, length us, event | category | flops | bytes accessed | tf_op | source)
XLA Modules:
  0.0 313.0 jit_solution(7488055508324398955)
XLA Ops:
  7.3 1.3 collective-permute-start.2
  8.6 4.0 %collective-permute-start.1 = (bf16[5,8,2048]{2,1,0:T(8,128)(2,1)}, bf16[5,8,2048]{2,1,0:T(8,128)(2,1)S(1)}, u32[]{:S(2)}, u32[]{:S(2)}) collective-permute-start(bf16[5,8,2048]{2,1,0:T(8,128)(2,1)} %bitcast.176), channel_id=1, source_target_pairs={{0,0},{51,1},{1,2},{52,3},{2,4},{53,5},{3,6},{54,7},{4,8},{55,9},{... | collective-permute-start | bytes 491528 | tf_op jit(solution)/shard_map/ppermute | solution.py:493
  12.6 1.3 fusion.26.index_ref
  13.9 8.2 %collective-permute-done.2 = bf16[5,8,2048]{2,1,0:T(8,128)(2,1)S(1)} collective-permute-done((bf16[5,8,2048]{2,1,0:T(8,128)(2,1)}, bf16[5,8,2048]{2,1,0:T(8,128)(2,1)S(1)}, u32[]{:S(2)}, u32[]{:S(2)}) %collective-permute-start.2) | collective-permute-done | bytes 163872 | tf_op jit(solution)/shard_map/ppermute | solution.py:493
  22.1 2.9 collective-permute-done.1
  25.9 2.2 pick_units.1
  28.2 3.8 %scatter_pages.1 = bf16[32,16,2048]{2,1,0:T(8,128)(2,1)} custom-call(s32[32]{0:T(128)} %bitcast.172, bf16[32,16,2048]{2,1,0:T(8,128)(2,1)} %bitcast.151), custom_call_target="tpu_custom_call" | custom-call | tf_op jit(solution)/shard_map/scatter_pages/pallas_call | solution.py:94
  32.1 7.4 %all-to-all-start = ((bf16[32,16,2048]{2,1,0:T(8,128)(2,1)}), bf16[32,16,2048]{2,1,0:T(8,128)(2,1)S(1)}, u32[]{:S(2)}, u32[]{:S(2)}) async-start(bf16[32,16,2048]{2,1,0:T(8,128)(2,1)} %scatter_pages.1), calls=%async_computation | async-start | bytes 4194304 | tf_op jit(solution)/shard_map/all_to_all | solution.py:484
  45.4 2.7 compare_reduce_fusion
  48.2 21.4 %all-to-all-done = bf16[32,16,2048]{2,1,0:T(8,128)(2,1)S(1)} async-done(((bf16[32,16,2048]{2,1,0:T(8,128)(2,1)}), bf16[32,16,2048]{2,1,0:T(8,128)(2,1)S(1)}, u32[]{:S(2)}, u32[]{:S(2)}) %all-to-all-start) | async-done | bytes 2097184 | tf_op jit(solution)/shard_map/all_to_all | solution.py:484
  69.5 1.4 collective-permute-start.5
  70.9 2.6 pad_add_fusion
  73.6 2.3 collective-permute-start
  76.7 1.2 reduce-window.14
  79.5 2.4 compare_select_fusion.1
  82.0 1.2 reduce-window.16
  84.6 44.4 %all-gather.6.cloned.1.call-done.weight_ref = bf16[2560,2048]{1,0:T(8,128)(2,1)} async-done(((bf16[40,2048]{1,0:T(8,128)(2,1)}), bf16[2560,2048]{1,0:T(8,128)(2,1)}) %all-gather.6.cloned.1.call-update) | async-done | bytes 10485776 | tf_op jit(solution)/shard_map/all_gather | solution.py:495
  129.1 15.7 %project_conv.2.x_ref.b_ref.c_ref = bf16[512,2560]{1,0:T(8,128)(2,1)} custom-call(bf16[16,2048]{1,0:T(8,128)(2,1)} %copy-done.7, bf16[512,2048]{1,0:T(8,128)(2,1)} %bitcast.146, bf16[2560,2048]{1,0:T(8,128)(2,1)} %all-gather.6.cloned.1.call-done.weight_ref, f32[4,2560]{1,0:T(4,128)} %pad_maximum_fusion.5.taps_ref, f32[1,2560]{1,0:T(1,128)} %pad_maximum_fusion.6.bias_ref, ...), custom_call_target="tpu_custom_call" | custom-call | flops 5536481280 | bytes 15728640 | tf_op jit(solution)/shard_map/project_conv/pallas_call | solution.py:191
  144.8 3.9 %block_states.2 = (f32[128,2048]{1,0:T(8,128)}, bf16[144,2048]{1,0:T(8,128)(2,1)}) custom-call(bf16[512,2560]{1,0:T(8,128)(2,1)} %project_conv.2.x_ref.b_ref.c_ref, bf16[512,2560]{1,0:T(8,128)(2,1)} %project_conv.2.x_ref.b_ref.c_ref, f32[512,32]{1,0:T(8,128)} %bitcast.152, f32[8,2048]{1,0:T(8,128)} %get-tuple-element.36.row_ref), custom_call_target="tpu_custom_call" | custom-call | flops 268435456 | bytes 4194304 | tf_op jit(solution)/shard_map/block_states/pallas_call | solution.py:249
  149.0 0.9 copy.85.mask_ref
  149.9 4.0 %collective-permute-start.4 = (bf16[16,2048]{1,0:T(8,128)(2,1)S(1)}, bf16[16,2048]{1,0:T(8,128)(2,1)S(1)}, u32[]{:S(2)}, u32[]{:S(2)}) collective-permute-start(bf16[16,2048]{1,0:T(8,128)(2,1)S(1)} %slice_bitcast_fusion), channel_id=1, source_target_pairs={{0,33},{1,32},{32,65},{33,64},{64,97},{65,96},{2,35},{3,34},{34,67... | collective-permute-start | bytes 196616 | tf_op jit(solution)/shard_map/ppermute | solution.py:488
  156.1 16.0 %project_conv.3.x_ref.b_ref.c_ref = bf16[512,2560]{1,0:T(8,128)(2,1)} custom-call(bf16[16,2048]{1,0:T(8,128)(2,1)} %copy-done.8, bf16[512,2048]{1,0:T(8,128)(2,1)} %bitcast.22.tok_ref, bf16[2560,2048]{1,0:T(8,128)(2,1)} %all-gather.6.cloned.1.call-done.weight_ref, f32[4,2560]{1,0:T(4,128)} %pad_maximum_fusion.5.taps_ref, ...), custom_call_target="tpu_custom_call" | custom-call | flops 5536481280 | bytes 15728640 | tf_op jit(solution)/shard_map/project_conv/pallas_call | solution.py:191
  172.1 4.0 %block_states.3 = (f32[128,2048]{1,0:T(8,128)}, bf16[144,2048]{1,0:T(8,128)(2,1)}) custom-call(bf16[512,2560]{1,0:T(8,128)(2,1)} %project_conv.3.x_ref.b_ref.c_ref, bf16[512,2560]{1,0:T(8,128)(2,1)} %project_conv.3.x_ref.b_ref.c_ref, f32[512,32]{1,0:T(8,128)} %bitcast.155, f32[8,2048]{1,0:T(8,128)} %get-tuple-element.35.row_ref), custom_call_target="tpu_custom_call" | custom-call | flops 268435456 | bytes 4194304 | tf_op jit(solution)/shard_map/block_states/pallas_call | solution.py:249
  180.1 9.8 %mix_blocks.2.y_ref = f32[512,2048]{1,0:T(8,128)} custom-call(bf16[512,2560]{1,0:T(8,128)(2,1)} %project_conv.2.x_ref.b_ref.c_ref, bf16[512,2560]{1,0:T(8,128)(2,1)} %project_conv.2.x_ref.b_ref.c_ref, bf16[512,2560]{1,0:T(8,128)(2,1)} %project_conv.2.x_ref.b_ref.c_ref, f32[8,8,512]{2,1,0:T(8,128)} %pad_maximum_fusion.1.decay_ref, ...), custom_call_target="tpu_custom_call" | custom-call | flops 536870912 | bytes 7340032 | tf_op jit(solution)/shard_map/mix_blocks/pallas_call | solution.py:325
  190.5 9.7 %mix_blocks.3.y_ref = f32[512,2048]{1,0:T(8,128)} custom-call(bf16[512,2560]{1,0:T(8,128)(2,1)} %project_conv.3.x_ref.b_ref.c_ref, bf16[512,2560]{1,0:T(8,128)(2,1)} %project_conv.3.x_ref.b_ref.c_ref, bf16[512,2560]{1,0:T(8,128)(2,1)} %project_conv.3.x_ref.b_ref.c_ref, f32[8,8,512]{2,1,0:T(8,128)} %pad_maximum_fusion.2.decay_ref, ...), custom_call_target="tpu_custom_call" | custom-call | flops 536870912 | bytes 7340032 | tf_op jit(solution)/shard_map/mix_blocks/pallas_call | solution.py:325
  200.2 10.9 %read_states.2 = (f32[512,2048]{1,0:T(8,128)}, f32[1,512]{1,0:T(1,128)}) custom-call(f32[512,2048]{1,0:T(8,128)} %mix_blocks.2.y_ref, bf16[512,2560]{1,0:T(8,128)(2,1)} %project_conv.2.x_ref.b_ref.c_ref, bf16[512,2560]{1,0:T(8,128)(2,1)} %project_conv.2.x_ref.b_ref.c_ref, f32[128,2048]{1,0:T(8,128)} %get-tuple-element.13.gained_ref, ...), custom_call_target="tpu_custom_call" | custom-call | flops 268435456 | bytes 14680064 | tf_op jit(solution)/shard_map/read_states/pallas_call | solution.py:388
  211.3 4.9 %all-gather.10.cloned.1.call-done = bf16[576,2048]{1,0:T(8,128)(2,1)} async-done(((bf16[144,2048]{1,0:T(8,128)(2,1)}), bf16[576,2048]{1,0:T(8,128)(2,1)}) %all-gather.10.cloned.1.call-update) | async-done | bytes 2359312 | tf_op jit(solution)/shard_map/all_gather | solution.py:533
  216.2 10.9 %read_states.3 = (f32[512,2048]{1,0:T(8,128)}, f32[1,512]{1,0:T(1,128)}) custom-call(f32[512,2048]{1,0:T(8,128)} %mix_blocks.3.y_ref, bf16[512,2560]{1,0:T(8,128)(2,1)} %project_conv.3.x_ref.b_ref.c_ref, bf16[512,2560]{1,0:T(8,128)(2,1)} %project_conv.3.x_ref.b_ref.c_ref, f32[128,2048]{1,0:T(8,128)} %get-tuple-element.17.gained_ref, ...), custom_call_target="tpu_custom_call" | custom-call | flops 268435456 | bytes 14680064 | tf_op jit(solution)/shard_map/read_states/pallas_call | solution.py:388
  228.9 4.2 %multiply_convert_fusion = (bf16[512,2048]{1,0:T(8,128)(2,1)S(1)}, bf16[512,2048]{1,0:T(8,128)(2,1)S(1)}) fusion(f32[512,2048]{1,0:T(8,128)} %get-tuple-element.20, f32[512]{0:T(512)S(1)} %bitcast.166, f32[2048]{0:T(1024)S(1)} %dynamic-slice-done, f32[512,2048]{1,0:T(8,128)} %get-tuple-element.15, f32[512]{0:T(512)S(1)} %bitcast.167), kind=kLoop, calls=%fused_computation | loop fusion | flops 6291456 | bytes 12595200 | tf_op jit(solution)/shard_map/convert_element_type | solution.py:543
  233.2 35.5 %all_to_all.15.own_ref = bf16[32,16,2048]{2,1,0:T(8,128)(2,1)} all-to-all(bf16[32,16,2048]{2,1,0:T(8,128)(2,1)S(1)} %bitcast.148), channel_id=1, replica_groups=mesh['seq'=4,'chip'=16,'core'=2] {'chip','core'}, dimensions={0} | all-to-all | bytes 4194304 | tf_op jit(solution)/shard_map/all_to_all | solution.py:544
  268.7 32.3 %all_to_all.16.other_ref = bf16[32,16,2048]{2,1,0:T(8,128)(2,1)} all-to-all(bf16[32,16,2048]{2,1,0:T(8,128)(2,1)S(1)} %bitcast.147), channel_id=1, replica_groups=mesh['seq'=4,'chip'=16,'core'=2] {'chip','core'}, dimensions={0} | all-to-all | bytes 4194304 | tf_op jit(solution)/shard_map/all_to_all | solution.py:544
  301.0 5.5 %join_pages.1 = bf16[32,16,4096]{2,1,0:T(8,128)(2,1)} custom-call(s32[32]{0:T(128)} %bitcast.173, bf16[32,16,2048]{2,1,0:T(8,128)(2,1)} %all_to_all.15.own_ref, bf16[32,16,2048]{2,1,0:T(8,128)(2,1)} %all_to_all.16.other_ref), custom_call_target="tpu_custom_call" | custom-call | tf_op jit(solution)/shard_map/join_pages/pallas_call | solution.py:137
  (124 shorter events, 20.6 us)
Async XLA Ops:
  6.5 69.4 %copy-start = (bf16[2048,64]{0,1:T(8,128)(2,1)S(1)}, bf16[2048,64]{0,1:T(8,128)(2,1)}, u32[]{:S(2)}) copy-start(bf16[2048,64]{0,1:T(8,128)(2,1)} %param.14) | copy-start | bytes 786436
  6.5 122.5 %all-gather.6.cloned.1.call-start = ((), (), s32[]{:S(2)}) async-start(), calls=%async_computation.3 | async-start | bytes 10649600 | tf_op jit(solution)/shard_map/all_gather | solution.py:495
  6.5 7.4 %collective-permute-start.3 = (bf16[5,8,2048]{2,1,0:T(8,128)(2,1)}, bf16[5,8,2048]{2,1,0:T(8,128)(2,1)S(1)}, u32[]{:S(2)}, u32[]{:S(2)}) collective-permute-start(bf16[5,8,2048]{2,1,0:T(8,128)(2,1)} %bitcast.174), channel_id=1, source_target_pairs={{51,102},{102,103},{108,114},{114,115},{115,116}} | collective-permute-start | bytes 491528 | tf_op jit(solution)/shard_map/ppermute | solution.py:493
  7.3 14.8 %collective-permute-start.2 = (bf16[5,8,2048]{2,1,0:T(8,128)(2,1)}, bf16[5,8,2048]{2,1,0:T(8,128)(2,1)S(1)}, u32[]{:S(2)}, u32[]{:S(2)}) collective-permute-start(bf16[5,8,2048]{2,1,0:T(8,128)(2,1)} %bitcast.175), channel_id=1, source_target_pairs={{52,1},{53,3},{54,5},{55,7},{56,9},{57,11},{58,13},{59,15},{60,17}... | collective-permute-start | bytes 491528 | tf_op jit(solution)/shard_map/ppermute | solution.py:493
  8.6 16.4 %collective-permute-start.1 = (bf16[5,8,2048]{2,1,0:T(8,128)(2,1)}, bf16[5,8,2048]{2,1,0:T(8,128)(2,1)S(1)}, u32[]{:S(2)}, u32[]{:S(2)}) collective-permute-start(bf16[5,8,2048]{2,1,0:T(8,128)(2,1)} %bitcast.176), channel_id=1, source_target_pairs={{0,0},{51,1},{1,2},{52,3},{2,4},{53,5},{3,6},{54,7},{4,8},{55,9},{... | collective-permute-start | bytes 491528 | tf_op jit(solution)/shard_map/ppermute | solution.py:493
  28.1 15.8 %collective-permute-start.6 = (s32[1,2048]{1,0:T(1,128)}, s32[1,2048]{1,0:T(1,128)S(1)}, u32[]{:S(2)}, u32[]{:S(2)}) collective-permute-start(s32[1,2048]{1,0:T(1,128)} %param.21), channel_id=1, source_target_pairs={{0,1},{1,0},{2,3},{3,2},{4,5},{5,4},{6,7},{7,6},{8,9},{9,8},{10,11... | collective-permute-start | bytes 24584 | tf_op jit(solution)/shard_map/ppermute | solution.py:489
  32.0 7.5 %copy-start.4 = (s32[1,2048]{1,0:T(1,128)S(1)}, s32[1,2048]{1,0:T(1,128)}, u32[]{:S(2)}) copy-start(s32[1,2048]{1,0:T(1,128)} %param.21) | copy-start | bytes 24580
  32.0 7.7 %copy-start.5 = (f32[5120]{0:T(1024)S(1)}, f32[5120]{0:T(1024)}, u32[]{:S(2)}) copy-start(f32[5120]{0:T(1024)} %param.16) | copy-start | bytes 61444
  32.1 7.8 %copy-start.3 = (f32[4,5120]{1,0:T(4,128)S(1)}, f32[4,5120]{1,0:T(4,128)}, u32[]{:S(2)}) copy-start(f32[4,5120]{1,0:T(4,128)} %param.15) | copy-start | bytes 245764
  32.1 9.8 %copy-start.9 = (f32[64]{0:T(128)S(1)}, f32[64]{0:T(128)}, u32[]{:S(2)}) copy-start(f32[64]{0:T(128)} %param.17) | copy-start | bytes 772
  32.1 9.9 %copy-start.10 = (f32[64]{0:T(128)S(1)}, f32[64]{0:T(128)}, u32[]{:S(2)}) copy-start(f32[64]{0:T(128)} %param.18) | copy-start | bytes 772
  32.1 9.9 %copy-start.11 = (f32[64]{0:T(128)S(1)}, f32[64]{0:T(128)}, u32[]{:S(2)}) copy-start(f32[64]{0:T(128)} %param.19) | copy-start | bytes 772
  32.1 37.4 %all-to-all-start = ((bf16[32,16,2048]{2,1,0:T(8,128)(2,1)}), bf16[32,16,2048]{2,1,0:T(8,128)(2,1)S(1)}, u32[]{:S(2)}, u32[]{:S(2)}) async-start(bf16[32,16,2048]{2,1,0:T(8,128)(2,1)} %scatter_pages.1), calls=%async_computation | async-start | bytes 4194304 | tf_op jit(solution)/shard_map/all_to_all | solution.py:484
  39.5 160.7 %all-gather.8.cloned.1.call-start = ((), (), s32[]{:S(2)}) async-start(), calls=%async_computation.4 | async-start | bytes 2949120 | tf_op jit(solution)/shard_map/all_gather | solution.py:533
  69.5 12.4 %copy-start.2 = (bf16[32,16,2048]{2,1,0:T(8,128)(2,1)}, bf16[32,16,2048]{2,1,0:T(8,128)(2,1)S(1)}, u32[]{:S(2)}) copy-start(bf16[32,16,2048]{2,1,0:T(8,128)(2,1)S(1)} %all-to-all-done) | copy-start | bytes 6291460
  69.5 10.0 %collective-permute-start.5 = (bf16[32,16,2048]{2,1,0:T(8,128)(2,1)S(1)}, bf16[32,16,2048]{2,1,0:T(8,128)(2,1)}, u32[]{:S(2)}, u32[]{:S(2)}) collective-permute-start(bf16[32,16,2048]{2,1,0:T(8,128)(2,1)S(1)} %all-to-all-done), channel_id=1, source_target_pairs={{0,1},{1,0},{2,3},{3,2},{4,5},{5,4},{6,7},{7,6},{8,9},{9,8},{10,11... | collective-permute-start | bytes 6291464 | tf_op jit(solution)/shard_map/ppermute | solution.py:485
  73.6 11.1 %collective-permute-start = (bf16[16,2048]{1,0:T(8,128)(2,1)S(1)}, bf16[16,2048]{1,0:T(8,128)(2,1)S(1)}, u32[]{:S(2)}, u32[]{:S(2)}) collective-permute-start(bf16[16,2048]{1,0:T(8,128)(2,1)S(1)} %slice_bitcast_fusion), channel_id=1, source_target_pairs={{0,32},{32,64},{64,96},{1,33},{33,65},{65,97},{2,34},{34,66},{66,9... | collective-permute-start | bytes 196616 | tf_op jit(solution)/shard_map/ppermute | solution.py:487
  84.6 44.5 %copy-start.7 = (bf16[16,2048]{1,0:T(8,128)(2,1)}, bf16[16,2048]{1,0:T(8,128)(2,1)S(1)}, u32[]{:S(2)}) copy-start(bf16[16,2048]{1,0:T(8,128)(2,1)S(1)} %collective-permute-done.halo_ref) | copy-start | bytes 196612
  148.8 67.4 %all-gather.10.cloned.1.call-start = ((), (), s32[]{:S(2)}) async-start(), calls=%async_computation.5 | async-start | bytes 2949120 | tf_op jit(solution)/shard_map/all_gather | solution.py:533
  149.9 5.6 %collective-permute-start.4 = (bf16[16,2048]{1,0:T(8,128)(2,1)S(1)}, bf16[16,2048]{1,0:T(8,128)(2,1)S(1)}, u32[]{:S(2)}, u32[]{:S(2)}) collective-permute-start(bf16[16,2048]{1,0:T(8,128)(2,1)S(1)} %slice_bitcast_fusion), channel_id=1, source_target_pairs={{0,33},{1,32},{32,65},{33,64},{64,97},{65,96},{2,35},{3,34},{34,67... | collective-permute-start | bytes 196616 | tf_op jit(solution)/shard_map/ppermute | solution.py:488
  155.5 0.6 copy-start.8
  211.1 16.8 %collective-permute-start.8 = (f32[1,512]{1,0:T(1,128)}, f32[1,512]{1,0:T(1,128)S(1)}, u32[]{:S(2)}, u32[]{:S(2)}) collective-permute-start(f32[1,512]{1,0:T(1,128)} %get-tuple-element.16), channel_id=1, source_target_pairs={{0,1},{1,0},{2,3},{3,2},{4,5},{5,4},{6,7},{7,6},{8,9},{9,8},{10,11... | collective-permute-start | bytes 6152 | tf_op jit(solution)/shard_map/ppermute | solution.py:539
  216.2 12.8 %copy-start.6 = (f32[1,512]{1,0:T(1,128)S(1)}, f32[1,512]{1,0:T(1,128)}, u32[]{:S(2)}) copy-start(f32[1,512]{1,0:T(1,128)} %get-tuple-element.16) | copy-start | bytes 6148
  216.2 12.8 %dynamic-slice-start = ((f32[4096]{0:T(1024)}, s32[]{:T(128)}), f32[2048]{0:T(1024)S(1)}, s32[]{:S(2)}) async-start(f32[4096]{0:T(1024)} %param.20, s32[]{:T(128)} %select_n.77), calls=%async_computation.6 | async-start | bytes 16896 | tf_op jit(solution)/shard_map/dynamic_slice | solution.py:516
  227.1 1.9 collective-permute-start.7
  268.7 37.7 %copy-start.1 = (bf16[2048,64]{0,1:T(8,128)(2,1)S(1)}, bf16[2048,64]{0,1:T(8,128)(2,1)}, u32[]{:S(2)}) copy-start(bf16[2048,64]{0,1:T(8,128)(2,1)} %param.14) | copy-start | bytes 786436
Sparse Core Ops, SparseCore 0:
  28.2 100.8 all-gather.5
  148.9 32.5 all-gather.7
  183.2 32.9 all-gather.9

commit v3 on v2

--- a/solution.py
+++ b/solution.py
@@ -24,20 +24,31 @@
 UNIT = 8
 PIECE = 5
 DEVICES = 128
+RANKS = DEVICES // CORES
+PARTS = (HALF // GROUPS + 2 * BC, HALF // GROUPS)
 
 
 def unit_of(core, at):
-    x_units, bc_units = HALF // UNIT, BC // UNIT
-    if at < x_units:
-        return x_units * core + at
-    if at < x_units + bc_units:
-        return INNER // UNIT + bc_units * core + (at - x_units)
-    return (INNER + 2 * BC) // UNIT + bc_units * core + (at - x_units - bc_units)
+    first, bc_units = HALF // GROUPS // UNIT, BC // UNIT
+    if at < first:
+        return HALF // UNIT * core + at
+    if at < first + bc_units:
+        return INNER // UNIT + bc_units * core + (at - first)
+    if at < first + 2 * bc_units:
+        return (INNER + BC * CORES) // UNIT + bc_units * core + (at - first - bc_units)
+    return HALF // UNIT * core + at - 2 * bc_units
+
+
+def places_of(rank):
+    early, late = PARTS[0] // UNIT // RANKS, PARTS[1] // UNIT // RANKS
+    return [early * rank + k for k in range(early)] + [
+        PARTS[0] // UNIT + late * rank + k for k in range(late)
+    ]
 
 
 def weight_moves():
     wanted = [
-        [divmod(unit_of(d % 2, PIECE * (d // 2) + k), PIECE) for k in range(PIECE)]
+        [divmod(unit_of(d % CORES, at), PIECE) for at in places_of(d // CORES)]
         for d in range(DEVICES)
     ]
     edges = sorted({(source, d) for d in range(DEVICES) for source, _ in wanted[d]})
@@ -113,35 +124,39 @@
     )(picks, units)
 
 
-def join_kernel(target_ref, own_ref, other_ref, out_ref, sems):
-    copies = []
-    for k in range(own_ref.shape[0]):
+def join_kernel(target_ref, even_ref, odd_ref, out_ref, sems):
+    count = even_ref.shape[0]
+
+    def copy(pages, page, k, half):
+        return pltpu.make_async_copy(
+            pages.at[page], out_ref.at[k, :, pl.ds(half * HALF, HALF)], sems.at[CORES * k + half]
+        )
+
+    for k in range(count):
         group = target_ref[k]
-        for part, (pages, page) in enumerate(((own_ref, group), (other_ref, group ^ 1))):
-            half = (group & 1) ^ part
-            copies.append(
-                pltpu.make_async_copy(
-                    pages.at[page],
-                    out_ref.at[k, :, pl.ds(pl.multiple_of(half * HALF, HALF), HALF)],
-                    sems.at[2 * k + part],
-                )
-            )
-    for copy in copies:
-        copy.start()
-    for copy in copies:
-        copy.wait()
-
-
-def join_pages(own, other, targets):
-    count, rows, width = own.shape
+        odd = group % CORES
+        for which, pages in enumerate((even_ref, odd_ref)):
+
+            @pl.when(odd == which)
+            def _():
+                for half in range(CORES):
+                    copy(pages, group - odd + half, k, half).start()
+
+    for k in range(count):
+        for half in range(CORES):
+            copy(even_ref, 0, k, half).wait()
+
+
+def join_pages(even, odd, targets):
+    count, rows, width = even.shape
     return pl.pallas_call(
         join_kernel,
-        out_shape=jax.ShapeDtypeStruct((count, rows, 2 * width), own.dtype),
+        out_shape=jax.ShapeDtypeStruct((count, rows, 2 * width), even.dtype),
         in_specs=[pl.BlockSpec(memory_space=pltpu.SMEM)] + [pl.BlockSpec(memory_space=pl.ANY)] * 2,
         out_specs=pl.BlockSpec(memory_space=pltpu.VMEM),
         scratch_shapes=[pltpu.SemaphoreType.DMA((2 * count,))],
         name="join_pages",
-    )(targets, own, other)
+    )(targets, even, odd)
 
 
 INTERPRET = False
@@ -155,6 +170,8 @@
 SENT = STATE + 16
 HEADS_STEP = 4
 STEP_COLS = HEADS_STEP * HEAD_DIM
+READ_COLS = 512
+NORM_ROWS = 128
 PER_GROUP = HEADS // GROUPS
 GROUP_COLS = PER_GROUP * HEAD_DIM
 
@@ -188,10 +205,11 @@
 
 
 def project_conv(halo, tokens, weight, taps, bias, masks):
+    width = weight.shape[0]
     return pl.pallas_call(
         conv_kernel,
-        grid=(OWN // CONV_COLS,),
-        out_shape=jax.ShapeDtypeStruct((ROWS, OWN), jnp.bfloat16),
+        grid=(width // CONV_COLS,),
+        out_shape=jax.ShapeDtypeStruct((ROWS, width), jnp.bfloat16),
         in_specs=[
             pl.BlockSpec((HALO, D), lambda n: (0, 0)),
             pl.BlockSpec((ROWS, D), lambda n: (0, 0)),
@@ -203,7 +221,9 @@
         out_specs=pl.BlockSpec((ROWS, CONV_COLS), lambda n: (0, n)),
         scratch_shapes=[pltpu.VMEM((CONV_COLS // CHUNK, HALO + ROWS, CHUNK), jnp.float32)],
         cost_estimate=pl.CostEstimate(
-            flops=2 * (ROWS + HALO) * D * OWN, transcendentals=ROWS * OWN, bytes_accessed=15 << 20
+            flops=2 * (ROWS + HALO) * D * width,
+            transcendentals=ROWS * width,
+            bytes_accessed=2 * (ROWS * D + width * D + ROWS * width),
         ),
         name="project_conv",
         interpret=INTERPRET,
@@ -221,58 +241,61 @@
     )
 
 
-def state_kernel(x_ref, b_ref, tail_ref, row_ref, gained_ref, local_ref):
-    tail = spread_heads(tail_ref[...], pl.program_id(0) * PER_GROUP, GROUP_COLS)
-    weighted = (x_ref[...].astype(jnp.float32) * tail).astype(jnp.bfloat16)
-    gained = [
-        lax.dot_general(
-            b_ref[b * SPAN : (b + 1) * SPAN, :],
-            weighted[b * SPAN : (b + 1) * SPAN],
-            (((0,), (0,)), ((), ())),
-            preferred_element_type=jnp.float32,
-        )
-        for b in range(BLOCKS)
-    ]
-    gained_ref[...] = gained[0]
-    local_ref[:STATE, :] = (row_ref[1:2, :] * gained[0] + gained[1]).astype(jnp.bfloat16)
-    left = row_ref[0:1, :] * row_ref[1:2, :]
-    row = lax.broadcasted_iota(jnp.int32, (SENT - STATE, GROUP_COLS), 0)
-    terms = jnp.zeros((SENT - STATE, GROUP_COLS), jnp.float32)
-    for at in range(TERMS):
-        term = left.astype(jnp.bfloat16).astype(jnp.float32)
-        terms = jnp.where(row == at, term, terms)
-        left = left - term
-    local_ref[STATE:, :] = terms.astype(jnp.bfloat16)
-
-
-def block_states(conv_out, tail, rows):
+def state_kernel(first_ref, second_ref, b_ref, tail_ref, row_ref, gained_ref, local_ref):
+    for group, x_ref in enumerate((first_ref, second_ref)):
+        cols = slice(group * GROUP_COLS, (group + 1) * GROUP_COLS)
+        tail = spread_heads(tail_ref[...], group * PER_GROUP, GROUP_COLS)
+        weighted = (x_ref[...].astype(jnp.float32) * tail).astype(jnp.bfloat16)
+        gained = [
+            lax.dot_general(
+                b_ref[b * SPAN : (b + 1) * SPAN, group * STATE : (group + 1) * STATE],
+                weighted[b * SPAN : (b + 1) * SPAN],
+                (((0,), (0,)), ((), ())),
+                preferred_element_type=jnp.float32,
+            )
+            for b in range(BLOCKS)
+        ]
+        gained_ref[:, cols] = gained[0]
+        local_ref[:STATE, cols] = (row_ref[1:2, cols] * gained[0] + gained[1]).astype(jnp.bfloat16)
+        left = row_ref[0:1, cols] * row_ref[1:2, cols]
+        row = lax.broadcasted_iota(jnp.int32, (SENT - STATE, GROUP_COLS), 0)
+        terms = jnp.zeros((SENT - STATE, GROUP_COLS), jnp.float32)
+        for at in range(TERMS):
+            term = left.astype(jnp.bfloat16).astype(jnp.float32)
+            terms = jnp.where(row == at, term, terms)
+            left = left - term
+        local_ref[STATE:, cols] = terms.astype(jnp.bfloat16)
+
+
+def block_states(first, second, tail, rows):
     return pl.pallas_call(
         state_kernel,
-        grid=(GROUPS,),
+        grid=(1,),
         out_shape=[
             jax.ShapeDtypeStruct((STATE, HALF), jnp.float32),
             jax.ShapeDtypeStruct((SENT, HALF), jnp.bfloat16),
         ],
         in_specs=[
-            pl.BlockSpec((ROWS, GROUP_COLS), lambda g: (0, g)),
-            pl.BlockSpec((ROWS, STATE), lambda g: (0, HALF // STATE + g)),
-            pl.BlockSpec((ROWS, HEADS), lambda g: (0, 0)),
-            pl.BlockSpec((8, GROUP_COLS), lambda g: (0, g)),
+            pl.BlockSpec((ROWS, GROUP_COLS), lambda i: (0, 0)),
+            pl.BlockSpec((ROWS, GROUP_COLS), lambda i: (0, 0)),
+            pl.BlockSpec((ROWS, BC), lambda i: (0, GROUP_COLS // BC)),
+            pl.BlockSpec((ROWS, HEADS), lambda i: (0, 0)),
+            pl.BlockSpec((8, HALF), lambda i: (0, 0)),
         ],
         out_specs=[
-            pl.BlockSpec((STATE, GROUP_COLS), lambda g: (0, g)),
-            pl.BlockSpec((SENT, GROUP_COLS), lambda g: (0, g)),
+            pl.BlockSpec((STATE, HALF), lambda i: (0, 0)),
+            pl.BlockSpec((SENT, HALF), lambda i: (0, 0)),
         ],
         cost_estimate=pl.CostEstimate(
             flops=2 * ROWS * HALF * STATE, transcendentals=0, bytes_accessed=4 << 20
         ),
         name="block_states",
         interpret=INTERPRET,
-    )(conv_out, conv_out, tail, rows)
+    )(first, second, first, tail, rows)
 
 
 def mixing_kernel(x_ref, b_ref, c_ref, decay_ref, seg_ref, out_ref, scores_ref, bias_ref):
-    @pl.when(pl.program_id(1) == 0)
+    @pl.when(pl.program_id(0) == 0)
     def _():
         at = lax.broadcasted_iota(jnp.int32, (SPAN, SPAN), 0)
         source = lax.broadcasted_iota(jnp.int32, (SPAN, SPAN), 1)
@@ -320,44 +343,45 @@
                 )
 
 
-def mix_blocks(conv_out, decay, seg):
+def mix_blocks(x_out, bc_out, group, decay, seg):
     steps = PER_GROUP // HEADS_STEP
+    at_b = GROUP_COLS // STATE + group
     return pl.pallas_call(
         mixing_kernel,
-        grid=(GROUPS, steps),
-        out_shape=jax.ShapeDtypeStruct((ROWS, HALF), jnp.float32),
+        grid=(steps,),
+        out_shape=jax.ShapeDtypeStruct((ROWS, GROUP_COLS), jnp.float32),
         in_specs=[
-            pl.BlockSpec((ROWS, STEP_COLS), lambda g, p: (0, g * steps + p)),
-            pl.BlockSpec((ROWS, STATE), lambda g, p: (0, HALF // STATE + g)),
-            pl.BlockSpec((ROWS, STATE), lambda g, p: (0, HALF // STATE + GROUPS + g)),
-            pl.BlockSpec((1, 8, ROWS), lambda g, p: (g * steps + p, 0, 0)),
-            pl.BlockSpec((8, ROWS), lambda g, p: (0, 0)),
-        ],
-        out_specs=pl.BlockSpec((ROWS, STEP_COLS), lambda g, p: (0, g * steps + p)),
+            pl.BlockSpec((ROWS, STEP_COLS), lambda p: (0, p)),
+            pl.BlockSpec((ROWS, STATE), lambda p: (0, at_b)),
+            pl.BlockSpec((ROWS, STATE), lambda p: (0, at_b + GROUPS)),
+            pl.BlockSpec((1, 8, ROWS), lambda p: (group * steps + p, 0, 0)),
+            pl.BlockSpec((8, ROWS), lambda p: (0, 0)),
+        ],
+        out_specs=pl.BlockSpec((ROWS, STEP_COLS), lambda p: (0, p)),
         scratch_shapes=[pltpu.VMEM((BLOCKS, SPAN, SPAN), jnp.float32)] * 2,
         cost_estimate=pl.CostEstimate(
-            flops=2 * ROWS * SPAN * HALF,
-            transcendentals=ROWS * SPAN * HEADS,
-            bytes_accessed=7 << 20,
+            flops=2 * ROWS * SPAN * GROUP_COLS,
+            transcendentals=ROWS * SPAN * PER_GROUP,
+            bytes_accessed=4 << 20,
         ),
         name="mix_blocks",
         interpret=INTERPRET,
-    )(conv_out, conv_out, conv_out, decay, seg)
+    )(x_out, bc_out, bc_out, decay, seg)
 
 
 def readout_kernel(
-    y_ref, x_ref, c_ref, gained_ref, states_ref, factor_ref, row_ref, out_ref, power_ref, part_ref
+    y_ref, x_ref, c_ref, gained_ref, states_ref, factor_ref, row_ref, out_ref, power_ref, part_ref, *, group
 ):
-    steps = PER_GROUP // HEADS_STEP
-    at = pl.program_id(0) * steps + pl.program_id(1)
-    incoming = jnp.zeros((STATE, STEP_COLS), jnp.float32)
+    at = pl.program_id(0)
+    incoming = jnp.zeros((STATE, READ_COLS), jnp.float32)
     for peer in range(states_ref.shape[0] - 1):
         terms = states_ref[peer, STATE:, :].astype(jnp.float32)
         through = (terms[0:1] + terms[1:2]) + terms[2:3]
         after = through * incoming + states_ref[peer, :STATE, :].astype(jnp.float32)
         incoming = jnp.where(row_ref[4 + peer : 5 + peer, :] > 0.5, after, incoming)
     second = row_ref[0:1, :] * incoming + gained_ref[...]
-    factor = spread_heads(factor_ref[...], at * HEADS_STEP, STEP_COLS)
+    first_head = group * PER_GROUP + at * (READ_COLS // HEAD_DIM)
+    factor = spread_heads(factor_ref[...], first_head, READ_COLS)
 
     @pl.when(at == 0)
     def _():
@@ -375,43 +399,74 @@
         )
         out_ref[rows, :] = combined
         squared = combined * combined
-        part_ref[rows, :] += squared[:, :128] + squared[:, 128:]
-
-    @pl.when(at == GROUPS * steps - 1)
+        total = squared[:, :128]
+        for tile in range(1, READ_COLS // 128):
+            total = total + squared[:, tile * 128 : (tile + 1) * 128]
+        part_ref[rows, :] += total
+
+    @pl.when(at == GROUP_COLS // READ_COLS - 1)
     def _():
         power_ref[...] = jnp.sum(part_ref[...].T, axis=0, keepdims=True)
 
 
-def read_states(mixed, conv_out, gained, states, factor, rows):
-    steps = PER_GROUP // HEADS_STEP
+def read_states(mixed, x_out, bc_out, group, gained, states, factor, rows):
+    steps = GROUP_COLS // READ_COLS
     peers = states.shape[0]
     return pl.pallas_call(
-        readout_kernel,
-        grid=(GROUPS, steps),
+        partial(readout_kernel, group=group),
+        grid=(steps,),
         out_shape=[
-            jax.ShapeDtypeStruct((ROWS, HALF), jnp.float32),
+            jax.ShapeDtypeStruct((ROWS, GROUP_COLS), jnp.float32),
             jax.ShapeDtypeStruct((1, ROWS), jnp.float32),
         ],
         in_specs=[
-            pl.BlockSpec((ROWS, STEP_COLS), lambda g, p: (0, g * steps + p)),
-            pl.BlockSpec((ROWS, STEP_COLS), lambda g, p: (0, g * steps + p)),
-            pl.BlockSpec((ROWS, STATE), lambda g, p: (0, HALF // STATE + GROUPS + g)),
-            pl.BlockSpec((STATE, STEP_COLS), lambda g, p: (0, g * steps + p)),
-            pl.BlockSpec((peers, SENT, STEP_COLS), lambda g, p: (0, 0, g * steps + p)),
-            pl.BlockSpec((ROWS, HEADS), lambda g, p: (0, 0)),
-            pl.BlockSpec((8, STEP_COLS), lambda g, p: (0, g * steps + p)),
+            pl.BlockSpec((ROWS, READ_COLS), lambda p: (0, p)),
+            pl.BlockSpec((ROWS, READ_COLS), lambda p: (0, p)),
+            pl.BlockSpec((ROWS, STATE), lambda p: (0, GROUP_COLS // STATE + GROUPS + group)),
+            pl.BlockSpec((STATE, READ_COLS), lambda p: (0, group * steps + p)),
+            pl.BlockSpec((peers, SENT, READ_COLS), lambda p: (0, 0, group * steps + p)),
+            pl.BlockSpec((ROWS, HEADS), lambda p: (0, 0)),
+            pl.BlockSpec((8, READ_COLS), lambda p: (0, group * steps + p)),
         ],
         out_specs=[
-            pl.BlockSpec((ROWS, STEP_COLS), lambda g, p: (0, g * steps + p)),
-            pl.BlockSpec((1, ROWS), lambda g, p: (0, 0)),
+            pl.BlockSpec((ROWS, READ_COLS), lambda p: (0, p)),
+            pl.BlockSpec((1, ROWS), lambda p: (0, 0)),
         ],
         scratch_shapes=[pltpu.VMEM((ROWS, 128), jnp.float32)],
         cost_estimate=pl.CostEstimate(
-            flops=2 * ROWS * STATE * HALF, transcendentals=0, bytes_accessed=14 << 20
+            flops=2 * ROWS * STATE * GROUP_COLS, transcendentals=0, bytes_accessed=7 << 20
         ),
         name="read_states",
         interpret=INTERPRET,
-    )(mixed, conv_out, conv_out, gained, states, factor, rows)
+    )(mixed, x_out, bc_out, gained, states, factor, rows)
+
+
+def norm_kernel(first_ref, second_ref, power_ref, gain_ref, out_ref):
+    mean = jnp.broadcast_to(power_ref[...], (8, NORM_ROWS)) / INNER
+    scale = lax.rsqrt(mean + 1e-05).T[:, 0:1]
+    for group, rows_ref in enumerate((first_ref, second_ref)):
+        cols = slice(group * GROUP_COLS, (group + 1) * GROUP_COLS)
+        out_ref[:, cols] = (rows_ref[...] * scale * gain_ref[:, cols]).astype(jnp.bfloat16)
+
+
+def normalize(first, second, power, gain):
+    return pl.pallas_call(
+        norm_kernel,
+        grid=(ROWS // NORM_ROWS,),
+        out_shape=jax.ShapeDtypeStruct((ROWS, HALF), jnp.bfloat16),
+        in_specs=[
+            pl.BlockSpec((NORM_ROWS, GROUP_COLS), lambda i: (i, 0)),
+            pl.BlockSpec((NORM_ROWS, GROUP_COLS), lambda i: (i, 0)),
+            pl.BlockSpec((1, NORM_ROWS), lambda i: (0, i)),
+            pl.BlockSpec((1, HALF), lambda i: (0, 0)),
+        ],
+        out_specs=pl.BlockSpec((NORM_ROWS, HALF), lambda i: (i, 0)),
+        cost_estimate=pl.CostEstimate(
+            flops=2 * ROWS * HALF, transcendentals=ROWS, bytes_accessed=6 << 20
+        ),
+        name="normalize",
+        interpret=INTERPRET,
+    )(first, second, power, gain)
 
 
 def prepare(tokens, labels, step_weight, step_bias, decay_rate):
@@ -477,32 +532,44 @@
     swap = [(0, 1), (1, 0)]
     peers = lax.axis_size("seq")
     onward = [(i, i + 1) for i in range(peers - 1)]
-    onward_swap = [(2 * i + k, 2 * (i + 1) + 1 - k) for i in range(peers - 1) for k in range(2)]
 
     targets = page_target[0]
     pages = scatter_pages(stream_tokens.reshape(request_groups, page_rows, D), targets)
     own = lax.all_to_all(pages, REQ, split_axis=0, concat_axis=0, tiled=True)
+    own, own_ids = lax.optimization_barrier((own, segment_ids))
     other = lax.ppermute(own, "core", swap)
-    last_page = own[request_groups - 1]
-    own_halo = lax.ppermute(last_page, "seq", onward)
-    other_halo = lax.ppermute(last_page, ("seq", "core"), onward_swap)
-    other_ids = lax.ppermute(segment_ids, "core", swap)
+    other_ids = lax.ppermute(own_ids, "core", swap)
+
+    def in_order(first, second):
+        return [jnp.where(core == 0, first, second), jnp.where(core == 0, second, first)]
+
+    tokens = [blocks.reshape(tok_rows, D) for blocks in in_order(own, other)]
+    ids = in_order(own_ids, other_ids)
+    halos = lax.ppermute(jnp.stack([rows[tok_rows - HALO :] for rows in tokens]), "seq", onward)
 
     pairs, picks = weight_moves()
     piece = xbc_weight.T.reshape(PIECE, UNIT, D)
     arrived = jnp.concatenate([lax.ppermute(piece, ALL, moves) for moves in pairs], axis=0)
-    units = pick_units(arrived, jnp.asarray(picks)[flat])
-    weight = lax.all_gather(units.reshape(PIECE * UNIT, D), ("seq", "chip"), axis=0, tiled=True)
+    mine = jnp.asarray(picks)[flat]
+    early = PARTS[0] // UNIT // RANKS
+    first_units = pick_units(arrived, mine[:early])
+    first_units, rest = lax.optimization_barrier((first_units, mine[early:]))
+    weights = [
+        lax.all_gather(units.reshape(-1, D), ("seq", "chip"), axis=0, tiled=True)
+        for units in (first_units, pick_units(arrived, rest))
+    ]
 
     def columns(values):
-        return jnp.concatenate(
+        x_cols = lax.dynamic_slice_in_dim(values, core * HALF, HALF, axis=-1)
+        early = jnp.concatenate(
             [
-                lax.dynamic_slice_in_dim(values, core * HALF, HALF, axis=-1),
+                x_cols[:, : HALF // GROUPS],
                 lax.dynamic_slice_in_dim(values, INNER + core * BC, BC, axis=-1),
-                lax.dynamic_slice_in_dim(values, INNER + 2 * BC + core * BC, BC, axis=-1),
+                lax.dynamic_slice_in_dim(values, INNER + CORES * BC + core * BC, BC, axis=-1),
             ],
             axis=-1,
         )
+        return early, x_cols[:, HALF // GROUPS :]
 
     def heads(values):
         return lax.dynamic_slice_in_dim(values, core * HEADS, HEADS, axis=-1)
@@ -513,7 +580,7 @@
 
     taps, bias = columns(conv_weight), columns(conv_bias[None, :])
     step_half, step_shift, rate = heads(step_weight), heads(step_bias), heads(decay_rate)
-    gain = lax.dynamic_slice_in_dim(norm_gain, core * HALF, HALF)
+    gain = lax.dynamic_slice_in_dim(norm_gain[None, :], core * HALF, HALF, axis=-1)
     ahead = (jnp.arange(peers) < seq_at).astype(jnp.float32)
     fixed_rows = jnp.concatenate(
         [
@@ -524,38 +591,60 @@
         axis=0,
     )
 
-    def states(tokens, halo, ids):
-        tokens = tokens.reshape(tok_rows, D)
-        ready = prepare(tokens, labels(ids), step_half, step_shift, rate)
-        rows = jnp.concatenate([over_columns(ready["passing"]), fixed_rows], axis=0)
-        conv_out = project_conv(halo, tokens, weight, taps, bias, ready["masks"])
-        gained, local = block_states(conv_out, ready["tail"], rows)
-        every = lax.all_gather(local, "seq")
-        return ready, rows, conv_out, gained, every
-
-    def outputs(ready, rows, conv_out, gained, every):
-        mixed = mix_blocks(conv_out, ready["decay"], ready["seg"])
-        combined, power = read_states(mixed, conv_out, gained, every, ready["factor"], rows)
-        return combined, power, lax.ppermute(power, "core", swap)
-
-    def sent_back(combined, power):
-        scale = lax.rsqrt(power[0] / INNER + 1e-05)
-        normed = (combined * scale[:, None] * gain[None, :]).astype(jnp.bfloat16)
-        return lax.all_to_all(
-            normed.reshape(request_groups, page_rows, HALF),
+    ready = [prepare(tokens[q], labels(ids[q]), step_half, step_shift, rate) for q in range(CORES)]
+
+    def convolve(q, part):
+        return project_conv(
+            halos[q], tokens[q], weights[part], taps[part], bias[part], ready[q]["masks"]
+        )
+
+    early = [convolve(q, 0) for q in range(CORES)]
+    mixed = [[mix_blocks(early[q], early[q], 0, ready[q]["decay"], ready[q]["seg"])] for q in range(CORES)]
+    weights[1], early, mixed = lax.optimization_barrier((weights[1], early, mixed))
+    late, rows, gained, every = [], [], [], []
+    for q in range(CORES):
+        late.append(convolve(q, 1))
+        rows.append(jnp.concatenate([over_columns(ready[q]["passing"]), fixed_rows], axis=0))
+        one, local = block_states(early[q], late[q], ready[q]["tail"], rows[q])
+        gained.append(one)
+        every.append(lax.all_gather(local, "seq"))
+    for q in range(CORES):
+        mixed[q].append(mix_blocks(late[q], early[q], 1, ready[q]["decay"], ready[q]["seg"]))
+
+    returned = []
+    normed = None
+    for q in range(CORES):
+        if q > 0:
+            normed, mixed[q] = lax.optimization_barrier((normed, mixed[q]))
+            returned.append(normed)
+        parts = [
+            read_states(
+                mixed[q][group],
+                (early, late)[group][q],
+                early[q],
+                group,
+                gained[q],
+                every[q],
+                ready[q]["factor"],
+                rows[q],
+            )
+            for group in range(GROUPS)
+        ]
+        power = parts[0][1] + parts[1][1]
+        power = power + lax.ppermute(power, "core", swap)
+        normed = normalize(parts[0][0], parts[1][0], power, gain)
+    returned.append(normed)
+    even, odd = [
+        lax.all_to_all(
+            rows_out.reshape(request_groups, page_rows, HALF),
             REQ,
             split_axis=0,
             concat_axis=0,
             tiled=True,
         )
-
-    own_states = states(own, own_halo, segment_ids)
-    other_states = states(other, other_halo, other_ids)
-    own_rows, own_power, own_swapped = outputs(*own_states)
-    other_rows, other_power, other_swapped = outputs(*other_states)
-    own_back = sent_back(own_rows, own_power + other_swapped)
-    other_back = sent_back(other_rows, other_power + own_swapped)
-    return join_pages(own_back, other_back, targets).reshape(tok_rows, INNER)
+        for rows_out in returned
+    ]
+    return join_pages(even, odd, targets).reshape(tok_rows, INNER)
 
 
 def solution(mesh):

time: 315 us -> 339 us (1.076)
  blocking collectives: 67.8 us -> 34.5 us
  Pallas kernels: 92.5 us -> 113 us
  starting transfers between devices: 22.3 us -> 41.4 us
  waiting for transfers between devices: 83 us -> 96.7 us
    all_to_all x2 -> x1, blocking collectives: 67.8 us -> 34.5 us  [per_device(): lax.all_to_all(rows_out.reshape(request_groups, page_rows, HALF), REQ, sp...]
    pallas_call x8 -> x16, Pallas kernels: 81 us -> 99.3 us  [the longest x4 37.7 us: project_conv(): pl.pallas_call(conv_kernel, grid=(width // CONV_COLS,), out_shape=jax.Sha...]
    ppermute x3 -> x4, starting transfers between devices: 6.04 us -> 18.6 us  [per_device(): lax.ppermute(piece, ALL, moves)]
    all_gather x3 -> x4, waiting for transfers between devices: 49.3 us -> 61.7 us  [the longest x2 47.5 us: per_device(): lax.all_gather(units.reshape(-1, D), ('seq', 'chip'), axis=0, tiled=True)]
    ppermute x3 -> x4, waiting for transfers between devices: 11.1 us -> 2.61 us  [per_device(): lax.ppermute(piece, ALL, moves)]
    all_to_all x0 -> x1, starting transfers between devices: none -> 7.17 us  [per_device(): lax.all_to_all(rows_out.reshape(request_groups, page_rows, HALF), REQ, sp...]
    all_to_all x0 -> x1, waiting for transfers between devices: none -> 5.93 us  [per_device(): lax.all_to_all(rows_out.reshape(request_groups, page_rows, HALF), REQ, sp...]
    convert_element_type x1 -> x0, other arithmetic: 4.22 us -> none  [sent_back(): normed = (combined * scale[:, None] * gain[None, :]).astype(jnp.bfloat16)]
  transfers between devices with their start and end apart: 13 -> 15, of which waited for: 7 -> 8; matrix products, arithmetic and copies ran while one was open for 9% -> 11% of each run, Pallas kernels for 21% -> 28%
where the time goes in v3:
time: 339 us; the launch traced here: 337 us
  Pallas kernels  113 us (33%)
  waiting for transfers between devices  96.7 us (29%)
  starting transfers between devices  41.4 us (12%)
  blocking collectives  34.5 us (10%)
  other arithmetic  18.4 us (5%)
  local copies, waits for them, and re-layouts  16.2 us (5%)
  between operations  13.7 us (4%)
    all_gather x2, waiting for transfers between devices, per_device(): lax.all_gather(units.reshape(-1, D), ('seq', 'chip'), axis=0, tiled=True)  47.5 us
    pallas_call x4, Pallas kernels, project_conv(): pl.pallas_call(conv_kernel, grid=(width // CONV_COLS,), out_shape=jax.Sha...  37.7 us
    all_to_all x1, blocking collectives, per_device(): lax.all_to_all(rows_out.reshape(request_groups, page_rows, HALF), REQ, sp...  34.5 us
    all_to_all x1, waiting for transfers between devices, per_device(): own = lax.all_to_all(pages, REQ, split_axis=0, concat_axis=0, tiled=True)  25.5 us
    pallas_call x4, Pallas kernels, mix_blocks(): pl.pallas_call(mixing_kernel, grid=(steps,), out_shape=jax.ShapeDtypeStru...  22.3 us
    pallas_call x4, Pallas kernels, read_states(): pl.pallas_call(partial(readout_kernel, group=group), grid=(steps,), out_s...  21 us
    ppermute x4, starting transfers between devices, per_device(): lax.ppermute(piece, ALL, moves)  18.6 us
    all_gather x2, waiting for transfers between devices, per_device(): every.append(lax.all_gather(local, 'seq'))  14.2 us
  transfers between devices with their start and end apart: 15, of which 8 were waited for; matrix products, arithmetic and copies ran while one was open for 11% of the time, Pallas kernels for 28%

profile of v3, /device:TPU:1, one launch (start us, length us, event | category | flops | bytes accessed | tf_op | source)
XLA Modules:
  0.0 337.0 jit_solution(2962378439527024324)
XLA Ops:
  7.3 8.1 %collective-permute-start.2 = (bf16[5,8,2048]{2,1,0:T(8,128)(2,1)}, bf16[5,8,2048]{2,1,0:T(8,128)(2,1)S(1)}, u32[]{:S(2)}, u32[]{:S(2)}) collective-permute-start(bf16[5,8,2048]{2,1,0:T(8,128)(2,1)} %bitcast.188), channel_id=1, source_target_pairs={{0,0},{76,1},{1,2},{52,3},{77,5},{26,6},{54,9},{27,10},{78,11},{4,... | collective-permute-start | bytes 491528 | tf_op jit(solution)/shard_map/ppermute | solution.py:552
  17.4 7.7 %collective-permute-start = (bf16[5,8,2048]{2,1,0:T(8,128)(2,1)}, bf16[5,8,2048]{2,1,0:T(8,128)(2,1)S(1)}, u32[]{:S(2)}, u32[]{:S(2)}) collective-permute-start(bf16[5,8,2048]{2,1,0:T(8,128)(2,1)} %bitcast.190), channel_id=1, source_target_pairs={{25,0},{77,1},{26,2},{51,3},{1,4},{52,5},{27,6},{78,7},{2,8},{53,9... | collective-permute-start | bytes 491528 | tf_op jit(solution)/shard_map/ppermute | solution.py:552
  32.8 3.8 %scatter_pages.1 = bf16[32,16,2048]{2,1,0:T(8,128)(2,1)} custom-call(s32[32]{0:T(128)} %bitcast.185, bf16[32,16,2048]{2,1,0:T(8,128)(2,1)} %bitcast.165), custom_call_target="tpu_custom_call" | custom-call | tf_op jit(solution)/shard_map/scatter_pages/pallas_call | solution.py:105
  36.7 7.5 %all-to-all-start = ((bf16[32,16,2048]{2,1,0:T(8,128)(2,1)}), bf16[32,16,2048]{2,1,0:T(8,128)(2,1)S(1)}, u32[]{:S(2)}, u32[]{:S(2)}) async-start(bf16[32,16,2048]{2,1,0:T(8,128)(2,1)} %scatter_pages.1), calls=%async_computation | async-start | bytes 4194304 | tf_op jit(solution)/shard_map/all_to_all | solution.py:538
  46.8 25.5 %all-to-all-done = bf16[32,16,2048]{2,1,0:T(8,128)(2,1)S(1)} async-done(((bf16[32,16,2048]{2,1,0:T(8,128)(2,1)}), bf16[32,16,2048]{2,1,0:T(8,128)(2,1)S(1)}, u32[]{:S(2)}, u32[]{:S(2)}) %all-to-all-start) | async-done | bytes 2097184 | tf_op jit(solution)/shard_map/all_to_all | solution.py:538
  72.3 2.8 collective-permute-start.6
  85.6 2.7 compare_reduce_fusion
  92.3 3.1 collective-permute-start.5
  106.5 11.3 %all-gather.9.cloned.1.call-done.weight_ref = bf16[1536,2048]{1,0:T(8,128)(2,1)} async-done(((bf16[24,2048]{1,0:T(8,128)(2,1)}), bf16[1536,2048]{1,0:T(8,128)(2,1)}) %all-gather.9.cloned.1.call-update) | async-done | bytes 6291472 | tf_op jit(solution)/shard_map/all_gather | solution.py:558
  117.8 10.7 %project_conv.4.x_ref.b_ref.c_ref.first_ref = bf16[512,1536]{1,0:T(8,128)(2,1)} custom-call(bf16[16,2048]{1,0:T(8,128)(2,1)} %get-tuple-element.56.halo_ref, bf16[512,2048]{1,0:T(8,128)(2,1)} %bitcast.157, bf16[1536,2048]{1,0:T(8,128)(2,1)} %all-gather.9.cloned.1.call-done.weight_ref, f32[4,1536]{1,0:T(4,128)} %pad_maximum_fusion.5.taps_ref, ...), custom_call_target="tpu_custom_call" | custom-call | flops 3321888768 | bytes 9961472 | tf_op jit(solution)/shard_map/project_conv/pallas_call | solution.py:209
  129.1 5.6 %mix_blocks.4.y_ref = f32[512,1024]{1,0:T(8,128)} custom-call(bf16[512,1536]{1,0:T(8,128)(2,1)} %project_conv.4.x_ref.b_ref.c_ref.first_ref, bf16[512,1536]{1,0:T(8,128)(2,1)} %project_conv.4.x_ref.b_ref.c_ref.first_ref, bf16[512,1536]{1,0:T(8,128)(2,1)} %project_conv.4.x_ref.b_ref.c_ref.first_ref, f32[8,8,512]{2,1,0:T(8,128)} %pad_maximum_fusion.1.decay_ref, ...), custom_call_target="tpu_custom_call" | custom-call | flops 268435456 | bytes 4194304 | tf_op jit(solution)/shard_map/mix_blocks/pallas_call | solution.py:349
  134.7 10.8 %project_conv.5.x_ref.b_ref.c_ref.first_ref = bf16[512,1536]{1,0:T(8,128)(2,1)} custom-call(bf16[16,2048]{1,0:T(8,128)(2,1)} %get-tuple-element.55.halo_ref, bf16[512,2048]{1,0:T(8,128)(2,1)} %bitcast.154, bf16[1536,2048]{1,0:T(8,128)(2,1)} %all-gather.9.cloned.1.call-done.weight_ref, f32[4,1536]{1,0:T(4,128)} %pad_maximum_fusion.5.taps_ref, ...), custom_call_target="tpu_custom_call" | custom-call | flops 3321888768 | bytes 9961472 | tf_op jit(solution)/shard_map/project_conv/pallas_call | solution.py:209
  146.0 5.6 %mix_blocks.5.y_ref = f32[512,1024]{1,0:T(8,128)} custom-call(bf16[512,1536]{1,0:T(8,128)(2,1)} %project_conv.5.x_ref.b_ref.c_ref.first_ref, bf16[512,1536]{1,0:T(8,128)(2,1)} %project_conv.5.x_ref.b_ref.c_ref.first_ref, bf16[512,1536]{1,0:T(8,128)(2,1)} %project_conv.5.x_ref.b_ref.c_ref.first_ref, f32[8,8,512]{2,1,0:T(8,128)} %pad_maximum_fusion.2.decay_ref, ...), custom_call_target="tpu_custom_call" | custom-call | flops 268435456 | bytes 4194304 | tf_op jit(solution)/shard_map/mix_blocks/pallas_call | solution.py:349
  151.6 36.2 %all-gather.7.cloned.1.call-done.weight_ref = bf16[1024,2048]{1,0:T(8,128)(2,1)} async-done(((bf16[16,2048]{1,0:T(8,128)(2,1)}), bf16[1024,2048]{1,0:T(8,128)(2,1)}) %all-gather.7.cloned.1.call-update) | async-done | bytes 4194320 | tf_op jit(solution)/shard_map/all_gather | solution.py:558
  187.8 8.1 %project_conv.6.second_ref.x_ref = bf16[512,1024]{1,0:T(8,128)(2,1)} custom-call(bf16[16,2048]{1,0:T(8,128)(2,1)} %get-tuple-element.56.halo_ref, bf16[512,2048]{1,0:T(8,128)(2,1)} %bitcast.158, bf16[1024,2048]{1,0:T(8,128)(2,1)} %all-gather.7.cloned.1.call-done.weight_ref, f32[4,1024]{1,0:T(4,128)} %get-tuple-element.57.taps_ref, ...), custom_call_target="tpu_custom_call" | custom-call | flops 2214592512 | bytes 7340032 | tf_op jit(solution)/shard_map/project_conv/pallas_call | solution.py:209
  195.9 4.3 %block_states.2 = (f32[128,2048]{1,0:T(8,128)}, bf16[144,2048]{1,0:T(8,128)(2,1)}) custom-call(bf16[512,1536]{1,0:T(8,128)(2,1)} %project_conv.4.x_ref.b_ref.c_ref.first_ref, bf16[512,1024]{1,0:T(8,128)(2,1)} %project_conv.6.second_ref.x_ref, bf16[512,1536]{1,0:T(8,128)(2,1)} %project_conv.4.x_ref.b_ref.c_ref.first_ref, f32[512,32]{1,0:T(8,128)} %bitcast.166, ...), custom_call_target="tpu_custom_call" | custom-call | flops 268435456 | bytes 4194304 | tf_op jit(solution)/shard_map/block_states/pallas_call | solution.py:271
  201.3 8.1 %project_conv.7.x_ref.second_ref = bf16[512,1024]{1,0:T(8,128)(2,1)} custom-call(bf16[16,2048]{1,0:T(8,128)(2,1)} %get-tuple-element.55.halo_ref, bf16[512,2048]{1,0:T(8,128)(2,1)} %bitcast.155, bf16[1024,2048]{1,0:T(8,128)(2,1)} %all-gather.7.cloned.1.call-done.weight_ref, f32[4,1024]{1,0:T(4,128)} %get-tuple-element.57.taps_ref, ...), custom_call_target="tpu_custom_call" | custom-call | flops 2214592512 | bytes 7340032 | tf_op jit(solution)/shard_map/project_conv/pallas_call | solution.py:209
  209.5 4.6 %block_states.3 = (f32[128,2048]{1,0:T(8,128)}, bf16[144,2048]{1,0:T(8,128)(2,1)}) custom-call(bf16[512,1536]{1,0:T(8,128)(2,1)} %project_conv.5.x_ref.b_ref.c_ref.first_ref, bf16[512,1024]{1,0:T(8,128)(2,1)} %project_conv.7.x_ref.second_ref, bf16[512,1536]{1,0:T(8,128)(2,1)} %project_conv.5.x_ref.b_ref.c_ref.first_ref, f32[512,32]{1,0:T(8,128)} %bitcast.167, ...), custom_call_target="tpu_custom_call" | custom-call | flops 268435456 | bytes 4194304 | tf_op jit(solution)/shard_map/block_states/pallas_call | solution.py:271
  215.5 5.6 %mix_blocks.6.y_ref = f32[512,1024]{1,0:T(8,128)} custom-call(bf16[512,1024]{1,0:T(8,128)(2,1)} %project_conv.6.second_ref.x_ref, bf16[512,1536]{1,0:T(8,128)(2,1)} %project_conv.4.x_ref.b_ref.c_ref.first_ref, bf16[512,1536]{1,0:T(8,128)(2,1)} %project_conv.4.x_ref.b_ref.c_ref.first_ref, f32[8,8,512]{2,1,0:T(8,128)} %pad_maximum_fusion.1.decay_ref, ...), custom_call_target="tpu_custom_call" | custom-call | flops 268435456 | bytes 4194304 | tf_op jit(solution)/shard_map/mix_blocks/pallas_call | solution.py:349
  221.1 10.6 %all-gather.11.cloned.1.call-done = bf16[576,2048]{1,0:T(8,128)(2,1)} async-done(((bf16[144,2048]{1,0:T(8,128)(2,1)}), bf16[576,2048]{1,0:T(8,128)(2,1)}) %all-gather.11.cloned.1.call-update) | async-done | bytes 2359312 | tf_op jit(solution)/shard_map/all_gather | solution.py:610
  231.7 5.2 %read_states.4 = (f32[512,1024]{1,0:T(8,128)}, f32[1,512]{1,0:T(1,128)}) custom-call(f32[512,1024]{1,0:T(8,128)} %mix_blocks.4.y_ref, bf16[512,1536]{1,0:T(8,128)(2,1)} %project_conv.4.x_ref.b_ref.c_ref.first_ref, bf16[512,1536]{1,0:T(8,128)(2,1)} %project_conv.4.x_ref.b_ref.c_ref.first_ref, f32[128,2048]{1,0:T(8,128)} %get-tuple-element.36.gained_ref, ...), custom_call_target="tpu_custom_call" | custom-call | flops 134217728 | bytes 7340032 | tf_op jit(solution)/shard_map/read_states/pallas_call | solution.py:415
  236.9 5.3 %read_states.5 = (f32[512,1024]{1,0:T(8,128)}, f32[1,512]{1,0:T(1,128)}) custom-call(f32[512,1024]{1,0:T(8,128)} %mix_blocks.6.y_ref, bf16[512,1024]{1,0:T(8,128)(2,1)} %project_conv.6.second_ref.x_ref, bf16[512,1536]{1,0:T(8,128)(2,1)} %project_conv.4.x_ref.b_ref.c_ref.first_ref, f32[128,2048]{1,0:T(8,128)} %get-tuple-element.36.gained_ref, ...), custom_call_target="tpu_custom_call" | custom-call | flops 134217728 | bytes 7340032 | tf_op jit(solution)/shard_map/read_states/pallas_call | solution.py:415
  243.7 5.6 %mix_blocks.7.y_ref = f32[512,1024]{1,0:T(8,128)} custom-call(bf16[512,1024]{1,0:T(8,128)(2,1)} %project_conv.7.x_ref.second_ref, bf16[512,1536]{1,0:T(8,128)(2,1)} %project_conv.5.x_ref.b_ref.c_ref.first_ref, bf16[512,1536]{1,0:T(8,128)(2,1)} %project_conv.5.x_ref.b_ref.c_ref.first_ref, f32[8,8,512]{2,1,0:T(8,128)} %pad_maximum_fusion.2.decay_ref, ...), custom_call_target="tpu_custom_call" | custom-call | flops 268435456 | bytes 4194304 | tf_op jit(solution)/shard_map/mix_blocks/pallas_call | solution.py:349
  249.9 4.7 %normalize.2 = bf16[512,2048]{1,0:T(8,128)(2,1)} custom-call(f32[512,1024]{1,0:T(8,128)} %get-tuple-element.38.first_ref, f32[512,1024]{1,0:T(8,128)} %get-tuple-element.39.second_ref, f32[1,512]{1,0:T(1,128)} %add.117.power_ref, f32[1,2048]{1,0:T(1,128)} %bitcast.178), custom_call_target="tpu_custom_call" | custom-call | flops 2097152 | bytes 6291456 | tf_op jit(solution)/shard_map/normalize/pallas_call | solution.py:453
  254.6 7.2 %all-to-all-start.1 = ((bf16[32,16,2048]{2,1,0:T(8,128)(2,1)}), bf16[32,16,2048]{2,1,0:T(8,128)(2,1)S(1)}, u32[]{:S(2)}, u32[]{:S(2)}) async-start(bf16[32,16,2048]{2,1,0:T(8,128)(2,1)} %bitcast.159), calls=%async_computation.1 | async-start | bytes 4194304 | tf_op jit(solution)/shard_map/all_to_all | solution.py:638
  262.6 3.7 %all-gather.13.cloned.1.call-done = bf16[576,2048]{1,0:T(8,128)(2,1)} async-done(((bf16[144,2048]{1,0:T(8,128)(2,1)}), bf16[576,2048]{1,0:T(8,128)(2,1)}) %all-gather.13.cloned.1.call-update) | async-done | bytes 2359312 | tf_op jit(solution)/shard_map/all_gather | solution.py:610
  266.2 5.3 %read_states.7 = (f32[512,1024]{1,0:T(8,128)}, f32[1,512]{1,0:T(1,128)}) custom-call(f32[512,1024]{1,0:T(8,128)} %mix_blocks.7.y_ref, bf16[512,1024]{1,0:T(8,128)(2,1)} %project_conv.7.x_ref.second_ref, bf16[512,1536]{1,0:T(8,128)(2,1)} %project_conv.5.x_ref.b_ref.c_ref.first_ref, f32[128,2048]{1,0:T(8,128)} %get-tuple-element.46.gained_ref, ...), custom_call_target="tpu_custom_call" | custom-call | flops 134217728 | bytes 7340032 | tf_op jit(solution)/shard_map/read_states/pallas_call | solution.py:415
  271.5 5.2 %read_states.6 = (f32[512,1024]{1,0:T(8,128)}, f32[1,512]{1,0:T(1,128)}) custom-call(f32[512,1024]{1,0:T(8,128)} %mix_blocks.5.y_ref, bf16[512,1536]{1,0:T(8,128)(2,1)} %project_conv.5.x_ref.b_ref.c_ref.first_ref, bf16[512,1536]{1,0:T(8,128)(2,1)} %project_conv.5.x_ref.b_ref.c_ref.first_ref, f32[128,2048]{1,0:T(8,128)} %get-tuple-element.46.gained_ref, ...), custom_call_target="tpu_custom_call" | custom-call | flops 134217728 | bytes 7340032 | tf_op jit(solution)/shard_map/read_states/pallas_call | solution.py:415
  279.7 4.7 %normalize.3 = bf16[512,2048]{1,0:T(8,128)(2,1)} custom-call(f32[512,1024]{1,0:T(8,128)} %get-tuple-element.48.first_ref, f32[512,1024]{1,0:T(8,128)} %get-tuple-element.50.second_ref, f32[1,512]{1,0:T(1,128)} %add.120.power_ref, f32[1,2048]{1,0:T(1,128)} %bitcast.179), custom_call_target="tpu_custom_call" | custom-call | flops 2097152 | bytes 6291456 | tf_op jit(solution)/shard_map/normalize/pallas_call | solution.py:453
  284.4 5.9 %all-to-all-done.1.even_ref = bf16[32,16,2048]{2,1,0:T(8,128)(2,1)S(1)} async-done(((bf16[32,16,2048]{2,1,0:T(8,128)(2,1)}), bf16[32,16,2048]{2,1,0:T(8,128)(2,1)S(1)}, u32[]{:S(2)}, u32[]{:S(2)}) %all-to-all-start.1) | async-done | bytes 2097184 | tf_op jit(solution)/shard_map/all_to_all | solution.py:638
  290.3 34.5 %all_to_all.15.odd_ref = bf16[32,16,2048]{2,1,0:T(8,128)(2,1)} all-to-all(bf16[32,16,2048]{2,1,0:T(8,128)(2,1)} %bitcast.160), channel_id=1, replica_groups=mesh['seq'=4,'chip'=16,'core'=2] {'chip','core'}, dimensions={0} | all-to-all | bytes 4194304 | tf_op jit(solution)/shard_map/all_to_all | solution.py:638
  324.8 5.6 %join_pages.1 = bf16[32,16,4096]{2,1,0:T(8,128)(2,1)} custom-call(s32[32]{0:T(128)} %bitcast.186, bf16[32,16,2048]{2,1,0:T(8,128)(2,1)} %copy-done.5, bf16[32,16,2048]{2,1,0:T(8,128)(2,1)} %all_to_all.15.odd_ref), custom_call_target="tpu_custom_call" | custom-call | tf_op jit(solution)/shard_map/join_pages/pallas_call | solution.py:152
  (158 shorter events, 47.7 us)
Async XLA Ops:
  6.5 88.9 %copy-start = (bf16[2048,64]{0,1:T(8,128)(2,1)S(1)}, bf16[2048,64]{0,1:T(8,128)(2,1)}, u32[]{:S(2)}) copy-start(bf16[2048,64]{0,1:T(8,128)(2,1)} %param.14) | copy-start | bytes 786436
  6.5 111.3 %all-gather.9.cloned.1.call-start = ((), (), s32[]{:S(2)}) async-start(), calls=%async_computation.4 | async-start | bytes 6389760 | tf_op jit(solution)/shard_map/all_gather | solution.py:558
  6.5 23.2 %collective-permute-start.3 = (bf16[5,8,2048]{2,1,0:T(8,128)(2,1)}, bf16[5,8,2048]{2,1,0:T(8,128)(2,1)S(1)}, u32[]{:S(2)}, u32[]{:S(2)}) collective-permute-start(bf16[5,8,2048]{2,1,0:T(8,128)(2,1)} %bitcast.187), channel_id=1, source_target_pairs={{2,6},{5,16},{8,26},{11,36},{14,46},{17,56},{20,66},{23,76},{43,86... | collective-permute-start | bytes 491528 | tf_op jit(solution)/shard_map/ppermute | solution.py:552
  7.3 22.3 %collective-permute-start.2 = (bf16[5,8,2048]{2,1,0:T(8,128)(2,1)}, bf16[5,8,2048]{2,1,0:T(8,128)(2,1)S(1)}, u32[]{:S(2)}, u32[]{:S(2)}) collective-permute-start(bf16[5,8,2048]{2,1,0:T(8,128)(2,1)} %bitcast.188), channel_id=1, source_target_pairs={{0,0},{76,1},{1,2},{52,3},{77,5},{26,6},{54,9},{27,10},{78,11},{4,... | collective-permute-start | bytes 491528 | tf_op jit(solution)/shard_map/ppermute | solution.py:552
  15.5 14.2 %collective-permute-start.1 = (bf16[5,8,2048]{2,1,0:T(8,128)(2,1)}, bf16[5,8,2048]{2,1,0:T(8,128)(2,1)S(1)}, u32[]{:S(2)}, u32[]{:S(2)}) collective-permute-start(bf16[5,8,2048]{2,1,0:T(8,128)(2,1)} %bitcast.189), channel_id=1, source_target_pairs={{51,1},{0,2},{77,3},{26,4},{1,6},{53,7},{27,8},{78,9},{54,11},{3,1... | collective-permute-start | bytes 491528 | tf_op jit(solution)/shard_map/ppermute | solution.py:552
  17.4 12.2 %collective-permute-start = (bf16[5,8,2048]{2,1,0:T(8,128)(2,1)}, bf16[5,8,2048]{2,1,0:T(8,128)(2,1)S(1)}, u32[]{:S(2)}, u32[]{:S(2)}) collective-permute-start(bf16[5,8,2048]{2,1,0:T(8,128)(2,1)} %bitcast.190), channel_id=1, source_target_pairs={{25,0},{77,1},{26,2},{51,3},{1,4},{52,5},{27,6},{78,7},{2,8},{53,9... | collective-permute-start | bytes 491528 | tf_op jit(solution)/shard_map/ppermute | solution.py:552
  29.7 0.9 copy-start.6
  36.6 7.7 %copy-start.9 = (f32[5120]{0:T(1024)S(1)}, f32[5120]{0:T(1024)}, u32[]{:S(2)}) copy-start(f32[5120]{0:T(1024)} %param.16) | copy-start | bytes 61444
  36.6 7.8 %copy-start.7 = (f32[4,5120]{1,0:T(4,128)S(1)}, f32[4,5120]{1,0:T(4,128)}, u32[]{:S(2)}) copy-start(f32[4,5120]{1,0:T(4,128)} %param.15) | copy-start | bytes 245764
  36.7 35.7 %copy-start.8 = (s32[1,2048]{1,0:T(1,128)S(1)}, s32[1,2048]{1,0:T(1,128)}, u32[]{:S(2)}) copy-start(s32[1,2048]{1,0:T(1,128)} %param.21) | copy-start | bytes 24580
  36.7 38.5 %copy-start.13 = (f32[64]{0:T(128)S(1)}, f32[64]{0:T(128)}, u32[]{:S(2)}) copy-start(f32[64]{0:T(128)} %param.17) | copy-start | bytes 772
  36.7 38.6 %copy-start.14 = (f32[64]{0:T(128)S(1)}, f32[64]{0:T(128)}, u32[]{:S(2)}) copy-start(f32[64]{0:T(128)} %param.18) | copy-start | bytes 772
  36.7 38.6 %copy-start.15 = (f32[64]{0:T(128)S(1)}, f32[64]{0:T(128)}, u32[]{:S(2)}) copy-start(f32[64]{0:T(128)} %param.19) | copy-start | bytes 772
  36.7 35.6 %all-to-all-start = ((bf16[32,16,2048]{2,1,0:T(8,128)(2,1)}), bf16[32,16,2048]{2,1,0:T(8,128)(2,1)S(1)}, u32[]{:S(2)}, u32[]{:S(2)}) async-start(bf16[32,16,2048]{2,1,0:T(8,128)(2,1)} %scatter_pages.1), calls=%async_computation | async-start | bytes 4194304 | tf_op jit(solution)/shard_map/all_to_all | solution.py:538
  44.2 143.5 %all-gather.7.cloned.1.call-start = ((), (), s32[]{:S(2)}) async-start(), calls=%async_computation.3 | async-start | bytes 4259840 | tf_op jit(solution)/shard_map/all_gather | solution.py:558
  72.3 16.1 %copy-start.4 = (bf16[32,16,2048]{2,1,0:T(8,128)(2,1)}, bf16[32,16,2048]{2,1,0:T(8,128)(2,1)S(1)}, u32[]{:S(2)}) copy-start(bf16[32,16,2048]{2,1,0:T(8,128)(2,1)S(1)} %all-to-all-done) | copy-start | bytes 6291460
  72.3 5.6 %collective-permute-start.6 = (s32[1,2048]{1,0:T(1,128)S(1)}, s32[1,2048]{1,0:T(1,128)S(1)}, u32[]{:S(2)}, u32[]{:S(2)}) collective-permute-start(s32[1,2048]{1,0:T(1,128)S(1)} %copy-done.8), channel_id=1, source_target_pairs={{0,1},{1,0},{2,3},{3,2},{4,5},{5,4},{6,7},{7,6},{8,9},{9,8},{10,11... | collective-permute-start | bytes 24584 | tf_op jit(solution)/shard_map/ppermute | solution.py:541
  77.8 153.9 %all-gather.11.cloned.1.call-start = ((), (), s32[]{:S(2)}) async-start(), calls=%async_computation.5 | async-start | bytes 2949120 | tf_op jit(solution)/shard_map/all_gather | solution.py:610
  77.8 10.6 %collective-permute-start.4 = (bf16[32,16,2048]{2,1,0:T(8,128)(2,1)S(1)}, bf16[32,16,2048]{2,1,0:T(8,128)(2,1)}, u32[]{:S(2)}, u32[]{:S(2)}) collective-permute-start(bf16[32,16,2048]{2,1,0:T(8,128)(2,1)S(1)} %all-to-all-done), channel_id=1, source_target_pairs={{0,1},{1,0},{2,3},{3,2},{4,5},{5,4},{6,7},{7,6},{8,9},{9,8},{10,11... | collective-permute-start | bytes 6291464 | tf_op jit(solution)/shard_map/ppermute | solution.py:540
  90.9 1.3 copy-start.3
  90.9 7.4 %copy-start.2 = (bf16[32,16,2048]{2,1,0:T(8,128)(2,1)}, bf16[32,16,2048]{2,1,0:T(8,128)(2,1)S(1)}, u32[]{:S(2)}) copy-start(bf16[32,16,2048]{2,1,0:T(8,128)(2,1)S(1)} %get-tuple-element.54) | copy-start | bytes 6291460
  92.3 13.6 %collective-permute-start.5 = (bf16[2,16,2048]{2,1,0:T(8,128)(2,1)S(1)}, bf16[2,16,2048]{2,1,0:T(8,128)(2,1)S(1)}, u32[]{:S(2)}, u32[]{:S(2)}) collective-permute-start(bf16[2,16,2048]{2,1,0:T(8,128)(2,1)S(1)} %pad_maximum_fusion), channel_id=1, source_target_pairs={{0,32},{32,64},{64,96},{1,33},{33,65},{65,97},{2,34},{34,66},{66,9... | collective-permute-start | bytes 393224 | tf_op jit(solution)/shard_map/ppermute | solution.py:548
  200.2 66.0 %all-gather.13.cloned.1.call-start = ((), (), s32[]{:S(2)}) async-start(), calls=%async_computation.6 | async-start | bytes 2949120 | tf_op jit(solution)/shard_map/all_gather | solution.py:610
  209.5 4.6 %copy-start.10 = (f32[4096]{0:T(1024)S(1)}, f32[4096]{0:T(1024)}, u32[]{:S(2)}) copy-start(f32[4096]{0:T(1024)} %param.20) | copy-start | bytes 49156
  236.9 5.3 %copy-start.11 = (f32[1,512]{1,0:T(1,128)S(1)}, f32[1,512]{1,0:T(1,128)}, u32[]{:S(2)}) copy-start(f32[1,512]{1,0:T(1,128)} %get-tuple-element.40) | copy-start | bytes 6148
  242.8 6.4 %collective-permute-start.7 = (f32[1,512]{1,0:T(1,128)S(1)}, f32[1,512]{1,0:T(1,128)S(1)}, u32[]{:S(2)}, u32[]{:S(2)}) collective-permute-start(f32[1,512]{1,0:T(1,128)S(1)} %add.116), channel_id=1, source_target_pairs={{0,1},{1,0},{2,3},{3,2},{4,5},{5,4},{6,7},{7,6},{8,9},{9,8},{10,11... | collective-permute-start | bytes 6152 | tf_op jit(solution)/shard_map/ppermute | solution.py:634
  254.6 35.8 %all-to-all-start.1 = ((bf16[32,16,2048]{2,1,0:T(8,128)(2,1)}), bf16[32,16,2048]{2,1,0:T(8,128)(2,1)S(1)}, u32[]{:S(2)}, u32[]{:S(2)}) async-start(bf16[32,16,2048]{2,1,0:T(8,128)(2,1)} %bitcast.159), calls=%async_computation.1 | async-start | bytes 4194304 | tf_op jit(solution)/shard_map/all_to_all | solution.py:638
  271.5 5.3 %copy-start.12 = (f32[1,512]{1,0:T(1,128)S(1)}, f32[1,512]{1,0:T(1,128)}, u32[]{:S(2)}) copy-start(f32[1,512]{1,0:T(1,128)} %get-tuple-element.52) | copy-start | bytes 6148
  277.4 1.7 collective-permute-start.8
  290.3 34.5 %copy-start.5 = (bf16[32,16,2048]{2,1,0:T(8,128)(2,1)}, bf16[32,16,2048]{2,1,0:T(8,128)(2,1)S(1)}, u32[]{:S(2)}) copy-start(bf16[32,16,2048]{2,1,0:T(8,128)(2,1)S(1)} %all-to-all-done.1.even_ref) | copy-start | bytes 6291460
  324.8 5.6 %copy-start.1 = (bf16[2048,64]{0,1:T(8,128)(2,1)S(1)}, bf16[2048,64]{0,1:T(8,128)(2,1)}, u32[]{:S(2)}) copy-start(bf16[2048,64]{0,1:T(8,128)(2,1)} %param.14) | copy-start | bytes 786436
Sparse Core Ops, SparseCore 0:
  32.9 84.8 all-gather.8
  120.7 67.0 all-gather.6
  200.3 31.3 all-gather.10
  233.2 32.9 all-gather.12

commit v4 on v2

--- a/solution.py
+++ b/solution.py
@@ -2,7 +2,6 @@
 
 import jax
 import jax.numpy as jnp
-import numpy as np
 from jax import lax
 from jax.experimental import pallas as pl
 from jax.experimental.pallas import tpu as pltpu
@@ -13,7 +12,6 @@
 KCONV = 4
 SPAN = 256
 INNER = 4096
-XBC = 5120
 D = 2048
 CORES = 2
 HEADS = 32
@@ -21,57 +19,6 @@
 HALF = 2048
 BC = GROUPS * STATE
 OWN = HALF + 2 * BC
-UNIT = 8
-PIECE = 5
-DEVICES = 128
-
-
-def unit_of(core, at):
-    x_units, bc_units = HALF // UNIT, BC // UNIT
-    if at < x_units:
-        return x_units * core + at
-    if at < x_units + bc_units:
-        return INNER // UNIT + bc_units * core + (at - x_units)
-    return (INNER + 2 * BC) // UNIT + bc_units * core + (at - x_units - bc_units)
-
-
-def weight_moves():
-    wanted = [
-        [divmod(unit_of(d % 2, PIECE * (d // 2) + k), PIECE) for k in range(PIECE)]
-        for d in range(DEVICES)
-    ]
-    edges = sorted({(source, d) for d in range(DEVICES) for source, _ in wanted[d]})
-    sent = [{} for _ in range(DEVICES)]
-    got = [{} for _ in range(DEVICES)]
-
-    def free(table):
-        return next(k for k in range(DEVICES) if k not in table)
-
-    for source, d in edges:
-        a, b = free(sent[source]), free(got[d])
-        if a != b:
-            path, at, tables, other, colour = [], d, got, sent, a
-            while colour in tables[at]:
-                nxt = tables[at][colour]
-                path.append((nxt, at, colour) if tables is got else (at, nxt, colour))
-                at, tables, other = nxt, other, tables
-                colour = b if colour == a else a
-            for s, t, colour in path:
-                del sent[s][colour]
-                del got[t][colour]
-            for s, t, colour in path:
-                sent[s][a + b - colour] = t
-                got[t][a + b - colour] = s
-        sent[source][a] = d
-        got[d][a] = source
-    rounds = 1 + max(k for table in got for k in table)
-    pairs = [[(got[d][k], d) for d in range(DEVICES) if k in got[d]] for k in range(rounds)]
-    picks = np.zeros((DEVICES, PIECE), np.int32)
-    for d in range(DEVICES):
-        where = {source: k for k, source in got[d].items()}
-        picks[d] = [where[source] * PIECE + slot for source, slot in wanted[d]]
-    return pairs, picks
-
 
 ALL = ("seq", "chip", "core")
 REQ = ("chip", "core")
@@ -101,47 +48,39 @@
     )(targets, pages)
 
 
-def pick_units(units, picks):
-    count = picks.shape[0]
-    return pl.pallas_call(
-        partial(move, places=lambda index: [(index[k], k) for k in range(count)]),
-        out_shape=jax.ShapeDtypeStruct((count,) + units.shape[1:], units.dtype),
-        in_specs=[pl.BlockSpec(memory_space=pltpu.SMEM), pl.BlockSpec(memory_space=pl.ANY)],
-        out_specs=pl.BlockSpec(memory_space=pltpu.VMEM),
-        scratch_shapes=[pltpu.SemaphoreType.DMA((count,))],
-        name="pick_units",
-    )(picks, units)
-
-
-def join_kernel(target_ref, own_ref, other_ref, out_ref, sems):
-    copies = []
-    for k in range(own_ref.shape[0]):
+def join_kernel(target_ref, even_ref, odd_ref, out_ref, sems):
+    count = even_ref.shape[0]
+
+    def copy(pages, page, k, half):
+        return pltpu.make_async_copy(
+            pages.at[page], out_ref.at[k, :, pl.ds(half * HALF, HALF)], sems.at[CORES * k + half]
+        )
+
+    for k in range(count):
         group = target_ref[k]
-        for part, (pages, page) in enumerate(((own_ref, group), (other_ref, group ^ 1))):
-            half = (group & 1) ^ part
-            copies.append(
-                pltpu.make_async_copy(
-                    pages.at[page],
-                    out_ref.at[k, :, pl.ds(pl.multiple_of(half * HALF, HALF), HALF)],
-                    sems.at[2 * k + part],
-                )
-            )
-    for copy in copies:
-        copy.start()
-    for copy in copies:
-        copy.wait()
-
-
-def join_pages(own, other, targets):
-    count, rows, width = own.shape
+        odd = group % CORES
+        for which, pages in enumerate((even_ref, odd_ref)):
+
+            @pl.when(odd == which)
+            def _():
+                for half in range(CORES):
+                    copy(pages, group - odd + half, k, half).start()
+
+    for k in range(count):
+        for half in range(CORES):
+            copy(even_ref, 0, k, half).wait()
+
+
+def join_pages(even, odd, targets):
+    count, rows, width = even.shape
     return pl.pallas_call(
         join_kernel,
-        out_shape=jax.ShapeDtypeStruct((count, rows, 2 * width), own.dtype),
+        out_shape=jax.ShapeDtypeStruct((count, rows, 2 * width), even.dtype),
         in_specs=[pl.BlockSpec(memory_space=pltpu.SMEM)] + [pl.BlockSpec(memory_space=pl.ANY)] * 2,
         out_specs=pl.BlockSpec(memory_space=pltpu.VMEM),
         scratch_shapes=[pltpu.SemaphoreType.DMA((2 * count,))],
         name="join_pages",
-    )(targets, own, other)
+    )(targets, even, odd)
 
 
 INTERPRET = False
@@ -159,19 +98,22 @@
 GROUP_COLS = PER_GROUP * HEAD_DIM
 
 
-def conv_kernel(halo_ref, tok_ref, weight_ref, taps_ref, bias_ref, mask_ref, out_ref, raw_ref):
+def conv_kernel(
+    core_ref, halo_ref, tok_ref, left_ref, right_ref, taps_ref, bias_ref, mask_ref, out_ref, raw_ref
+):
+    del core_ref
     masks = [mask_ref[:, k : k + 1] for k in range(KCONV - 1)]
-    for part in range(CONV_COLS // CHUNK):
-        cols = slice(part * CHUNK, (part + 1) * CHUNK)
-        weight = weight_ref[cols, :]
+    for part, weight_ref in enumerate((left_ref, right_ref)):
         dims = (((1,), (1,)), ((), ()))
         raw_ref[part, :HALO, :] = (
-            lax.dot_general(halo_ref[...], weight, dims, preferred_element_type=jnp.float32)
+            lax.dot_general(
+                halo_ref[...], weight_ref[...], dims, preferred_element_type=jnp.float32
+            )
             .astype(jnp.bfloat16)
             .astype(jnp.float32)
         )
         raw_ref[part, HALO:, :] = (
-            lax.dot_general(tok_ref[...], weight, dims, preferred_element_type=jnp.float32)
+            lax.dot_general(tok_ref[...], weight_ref[...], dims, preferred_element_type=jnp.float32)
             .astype(jnp.bfloat16)
             .astype(jnp.float32)
         )
@@ -187,27 +129,41 @@
         out_ref[:, cols] = (summed * (0.5 + 0.5 * jnp.tanh(0.5 * summed))).astype(jnp.bfloat16)
 
 
-def project_conv(halo, tokens, weight, taps, bias, masks):
+def project_conv(core, halo, tokens, weight, taps, bias, masks):
+    x_steps = HALF // CONV_COLS
+
+    def chunk(right):
+        def at(n, core_ref):
+            x_chunk = core_ref[0] * (HALF // CHUNK) + 2 * n + right
+            bc_chunk = INNER // CHUNK + right * CORES * BC // CHUNK + core_ref[0]
+            return jnp.where(n < x_steps, x_chunk, bc_chunk), 0
+
+        return pl.BlockSpec((CHUNK, D), at)
+
     return pl.pallas_call(
         conv_kernel,
-        grid=(OWN // CONV_COLS,),
+        grid_spec=pltpu.PrefetchScalarGridSpec(
+            num_scalar_prefetch=1,
+            grid=(OWN // CONV_COLS,),
+            in_specs=[
+                pl.BlockSpec((HALO, D), lambda n, core_ref: (0, 0)),
+                pl.BlockSpec((ROWS, D), lambda n, core_ref: (0, 0)),
+                chunk(0),
+                chunk(1),
+                pl.BlockSpec((KCONV, CONV_COLS), lambda n, core_ref: (0, n)),
+                pl.BlockSpec((1, CONV_COLS), lambda n, core_ref: (0, n)),
+                pl.BlockSpec((ROWS, KCONV - 1), lambda n, core_ref: (0, 0)),
+            ],
+            out_specs=pl.BlockSpec((ROWS, CONV_COLS), lambda n, core_ref: (0, n)),
+            scratch_shapes=[pltpu.VMEM((CONV_COLS // CHUNK, HALO + ROWS, CHUNK), jnp.float32)],
+        ),
         out_shape=jax.ShapeDtypeStruct((ROWS, OWN), jnp.bfloat16),
-        in_specs=[
-            pl.BlockSpec((HALO, D), lambda n: (0, 0)),
-            pl.BlockSpec((ROWS, D), lambda n: (0, 0)),
-            pl.BlockSpec((CONV_COLS, D), lambda n: (n, 0)),
-            pl.BlockSpec((KCONV, CONV_COLS), lambda n: (0, n)),
-            pl.BlockSpec((1, CONV_COLS), lambda n: (0, n)),
-            pl.BlockSpec((ROWS, KCONV - 1), lambda n: (0, 0)),
-        ],
-        out_specs=pl.BlockSpec((ROWS, CONV_COLS), lambda n: (0, n)),
-        scratch_shapes=[pltpu.VMEM((CONV_COLS // CHUNK, HALO + ROWS, CHUNK), jnp.float32)],
         cost_estimate=pl.CostEstimate(
             flops=2 * (ROWS + HALO) * D * OWN, transcendentals=ROWS * OWN, bytes_accessed=15 << 20
         ),
         name="project_conv",
         interpret=INTERPRET,
-    )(halo, tokens, weight, taps, bias, masks)
+    )(core, halo, tokens, weight, weight, taps, bias, masks)
 
 
 def spread_heads(values, first_head, columns):
@@ -317,7 +273,7 @@
                     )
                 out_ref[b * SPAN + part * half : b * SPAN + reach, cols] = jnp.where(
                     lane < HEAD_DIM, found[0], found[1]
-                )
+                ).astype(jnp.bfloat16)
 
 
 def mix_blocks(conv_out, decay, seg):
@@ -325,7 +281,7 @@
     return pl.pallas_call(
         mixing_kernel,
         grid=(GROUPS, steps),
-        out_shape=jax.ShapeDtypeStruct((ROWS, HALF), jnp.float32),
+        out_shape=jax.ShapeDtypeStruct((ROWS, HALF), jnp.bfloat16),
         in_specs=[
             pl.BlockSpec((ROWS, STEP_COLS), lambda g, p: (0, g * steps + p)),
             pl.BlockSpec((ROWS, STATE), lambda g, p: (0, HALF // STATE + g)),
@@ -369,11 +325,11 @@
             c_ref[rows, :], state.astype(jnp.bfloat16), preferred_element_type=jnp.float32
         )
         combined = (
-            y_ref[rows, :]
+            y_ref[rows, :].astype(jnp.float32)
             + readout * factor[rows]
             + row_ref[2:3, :] * x_ref[rows, :].astype(jnp.float32)
         )
-        out_ref[rows, :] = combined
+        out_ref[rows, :] = combined.astype(jnp.bfloat16)
         squared = combined * combined
         part_ref[rows, :] += squared[:, :128] + squared[:, 128:]
 
@@ -389,7 +345,7 @@
         readout_kernel,
         grid=(GROUPS, steps),
         out_shape=[
-            jax.ShapeDtypeStruct((ROWS, HALF), jnp.float32),
+            jax.ShapeDtypeStruct((ROWS, HALF), jnp.bfloat16),
             jax.ShapeDtypeStruct((1, ROWS), jnp.float32),
         ],
         in_specs=[
@@ -473,33 +429,32 @@
     tok_rows = stream_tokens.shape[0]
     page_rows = tok_rows // request_groups
     seq_at, core = lax.axis_index("seq"), lax.axis_index("core")
-    flat = (seq_at * lax.axis_size("chip") + lax.axis_index("chip")) * CORES + core
     swap = [(0, 1), (1, 0)]
     peers = lax.axis_size("seq")
     onward = [(i, i + 1) for i in range(peers - 1)]
-    onward_swap = [(2 * i + k, 2 * (i + 1) + 1 - k) for i in range(peers - 1) for k in range(2)]
 
     targets = page_target[0]
     pages = scatter_pages(stream_tokens.reshape(request_groups, page_rows, D), targets)
     own = lax.all_to_all(pages, REQ, split_axis=0, concat_axis=0, tiled=True)
+    own, own_ids = lax.optimization_barrier((own, segment_ids))
     other = lax.ppermute(own, "core", swap)
-    last_page = own[request_groups - 1]
-    own_halo = lax.ppermute(last_page, "seq", onward)
-    other_halo = lax.ppermute(last_page, ("seq", "core"), onward_swap)
-    other_ids = lax.ppermute(segment_ids, "core", swap)
-
-    pairs, picks = weight_moves()
-    piece = xbc_weight.T.reshape(PIECE, UNIT, D)
-    arrived = jnp.concatenate([lax.ppermute(piece, ALL, moves) for moves in pairs], axis=0)
-    units = pick_units(arrived, jnp.asarray(picks)[flat])
-    weight = lax.all_gather(units.reshape(PIECE * UNIT, D), ("seq", "chip"), axis=0, tiled=True)
+    other_ids = lax.ppermute(own_ids, "core", swap)
+
+    def in_order(first, second):
+        return [jnp.where(core == 0, first, second), jnp.where(core == 0, second, first)]
+
+    tokens = [blocks.reshape(tok_rows, D) for blocks in in_order(own, other)]
+    ids = in_order(own_ids, other_ids)
+    halos = lax.ppermute(jnp.stack([rows[tok_rows - HALO :] for rows in tokens]), "seq", onward)
+
+    weight = lax.all_gather(xbc_weight.T, ALL, axis=0, tiled=True)
 
     def columns(values):
         return jnp.concatenate(
             [
                 lax.dynamic_slice_in_dim(values, core * HALF, HALF, axis=-1),
                 lax.dynamic_slice_in_dim(values, INNER + core * BC, BC, axis=-1),
-                lax.dynamic_slice_in_dim(values, INNER + 2 * BC + core * BC, BC, axis=-1),
+                lax.dynamic_slice_in_dim(values, INNER + CORES * BC + core * BC, BC, axis=-1),
             ],
             axis=-1,
         )
@@ -513,7 +468,7 @@
 
     taps, bias = columns(conv_weight), columns(conv_bias[None, :])
     step_half, step_shift, rate = heads(step_weight), heads(step_bias), heads(decay_rate)
-    gain = lax.dynamic_slice_in_dim(norm_gain, core * HALF, HALF)
+    gain = lax.dynamic_slice_in_dim(norm_gain[None, :], core * HALF, HALF, axis=-1)
     ahead = (jnp.arange(peers) < seq_at).astype(jnp.float32)
     fixed_rows = jnp.concatenate(
         [
@@ -524,38 +479,44 @@
         axis=0,
     )
 
-    def states(tokens, halo, ids):
-        tokens = tokens.reshape(tok_rows, D)
-        ready = prepare(tokens, labels(ids), step_half, step_shift, rate)
-        rows = jnp.concatenate([over_columns(ready["passing"]), fixed_rows], axis=0)
-        conv_out = project_conv(halo, tokens, weight, taps, bias, ready["masks"])
-        gained, local = block_states(conv_out, ready["tail"], rows)
-        every = lax.all_gather(local, "seq")
-        return ready, rows, conv_out, gained, every
-
-    def outputs(ready, rows, conv_out, gained, every):
-        mixed = mix_blocks(conv_out, ready["decay"], ready["seg"])
-        combined, power = read_states(mixed, conv_out, gained, every, ready["factor"], rows)
-        return combined, power, lax.ppermute(power, "core", swap)
-
-    def sent_back(combined, power):
+    at_core = core.astype(jnp.int32)[None]
+    ready, rows, conv_out, gained, every = [], [], [], [], []
+    for q in range(CORES):
+        one = prepare(tokens[q], labels(ids[q]), step_half, step_shift, rate)
+        ready.append(one)
+        rows.append(jnp.concatenate([over_columns(one["passing"]), fixed_rows], axis=0))
+        conv_out.append(
+            project_conv(at_core, halos[q], tokens[q], weight, taps, bias, one["masks"])
+        )
+        after_first, local = block_states(conv_out[q], one["tail"], rows[q])
+        gained.append(after_first)
+        every.append(lax.all_gather(local, "seq"))
+
+    returned = []
+    for q in range(CORES):
+        decay = ready[q]["decay"]
+        if q > 0:
+            returned[0], decay = lax.optimization_barrier((returned[0], decay))
+        mixed = mix_blocks(conv_out[q], decay, ready[q]["seg"])
+        combined, power = read_states(
+            mixed, conv_out[q], gained[q], every[q], ready[q]["factor"], rows[q]
+        )
+        power = power + lax.ppermute(power, "core", swap)
         scale = lax.rsqrt(power[0] / INNER + 1e-05)
-        normed = (combined * scale[:, None] * gain[None, :]).astype(jnp.bfloat16)
-        return lax.all_to_all(
-            normed.reshape(request_groups, page_rows, HALF),
+        returned.append(
+            (combined.astype(jnp.float32) * scale[:, None] * gain).astype(jnp.bfloat16)
+        )
+    even, odd = [
+        lax.all_to_all(
+            rows_out.reshape(request_groups, page_rows, HALF),
             REQ,
             split_axis=0,
             concat_axis=0,
             tiled=True,
         )
-
-    own_states = states(own, own_halo, segment_ids)
-    other_states = states(other, other_halo, other_ids)
-    own_rows, own_power, own_swapped = outputs(*own_states)
-    other_rows, other_power, other_swapped = outputs(*other_states)
-    own_back = sent_back(own_rows, own_power + other_swapped)
-    other_back = sent_back(other_rows, other_power + own_swapped)
-    return join_pages(own_back, other_back, targets).reshape(tok_rows, INNER)
+        for rows_out in returned
+    ]
+    return join_pages(even, odd, targets).reshape(tok_rows, INNER)
 
 
 def solution(mesh):

time: 315 us -> 266 us (0.84)
  blocking collectives: 67.8 us -> 33.3 us
  waiting for transfers between devices: 83 us -> 68.9 us
  other arithmetic: 17.8 us -> 21.9 us
  Pallas kernels: 92.5 us -> 88.5 us
    all_to_all x2 -> x1, blocking collectives: 67.8 us -> 33.3 us  [per_device(): lax.all_to_all(rows_out.reshape(request_groups, page_rows, HALF), REQ, sp...]
    all_gather x3, waiting for transfers between devices: 49.3 us -> 34.9 us  [the longest x1 34.9 us: per_device(): weight = lax.all_gather(xbc_weight.T, ALL, axis=0, tiled=True)]
    ppermute x8 -> x4, waiting for transfers between devices: 12.2 us -> 1.67 us  [the longest x2 1.44 us: per_device(): power = power + lax.ppermute(power, 'core', swap)]
    ppermute x8 -> x4, starting transfers between devices: 13.5 us -> 6.16 us  [the longest x1 3.07 us: per_device(): lax.ppermute(jnp.stack([rows[tok_rows - HALO:] for rows in tokens]), 'seq...]
    all_to_all x1, waiting for transfers between devices: 21.4 us -> 28.1 us  [per_device(): own = lax.all_to_all(pages, REQ, split_axis=0, concat_axis=0, tiled=True)]
    all_to_all x0 -> x1, starting transfers between devices: none -> 6.32 us  [per_device(): lax.all_to_all(rows_out.reshape(request_groups, page_rows, HALF), REQ, sp...]
    all_to_all x0 -> x1, waiting for transfers between devices: none -> 3.54 us  [per_device(): lax.all_to_all(rows_out.reshape(request_groups, page_rows, HALF), REQ, sp...]
    pallas_call x3 -> x2, Pallas kernels: 33.9 us -> 32.2 us  [project_conv(): pl.pallas_call(conv_kernel, grid_spec=pltpu.PrefetchScalarGridSpec(num_sc...]
  transfers between devices with their start and end apart: 13 -> 10, of which waited for: 7 -> 6; matrix products, arithmetic and copies ran while one was open for 9% -> 14% of each run, Pallas kernels for 21% -> 24%
where the time goes in v4:
time: 266 us; the launch traced here: 265 us
  Pallas kernels  88.5 us (33%)
  waiting for transfers between devices  68.9 us (26%)
  blocking collectives  33.3 us (13%)
  starting transfers between devices  22.5 us (8%)
  other arithmetic  21.9 us (8%)
  between operations  13.5 us (5%)
  local copies, waits for them, and re-layouts  13.1 us (5%)
  matrix products  3.14 us (1%)
    all_gather x1, waiting for transfers between devices, per_device(): weight = lax.all_gather(xbc_weight.T, ALL, axis=0, tiled=True)  34.9 us
    all_to_all x1, blocking collectives, per_device(): lax.all_to_all(rows_out.reshape(request_groups, page_rows, HALF), REQ, sp...  33.3 us
    pallas_call x2, Pallas kernels, project_conv(): pl.pallas_call(conv_kernel, grid_spec=pltpu.PrefetchScalarGridSpec(num_sc...  32.2 us
    all_to_all x1, waiting for transfers between devices, per_device(): own = lax.all_to_all(pages, REQ, split_axis=0, concat_axis=0, tiled=True)  28.1 us
    pallas_call x2, Pallas kernels, read_states(): pl.pallas_call(readout_kernel, grid=(GROUPS, steps), out_shape=[jax.Shape...  20.1 us
    pallas_call x2, Pallas kernels, mix_blocks(): pl.pallas_call(mixing_kernel, grid=(GROUPS, steps), out_shape=jax.ShapeDt...  18.7 us
    all_to_all x1, starting transfers between devices, per_device(): own = lax.all_to_all(pages, REQ, split_axis=0, concat_axis=0, tiled=True)  9.73 us
    pallas_call x2, Pallas kernels, block_states(): pl.pallas_call(state_kernel, grid=(GROUPS,), out_shape=[jax.ShapeDtypeStr...  7.98 us
  transfers between devices with their start and end apart: 10, of which 6 were waited for; matrix products, arithmetic and copies ran while one was open for 14% of the time, Pallas kernels for 24%

profile of v4, /device:TPU:1, one launch (start us, length us, event | category | flops | bytes accessed | tf_op | source)
XLA Modules:
  0.0 264.9 jit_solution(5948703184774919702)
XLA Ops:
  7.3 3.8 %scatter_pages.1 = bf16[32,16,2048]{2,1,0:T(8,128)(2,1)} custom-call(s32[32]{0:T(128)} %bitcast.171, bf16[32,16,2048]{2,1,0:T(8,128)(2,1)} %bitcast.150), custom_call_target="tpu_custom_call" | custom-call | tf_op jit(solution)/shard_map/scatter_pages/pallas_call | solution.py:41
  11.2 9.7 %all-to-all-start = ((bf16[32,16,2048]{2,1,0:T(8,128)(2,1)}), bf16[32,16,2048]{2,1,0:T(8,128)(2,1)S(1)}, u32[]{:S(2)}, u32[]{:S(2)}) async-start(bf16[32,16,2048]{2,1,0:T(8,128)(2,1)} %scatter_pages.1), calls=%async_computation | async-start | bytes 4194304 | tf_op jit(solution)/shard_map/all_to_all | solution.py:438
  22.3 28.1 %all-to-all-done = bf16[32,16,2048]{2,1,0:T(8,128)(2,1)S(1)} async-done(((bf16[32,16,2048]{2,1,0:T(8,128)(2,1)}), bf16[32,16,2048]{2,1,0:T(8,128)(2,1)S(1)}, u32[]{:S(2)}, u32[]{:S(2)}) %all-to-all-start) | async-done | bytes 2097184 | tf_op jit(solution)/shard_map/all_to_all | solution.py:438
  50.4 2.3 collective-permute-start.2
  56.5 0.9 copy.76.mask_ref
  57.3 2.6 pad_add_fusion
  60.2 1.4 compare_reduce_fusion.1
  61.6 1.5 compare_reduce_fusion
  63.2 2.5 broadcast_select_fusion.1
  65.7 1.3 copy-done.3
  67.1 3.1 %collective-permute-start.1 = (bf16[2,16,2048]{2,1,0:T(8,128)(2,1)S(1)}, bf16[2,16,2048]{2,1,0:T(8,128)(2,1)S(1)}, u32[]{:S(2)}, u32[]{:S(2)}) collective-permute-start(bf16[2,16,2048]{2,1,0:T(8,128)(2,1)S(1)} %pad_maximum_fusion), channel_id=1, source_target_pairs={{0,32},{32,64},{64,96},{1,33},{33,65},{65,97},{2,34},{34,66},{66,9... | collective-permute-start | bytes 393224 | tf_op jit(solution)/shard_map/ppermute | solution.py:448
  71.0 1.2 reduce-window.16
  72.9 2.4 compare_select_fusion.3
  75.3 1.2 reduce-window.14
  78.0 0.9 copy.82
  79.6 34.9 %all-gather.6.cloned.1.call-done.left_ref.right_ref = bf16[5120,2048]{1,0:T(8,128)(2,1)} async-done(((bf16[40,2048]{1,0:T(8,128)(2,1)}), bf16[5120,2048]{1,0:T(8,128)(2,1)}) %all-gather.6.cloned.1.call-update) | async-done | bytes 20971536 | tf_op jit(solution)/shard_map/all_gather | solution.py:450
  114.4 16.1 %project_conv.2.x_ref.b_ref.c_ref = bf16[512,2560]{1,0:T(8,128)(2,1)} custom-call(s32[1]{0:T(128)} %bitcast.1.core_ref, bf16[16,2048]{1,0:T(8,128)(2,1)} %get-tuple-element.32.halo_ref, bf16[512,2048]{1,0:T(8,128)(2,1)} %bitcast.146, bf16[5120,2048]{1,0:T(8,128)(2,1)} %all-gather.6.cloned.1.call-done.left_ref.right_ref, ...), custom_call_target="tpu_custom_call" | custom-call | flops 5536481280 | bytes 15728640 | tf_op jit(solution)/shard_map/project_conv/pallas_call | solution.py:143
  130.5 4.0 %block_states.2 = (f32[128,2048]{1,0:T(8,128)}, bf16[144,2048]{1,0:T(8,128)(2,1)}) custom-call(bf16[512,2560]{1,0:T(8,128)(2,1)} %project_conv.2.x_ref.b_ref.c_ref, bf16[512,2560]{1,0:T(8,128)(2,1)} %project_conv.2.x_ref.b_ref.c_ref, f32[512,32]{1,0:T(8,128)} %bitcast.152, f32[8,2048]{1,0:T(8,128)} %get-tuple-element.50.row_ref), custom_call_target="tpu_custom_call" | custom-call | flops 268435456 | bytes 4194304 | tf_op jit(solution)/shard_map/block_states/pallas_call | solution.py:205
  134.9 0.9 copy.88.mask_ref
  136.8 16.1 %project_conv.3.x_ref.b_ref.c_ref = bf16[512,2560]{1,0:T(8,128)(2,1)} custom-call(s32[1]{0:T(128)} %bitcast.1.core_ref, bf16[16,2048]{1,0:T(8,128)(2,1)} %get-tuple-element.31.halo_ref, bf16[512,2048]{1,0:T(8,128)(2,1)} %bitcast.144, bf16[5120,2048]{1,0:T(8,128)(2,1)} %all-gather.6.cloned.1.call-done.left_ref.right_ref, ...), custom_call_target="tpu_custom_call" | custom-call | flops 5536481280 | bytes 15728640 | tf_op jit(solution)/shard_map/project_conv/pallas_call | solution.py:143
  153.0 4.0 %block_states.3 = (f32[128,2048]{1,0:T(8,128)}, bf16[144,2048]{1,0:T(8,128)(2,1)}) custom-call(bf16[512,2560]{1,0:T(8,128)(2,1)} %project_conv.3.x_ref.b_ref.c_ref, bf16[512,2560]{1,0:T(8,128)(2,1)} %project_conv.3.x_ref.b_ref.c_ref, f32[512,32]{1,0:T(8,128)} %bitcast.154, f32[8,2048]{1,0:T(8,128)} %get-tuple-element.49.row_ref), custom_call_target="tpu_custom_call" | custom-call | flops 268435456 | bytes 4194304 | tf_op jit(solution)/shard_map/block_states/pallas_call | solution.py:205
  159.4 9.3 %mix_blocks.2.y_ref = bf16[512,2048]{1,0:T(8,128)(2,1)} custom-call(bf16[512,2560]{1,0:T(8,128)(2,1)} %project_conv.2.x_ref.b_ref.c_ref, bf16[512,2560]{1,0:T(8,128)(2,1)} %project_conv.2.x_ref.b_ref.c_ref, bf16[512,2560]{1,0:T(8,128)(2,1)} %project_conv.2.x_ref.b_ref.c_ref, f32[8,8,512]{2,1,0:T(8,128)} %pad_maximum_fusion.1.decay_ref, ...), custom_call_target="tpu_custom_call" | custom-call | flops 536870912 | bytes 7340032 | tf_op jit(solution)/shard_map/mix_blocks/pallas_call | solution.py:281
  168.7 10.1 %read_states.2 = (bf16[512,2048]{1,0:T(8,128)(2,1)}, f32[1,512]{1,0:T(1,128)}) custom-call(bf16[512,2048]{1,0:T(8,128)(2,1)} %mix_blocks.2.y_ref, bf16[512,2560]{1,0:T(8,128)(2,1)} %project_conv.2.x_ref.b_ref.c_ref, bf16[512,2560]{1,0:T(8,128)(2,1)} %project_conv.2.x_ref.b_ref.c_ref, f32[128,2048]{1,0:T(8,128)} %get-tuple-element.19.gained_ref, ...), custom_call_target="tpu_custom_call" | custom-call | flops 268435456 | bytes 14680064 | tf_op jit(solution)/shard_map/read_states/pallas_call | solution.py:344
  180.9 3.5 %multiply_convert_fusion.1 = bf16[512,2048]{1,0:T(8,128)(2,1)} fusion(bf16[512,2048]{1,0:T(8,128)(2,1)} %get-tuple-element.21, f32[2048]{0:T(1024)S(1)} %dynamic-slice.15, f32[512]{0:T(512)S(1)} %bitcast.168), kind=kLoop, calls=%fused_computation.1 | loop fusion | flops 4194304 | bytes 4204544 | tf_op jit(solution)/shard_map/convert_element_type | solution.py:507
  184.4 6.3 %all-to-all-start.1 = ((bf16[32,16,2048]{2,1,0:T(8,128)(2,1)}), bf16[32,16,2048]{2,1,0:T(8,128)(2,1)}, u32[]{:S(2)}, u32[]{:S(2)}) async-start(bf16[32,16,2048]{2,1,0:T(8,128)(2,1)} %bitcast.25), calls=%async_computation.1 | async-start | bytes 4194304 | tf_op jit(solution)/shard_map/all_to_all | solution.py:510
  192.1 9.4 %mix_blocks.3.y_ref = bf16[512,2048]{1,0:T(8,128)(2,1)} custom-call(bf16[512,2560]{1,0:T(8,128)(2,1)} %project_conv.3.x_ref.b_ref.c_ref, bf16[512,2560]{1,0:T(8,128)(2,1)} %project_conv.3.x_ref.b_ref.c_ref, bf16[512,2560]{1,0:T(8,128)(2,1)} %project_conv.3.x_ref.b_ref.c_ref, f32[8,8,512]{2,1,0:T(8,128)} %pad_maximum_fusion.2.decay_ref, ...), custom_call_target="tpu_custom_call" | custom-call | flops 536870912 | bytes 7340032 | tf_op jit(solution)/shard_map/mix_blocks/pallas_call | solution.py:281
  201.5 10.0 %read_states.3 = (bf16[512,2048]{1,0:T(8,128)(2,1)}, f32[1,512]{1,0:T(1,128)}) custom-call(bf16[512,2048]{1,0:T(8,128)(2,1)} %mix_blocks.3.y_ref, bf16[512,2560]{1,0:T(8,128)(2,1)} %project_conv.3.x_ref.b_ref.c_ref, bf16[512,2560]{1,0:T(8,128)(2,1)} %project_conv.3.x_ref.b_ref.c_ref, f32[128,2048]{1,0:T(8,128)} %get-tuple-element.25.gained_ref, ...), custom_call_target="tpu_custom_call" | custom-call | flops 268435456 | bytes 14680064 | tf_op jit(solution)/shard_map/read_states/pallas_call | solution.py:344
  212.0 1.0 collective-permute-done.4
  213.8 2.1 multiply_convert_fusion
  215.9 3.5 %all-to-all-done.1.even_ref = bf16[32,16,2048]{2,1,0:T(8,128)(2,1)} async-done(((bf16[32,16,2048]{2,1,0:T(8,128)(2,1)}), bf16[32,16,2048]{2,1,0:T(8,128)(2,1)}, u32[]{:S(2)}, u32[]{:S(2)}) %all-to-all-start.1) | async-done | bytes 2097184 | tf_op jit(solution)/shard_map/all_to_all | solution.py:510
  219.4 33.3 %all_to_all.15.odd_ref = bf16[32,16,2048]{2,1,0:T(8,128)(2,1)} all-to-all(bf16[32,16,2048]{2,1,0:T(8,128)(2,1)S(1)} %bitcast.147), channel_id=1, replica_groups=mesh['seq'=4,'chip'=16,'core'=2] {'chip','core'}, dimensions={0} | all-to-all | bytes 4194304 | tf_op jit(solution)/shard_map/all_to_all | solution.py:510
  252.8 5.6 %join_pages.1 = bf16[32,16,4096]{2,1,0:T(8,128)(2,1)} custom-call(s32[32]{0:T(128)} %bitcast.172, bf16[32,16,2048]{2,1,0:T(8,128)(2,1)} %all-to-all-done.1.even_ref, bf16[32,16,2048]{2,1,0:T(8,128)(2,1)} %all_to_all.15.odd_ref), custom_call_target="tpu_custom_call" | custom-call | tf_op jit(solution)/shard_map/join_pages/pallas_call | solution.py:76
  (120 shorter events, 18.4 us)
Async XLA Ops:
  6.5 63.6 %copy-start = (bf16[2048,64]{0,1:T(8,128)(2,1)S(1)}, bf16[2048,64]{0,1:T(8,128)(2,1)}, u32[]{:S(2)}) copy-start(bf16[2048,64]{0,1:T(8,128)(2,1)} %param.13) | copy-start | bytes 786436
  6.5 107.9 %all-gather.6.cloned.1.call-start = ((), (), s32[]{:S(2)}) async-start(), calls=%async_computation.3 | async-start | bytes 21135360 | tf_op jit(solution)/shard_map/all_gather | solution.py:450
  11.1 9.9 %copy-start.7 = (f32[5120]{0:T(1024)S(1)}, f32[5120]{0:T(1024)}, u32[]{:S(2)}) copy-start(f32[5120]{0:T(1024)} %param.15) | copy-start | bytes 61444
  11.1 10.0 %copy-start.5 = (f32[4,5120]{1,0:T(4,128)S(1)}, f32[4,5120]{1,0:T(4,128)}, u32[]{:S(2)}) copy-start(f32[4,5120]{1,0:T(4,128)} %param.14) | copy-start | bytes 245764
  11.1 39.3 %copy-start.6 = (s32[1,2048]{1,0:T(1,128)S(1)}, s32[1,2048]{1,0:T(1,128)}, u32[]{:S(2)}) copy-start(s32[1,2048]{1,0:T(1,128)} %param.20) | copy-start | bytes 24580
  11.1 41.5 %copy-start.9 = (f32[64]{0:T(128)S(1)}, f32[64]{0:T(128)}, u32[]{:S(2)}) copy-start(f32[64]{0:T(128)} %param.16) | copy-start | bytes 772
  11.1 41.6 %copy-start.10 = (f32[64]{0:T(128)S(1)}, f32[64]{0:T(128)}, u32[]{:S(2)}) copy-start(f32[64]{0:T(128)} %param.17) | copy-start | bytes 772
  11.2 41.7 %copy-start.11 = (f32[64]{0:T(128)S(1)}, f32[64]{0:T(128)}, u32[]{:S(2)}) copy-start(f32[64]{0:T(128)} %param.18) | copy-start | bytes 772
  11.2 39.2 %all-to-all-start = ((bf16[32,16,2048]{2,1,0:T(8,128)(2,1)}), bf16[32,16,2048]{2,1,0:T(8,128)(2,1)S(1)}, u32[]{:S(2)}, u32[]{:S(2)}) async-start(bf16[32,16,2048]{2,1,0:T(8,128)(2,1)} %scatter_pages.1), calls=%async_computation | async-start | bytes 4194304 | tf_op jit(solution)/shard_map/all_to_all | solution.py:438
  20.9 147.8 %all-gather.8.cloned.1.call-start = ((), (), s32[]{:S(2)}) async-start(), calls=%async_computation.4 | async-start | bytes 2949120 | tf_op jit(solution)/shard_map/all_gather | solution.py:493
  50.4 12.8 %copy-start.4 = (bf16[32,16,2048]{2,1,0:T(8,128)(2,1)}, bf16[32,16,2048]{2,1,0:T(8,128)(2,1)S(1)}, u32[]{:S(2)}) copy-start(bf16[32,16,2048]{2,1,0:T(8,128)(2,1)S(1)} %all-to-all-done) | copy-start | bytes 6291460
  50.4 3.1 %collective-permute-start.2 = (s32[1,2048]{1,0:T(1,128)S(1)}, s32[1,2048]{1,0:T(1,128)S(1)}, u32[]{:S(2)}, u32[]{:S(2)}) collective-permute-start(s32[1,2048]{1,0:T(1,128)S(1)} %copy-done.6), channel_id=1, source_target_pairs={{0,1},{1,0},{2,3},{3,2},{4,5},{5,4},{6,7},{7,6},{8,9},{9,8},{10,11... | collective-permute-start | bytes 24584 | tf_op jit(solution)/shard_map/ppermute | solution.py:441
  53.2 10.0 %collective-permute-start = (bf16[32,16,2048]{2,1,0:T(8,128)(2,1)S(1)}, bf16[32,16,2048]{2,1,0:T(8,128)(2,1)}, u32[]{:S(2)}, u32[]{:S(2)}) collective-permute-start(bf16[32,16,2048]{2,1,0:T(8,128)(2,1)S(1)} %all-to-all-done), channel_id=1, source_target_pairs={{0,1},{1,0},{2,3},{3,2},{4,5},{5,4},{6,7},{7,6},{8,9},{9,8},{10,11... | collective-permute-start | bytes 6291464 | tf_op jit(solution)/shard_map/ppermute | solution.py:440
  65.7 1.4 copy-start.3
  65.7 9.5 %copy-start.2 = (bf16[32,16,2048]{2,1,0:T(8,128)(2,1)}, bf16[32,16,2048]{2,1,0:T(8,128)(2,1)S(1)}, u32[]{:S(2)}) copy-start(bf16[32,16,2048]{2,1,0:T(8,128)(2,1)S(1)} %get-tuple-element.30) | copy-start | bytes 6291460
  67.1 11.8 %collective-permute-start.1 = (bf16[2,16,2048]{2,1,0:T(8,128)(2,1)S(1)}, bf16[2,16,2048]{2,1,0:T(8,128)(2,1)S(1)}, u32[]{:S(2)}, u32[]{:S(2)}) collective-permute-start(bf16[2,16,2048]{2,1,0:T(8,128)(2,1)S(1)} %pad_maximum_fusion), channel_id=1, source_target_pairs={{0,32},{32,64},{64,96},{1,33},{33,65},{65,97},{2,34},{34,66},{66,9... | collective-permute-start | bytes 393224 | tf_op jit(solution)/shard_map/ppermute | solution.py:448
  134.5 67.0 %all-gather.10.cloned.1.call-start = ((), (), s32[]{:S(2)}) async-start(), calls=%async_computation.5 | async-start | bytes 2949120 | tf_op jit(solution)/shard_map/all_gather | solution.py:493
  153.0 4.0 %copy-start.8 = (f32[4096]{0:T(1024)S(1)}, f32[4096]{0:T(1024)}, u32[]{:S(2)}) copy-start(f32[4096]{0:T(1024)} %param.19) | copy-start | bytes 49156
  178.8 1.4 collective-permute-start.3
  184.4 35.1 %all-to-all-start.1 = ((bf16[32,16,2048]{2,1,0:T(8,128)(2,1)}), bf16[32,16,2048]{2,1,0:T(8,128)(2,1)}, u32[]{:S(2)}, u32[]{:S(2)}) async-start(bf16[32,16,2048]{2,1,0:T(8,128)(2,1)} %bitcast.25), calls=%async_computation.1 | async-start | bytes 4194304 | tf_op jit(solution)/shard_map/all_to_all | solution.py:510
  211.6 1.5 collective-permute-start.4
  252.8 5.6 %copy-start.1 = (bf16[2048,64]{0,1:T(8,128)(2,1)S(1)}, bf16[2048,64]{0,1:T(8,128)(2,1)}, u32[]{:S(2)}) copy-start(bf16[2048,64]{0,1:T(8,128)(2,1)} %param.13) | copy-start | bytes 786436
Sparse Core Ops, SparseCore 0:
  10.2 104.1 all-gather.5
  134.7 31.7 all-gather.7
  168.1 32.9 all-gather.9

commit v5 on v4

--- a/solution.py
+++ b/solution.py
@@ -48,13 +48,18 @@
     )(targets, pages)
 
 
-def join_kernel(target_ref, even_ref, odd_ref, out_ref, sems):
+def join_kernel(target_ref, even_ref, odd_ref, out_ref, held_ref, read_sems, write_sems):
     count = even_ref.shape[0]
 
-    def copy(pages, page, k, half):
+    def read(pages, page, k, half):
         return pltpu.make_async_copy(
-            pages.at[page], out_ref.at[k, :, pl.ds(half * HALF, HALF)], sems.at[CORES * k + half]
-        )
+            pages.at[page],
+            held_ref.at[k, :, pl.ds(half * HALF, HALF)],
+            read_sems.at[CORES * k + half],
+        )
+
+    def write(k):
+        return pltpu.make_async_copy(held_ref.at[k], out_ref.at[k], write_sems.at[k])
 
     for k in range(count):
         group = target_ref[k]
@@ -64,11 +69,14 @@
             @pl.when(odd == which)
             def _():
                 for half in range(CORES):
-                    copy(pages, group - odd + half, k, half).start()
+                    read(pages, group - odd + half, k, half).start()
 
     for k in range(count):
         for half in range(CORES):
-            copy(even_ref, 0, k, half).wait()
+            read(even_ref, 0, k, half).wait()
+        write(k).start()
+    for k in range(count):
+        write(k).wait()
 
 
 def join_pages(even, odd, targets):
@@ -77,8 +85,12 @@
         join_kernel,
         out_shape=jax.ShapeDtypeStruct((count, rows, 2 * width), even.dtype),
         in_specs=[pl.BlockSpec(memory_space=pltpu.SMEM)] + [pl.BlockSpec(memory_space=pl.ANY)] * 2,
-        out_specs=pl.BlockSpec(memory_space=pltpu.VMEM),
-        scratch_shapes=[pltpu.SemaphoreType.DMA((2 * count,))],
+        out_specs=pl.BlockSpec(memory_space=pl.ANY),
+        scratch_shapes=[
+            pltpu.VMEM((count, rows, 2 * width), even.dtype),
+            pltpu.SemaphoreType.DMA((CORES * count,)),
+            pltpu.SemaphoreType.DMA((count,)),
+        ],
         name="join_pages",
     )(targets, even, odd)
 
@@ -94,6 +106,7 @@
 SENT = STATE + 16
 HEADS_STEP = 4
 STEP_COLS = HEADS_STEP * HEAD_DIM
+READ_COLS = 512
 PER_GROUP = HEADS // GROUPS
 GROUP_COLS = PER_GROUP * HEAD_DIM
 
@@ -166,15 +179,16 @@
     )(core, halo, tokens, weight, weight, taps, bias, masks)
 
 
-def spread_heads(values, first_head, columns):
-    upper = values.astype(jnp.bfloat16)
-    lower = (values - upper.astype(jnp.float32)).astype(jnp.bfloat16)
-    head = lax.broadcasted_iota(jnp.int32, (HEADS, columns), 0)
-    column = lax.broadcasted_iota(jnp.int32, (HEADS, columns), 1)
+def spread_heads(terms, first_head, columns):
+    head = lax.broadcasted_iota(jnp.int32, (2 * HEADS, columns), 0) % HEADS
+    column = lax.broadcasted_iota(jnp.int32, (2 * HEADS, columns), 1)
     chosen = (head == first_head + column // HEAD_DIM).astype(jnp.bfloat16)
-    return jnp.dot(upper, chosen, preferred_element_type=jnp.float32) + jnp.dot(
-        lower, chosen, preferred_element_type=jnp.float32
-    )
+    return jnp.dot(terms, chosen, preferred_element_type=jnp.float32)
+
+
+def two_terms(values):
+    upper = lax.reduce_precision(values, 8, 7)
+    return jnp.concatenate([upper, values - upper], axis=-1).astype(jnp.bfloat16)
 
 
 def state_kernel(x_ref, b_ref, tail_ref, row_ref, gained_ref, local_ref):
@@ -212,7 +226,7 @@
         in_specs=[
             pl.BlockSpec((ROWS, GROUP_COLS), lambda g: (0, g)),
             pl.BlockSpec((ROWS, STATE), lambda g: (0, HALF // STATE + g)),
-            pl.BlockSpec((ROWS, HEADS), lambda g: (0, 0)),
+            pl.BlockSpec((ROWS, 2 * HEADS), lambda g: (0, 0)),
             pl.BlockSpec((8, GROUP_COLS), lambda g: (0, g)),
         ],
         out_specs=[
@@ -255,24 +269,25 @@
             for part in range(2):
                 reach = (part + 1) * half
                 rows = slice(part * half, reach)
-                found = []
+                mixing = []
                 for head in (2 * pair, 2 * pair + 1):
                     spread = (
                         down[rows, head : head + 1]
                         - decay[HEADS_STEP + head : HEADS_STEP + head + 1, :reach]
                     )
-                    mixing = (
-                        jnp.exp2(spread + bias_ref[b, rows, :reach]) * scores_ref[b, rows, :reach]
-                    ).astype(jnp.bfloat16)
-                    found.append(
-                        jnp.dot(
-                            mixing,
-                            x_ref[b * SPAN : b * SPAN + reach, cols],
-                            preferred_element_type=jnp.float32,
-                        )
+                    mixing.append(
+                        (
+                            jnp.exp2(spread + bias_ref[b, rows, :reach])
+                            * scores_ref[b, rows, :reach]
+                        ).astype(jnp.bfloat16)
                     )
+                found = jnp.dot(
+                    jnp.concatenate(mixing, axis=0),
+                    x_ref[b * SPAN : b * SPAN + reach, cols],
+                    preferred_element_type=jnp.float32,
+                )
                 out_ref[b * SPAN + part * half : b * SPAN + reach, cols] = jnp.where(
-                    lane < HEAD_DIM, found[0], found[1]
+                    lane < HEAD_DIM, found[:half], found[half:]
                 ).astype(jnp.bfloat16)
 
 
@@ -304,16 +319,16 @@
 def readout_kernel(
     y_ref, x_ref, c_ref, gained_ref, states_ref, factor_ref, row_ref, out_ref, power_ref, part_ref
 ):
-    steps = PER_GROUP // HEADS_STEP
+    steps = GROUP_COLS // READ_COLS
     at = pl.program_id(0) * steps + pl.program_id(1)
-    incoming = jnp.zeros((STATE, STEP_COLS), jnp.float32)
+    incoming = jnp.zeros((STATE, READ_COLS), jnp.float32)
     for peer in range(states_ref.shape[0] - 1):
         terms = states_ref[peer, STATE:, :].astype(jnp.float32)
         through = (terms[0:1] + terms[1:2]) + terms[2:3]
         after = through * incoming + states_ref[peer, :STATE, :].astype(jnp.float32)
         incoming = jnp.where(row_ref[4 + peer : 5 + peer, :] > 0.5, after, incoming)
     second = row_ref[0:1, :] * incoming + gained_ref[...]
-    factor = spread_heads(factor_ref[...], at * HEADS_STEP, STEP_COLS)
+    factor = spread_heads(factor_ref[...], at * (READ_COLS // HEAD_DIM), READ_COLS)
 
     @pl.when(at == 0)
     def _():
@@ -331,7 +346,10 @@
         )
         out_ref[rows, :] = combined.astype(jnp.bfloat16)
         squared = combined * combined
-        part_ref[rows, :] += squared[:, :128] + squared[:, 128:]
+        total = squared[:, :128]
+        for tile in range(1, READ_COLS // 128):
+            total = total + squared[:, tile * 128 : (tile + 1) * 128]
+        part_ref[rows, :] += total
 
     @pl.when(at == GROUPS * steps - 1)
     def _():
@@ -339,7 +357,7 @@
 
 
 def read_states(mixed, conv_out, gained, states, factor, rows):
-    steps = PER_GROUP // HEADS_STEP
+    steps = GROUP_COLS // READ_COLS
     peers = states.shape[0]
     return pl.pallas_call(
         readout_kernel,
@@ -349,16 +367,16 @@
             jax.ShapeDtypeStruct((1, ROWS), jnp.float32),
         ],
         in_specs=[
-            pl.BlockSpec((ROWS, STEP_COLS), lambda g, p: (0, g * steps + p)),
-            pl.BlockSpec((ROWS, STEP_COLS), lambda g, p: (0, g * steps + p)),
+            pl.BlockSpec((ROWS, READ_COLS), lambda g, p: (0, g * steps + p)),
+            pl.BlockSpec((ROWS, READ_COLS), lambda g, p: (0, g * steps + p)),
             pl.BlockSpec((ROWS, STATE), lambda g, p: (0, HALF // STATE + GROUPS + g)),
-            pl.BlockSpec((STATE, STEP_COLS), lambda g, p: (0, g * steps + p)),
-            pl.BlockSpec((peers, SENT, STEP_COLS), lambda g, p: (0, 0, g * steps + p)),
-            pl.BlockSpec((ROWS, HEADS), lambda g, p: (0, 0)),
-            pl.BlockSpec((8, STEP_COLS), lambda g, p: (0, g * steps + p)),
+            pl.BlockSpec((STATE, READ_COLS), lambda g, p: (0, g * steps + p)),
+            pl.BlockSpec((peers, SENT, READ_COLS), lambda g, p: (0, 0, g * steps + p)),
+            pl.BlockSpec((ROWS, 2 * HEADS), lambda g, p: (0, 0)),
+            pl.BlockSpec((8, READ_COLS), lambda g, p: (0, g * steps + p)),
         ],
         out_specs=[
-            pl.BlockSpec((ROWS, STEP_COLS), lambda g, p: (0, g * steps + p)),
+            pl.BlockSpec((ROWS, READ_COLS), lambda g, p: (0, g * steps + p)),
             pl.BlockSpec((1, ROWS), lambda g, p: (0, 0)),
         ],
         scratch_shapes=[pltpu.VMEM((ROWS, 128), jnp.float32)],
@@ -399,8 +417,8 @@
     )
     seg_rows = jnp.broadcast_to(seg.astype(jnp.float32)[None, :], (8, ROWS))
     return dict(
-        tail=tail.reshape(ROWS, HEADS),
-        factor=factor.reshape(ROWS, HEADS),
+        tail=two_terms(tail.reshape(ROWS, HEADS)),
+        factor=two_terms(factor.reshape(ROWS, HEADS)),
         passing=passing,
         masks=masks,
         decay=decay,
@@ -482,11 +500,17 @@
     at_core = core.astype(jnp.int32)[None]
     ready, rows, conv_out, gained, every = [], [], [], [], []
     for q in range(CORES):
-        one = prepare(tokens[q], labels(ids[q]), step_half, step_shift, rate)
-        ready.append(one)
-        rows.append(jnp.concatenate([over_columns(one["passing"]), fixed_rows], axis=0))
+        ready.append(prepare(tokens[q], labels(ids[q]), step_half, step_shift, rate))
+        rows.append(jnp.concatenate([over_columns(ready[q]["passing"]), fixed_rows], axis=0))
+    weight, ready, rows, halos, taps, bias, gain = lax.optimization_barrier(
+        (weight, ready, rows, [halos[q] for q in range(CORES)], taps, bias, gain)
+    )
+    for q in range(CORES):
+        one = ready[q]
         conv_out.append(
-            project_conv(at_core, halos[q], tokens[q], weight, taps, bias, one["masks"])
+            project_conv(
+                at_core, halos[q], tokens[q], weight, taps, bias, one["masks"]
+            )
         )
         after_first, local = block_states(conv_out[q], one["tail"], rows[q])
         gained.append(after_first)

time: 266 us -> 264 us (level)
  Pallas kernels: 88.5 us -> 82.2 us
  local copies, waits for them, and re-layouts: 13.1 us -> 7.41 us
  other arithmetic: 21.9 us -> 26.5 us
  waiting for transfers between devices: 68.9 us -> 73.1 us
    all_gather x2, waiting for transfers between devices: 0.01 us -> 7.14 us  [per_device(): every.append(lax.all_gather(local, 'seq'))]
    pallas_call x2, Pallas kernels: 20.1 us -> 15 us  [read_states(): pl.pallas_call(readout_kernel, grid=(GROUPS, steps), out_shape=[jax.Shape...]
    concatenate x1 -> x5, other arithmetic: 0.73 us -> 3.75 us  [the longest x4 3.01 us: two_terms(): jnp.concatenate([upper, values - upper], axis=-1).astype(jnp.bfloat16)]
    select_n x3 -> x0, other arithmetic: 2.73 us -> none  [the longest x1 2.53 us: in_order(): jnp.where(core == 0, first, second)]
  transfers between devices with their start and end apart: 10 -> 10, of which waited for: 6 -> 8; matrix products, arithmetic and copies ran while one was open for 14% -> 13% of each run, Pallas kernels for 24% -> 22%
where the time goes in v5:
time: 264 us; the launch traced here: 262 us
  Pallas kernels  82.2 us (31%)
  waiting for transfers between devices  73.1 us (28%)
  blocking collectives  33.3 us (13%)
  other arithmetic  26.5 us (10%)
  starting transfers between devices  24.7 us (9%)
  between operations  13.6 us (5%)
  local copies, waits for them, and re-layouts  7.41 us (3%)
    all_to_all x1, blocking collectives, per_device(): lax.all_to_all(rows_out.reshape(request_groups, page_rows, HALF), REQ, sp...  33.3 us
    all_gather x1, waiting for transfers between devices, per_device(): weight = lax.all_gather(xbc_weight.T, ALL, axis=0, tiled=True)  32.3 us
    pallas_call x2, Pallas kernels, project_conv(): pl.pallas_call(conv_kernel, grid_spec=pltpu.PrefetchScalarGridSpec(num_sc...  32.2 us
    all_to_all x1, waiting for transfers between devices, per_device(): own = lax.all_to_all(pages, REQ, split_axis=0, concat_axis=0, tiled=True)  28 us
    pallas_call x2, Pallas kernels, mix_blocks(): pl.pallas_call(mixing_kernel, grid=(GROUPS, steps), out_shape=jax.ShapeDt...  18.7 us
    pallas_call x2, Pallas kernels, read_states(): pl.pallas_call(readout_kernel, grid=(GROUPS, steps), out_shape=[jax.Shape...  15 us
    all_to_all x1, starting transfers between devices, per_device(): own = lax.all_to_all(pages, REQ, split_axis=0, concat_axis=0, tiled=True)  9.73 us
    all_to_all x1, starting transfers between devices, per_device(): lax.all_to_all(rows_out.reshape(request_groups, page_rows, HALF), REQ, sp...  7.42 us
  transfers between devices with their start and end apart: 10, of which 8 were waited for; matrix products, arithmetic and copies ran while one was open for 13% of the time, Pallas kernels for 22%

profile of v5, /device:TPU:1, one launch (start us, length us, event | category | flops | bytes accessed | tf_op | source)
XLA Modules:
  0.0 262.4 jit_solution(16945517337719753299)
XLA Ops:
  7.3 3.8 %scatter_pages.1 = bf16[32,16,2048]{2,1,0:T(8,128)(2,1)} custom-call(s32[32]{0:T(128)} %bitcast.177, bf16[32,16,2048]{2,1,0:T(8,128)(2,1)} %bitcast.160), custom_call_target="tpu_custom_call" | custom-call | tf_op jit(solution)/shard_map/scatter_pages/pallas_call | solution.py:41
  11.2 9.7 %all-to-all-start = ((bf16[32,16,2048]{2,1,0:T(8,128)(2,1)}), bf16[32,16,2048]{2,1,0:T(8,128)(2,1)S(1)}, u32[]{:S(2)}, u32[]{:S(2)}) async-start(bf16[32,16,2048]{2,1,0:T(8,128)(2,1)} %scatter_pages.1), calls=%async_computation | async-start | bytes 4194304 | tf_op jit(solution)/shard_map/all_to_all | solution.py:456
  22.3 28.0 %all-to-all-done = bf16[32,16,2048]{2,1,0:T(8,128)(2,1)S(1)} async-done(((bf16[32,16,2048]{2,1,0:T(8,128)(2,1)}), bf16[32,16,2048]{2,1,0:T(8,128)(2,1)S(1)}, u32[]{:S(2)}, u32[]{:S(2)}) %all-to-all-start) | async-done | bytes 2097184 | tf_op jit(solution)/shard_map/all_to_all | solution.py:456
  50.4 2.3 collective-permute-start.1
  58.3 2.5 pad_add_fusion.2
  61.1 1.4 compare_reduce_fusion
  62.4 1.5 compare_reduce_fusion.1
  64.1 2.5 broadcast_select_fusion
  66.7 3.1 %collective-permute-start.2 = (bf16[2,16,2048]{2,1,0:T(8,128)(2,1)S(1)}, bf16[2,16,2048]{2,1,0:T(8,128)(2,1)S(1)}, u32[]{:S(2)}, u32[]{:S(2)}) collective-permute-start(bf16[2,16,2048]{2,1,0:T(8,128)(2,1)S(1)} %pad_maximum_fusion.6), channel_id=1, source_target_pairs={{0,32},{32,64},{64,96},{1,33},{33,65},{65,97},{2,34},{34,66},{66,9... | collective-permute-start | bytes 393224 | tf_op jit(solution)/shard_map/ppermute | solution.py:466
  70.6 1.2 reduce-window.14
  73.3 1.2 reduce-window.16
  82.2 32.3 %all-gather.6.cloned.1.call-done.left_ref.right_ref = bf16[5120,2048]{1,0:T(8,128)(2,1)} async-done(((bf16[40,2048]{1,0:T(8,128)(2,1)}), bf16[5120,2048]{1,0:T(8,128)(2,1)}) %all-gather.6.cloned.1.call-update) | async-done | bytes 20971536 | tf_op jit(solution)/shard_map/all_gather | solution.py:468
  115.7 16.1 %project_conv.2.x_ref.b_ref.c_ref = bf16[512,2560]{1,0:T(8,128)(2,1)} custom-call(s32[1]{0:T(128)} %bitcast.1.core_ref, bf16[16,2048]{1,0:T(8,128)(2,1)} %get-tuple-element.37.halo_ref, bf16[512,2048]{1,0:T(8,128)(2,1)} %bitcast.156, bf16[5120,2048]{1,0:T(8,128)(2,1)} %all-gather.6.cloned.1.call-done.left_ref.right_ref, ...), custom_call_target="tpu_custom_call" | custom-call | flops 5536481280 | bytes 15728640 | tf_op jit(solution)/shard_map/project_conv/pallas_call | solution.py:156
  131.8 3.4 %block_states.2 = (f32[128,2048]{1,0:T(8,128)}, bf16[144,2048]{1,0:T(8,128)(2,1)}) custom-call(bf16[512,2560]{1,0:T(8,128)(2,1)} %project_conv.2.x_ref.b_ref.c_ref, bf16[512,2560]{1,0:T(8,128)(2,1)} %project_conv.2.x_ref.b_ref.c_ref, bf16[512,64]{1,0:T(8,128)(2,1)} %pad_maximum_fusion.2.tail_ref, f32[8,2048]{1,0:T(8,128)} %get-tuple-element.45.row_ref), custom_call_target="tpu_custom_call" | custom-call | flops 268435456 | bytes 4194304 | tf_op jit(solution)/shard_map/block_states/pallas_call | solution.py:219
  135.4 16.2 %project_conv.3.x_ref.b_ref.c_ref = bf16[512,2560]{1,0:T(8,128)(2,1)} custom-call(s32[1]{0:T(128)} %bitcast.1.core_ref, bf16[16,2048]{1,0:T(8,128)(2,1)} %get-tuple-element.54.halo_ref, bf16[512,2048]{1,0:T(8,128)(2,1)} %bitcast.154, bf16[5120,2048]{1,0:T(8,128)(2,1)} %all-gather.6.cloned.1.call-done.left_ref.right_ref, ...), custom_call_target="tpu_custom_call" | custom-call | flops 5536481280 | bytes 15728640 | tf_op jit(solution)/shard_map/project_conv/pallas_call | solution.py:156
  151.6 3.4 %block_states.3 = (f32[128,2048]{1,0:T(8,128)}, bf16[144,2048]{1,0:T(8,128)(2,1)}) custom-call(bf16[512,2560]{1,0:T(8,128)(2,1)} %project_conv.3.x_ref.b_ref.c_ref, bf16[512,2560]{1,0:T(8,128)(2,1)} %project_conv.3.x_ref.b_ref.c_ref, bf16[512,64]{1,0:T(8,128)(2,1)} %pad_maximum_fusion.5.tail_ref, f32[8,2048]{1,0:T(8,128)} %get-tuple-element.59.row_ref), custom_call_target="tpu_custom_call" | custom-call | flops 268435456 | bytes 4194304 | tf_op jit(solution)/shard_map/block_states/pallas_call | solution.py:219
  154.9 9.4 %mix_blocks.2.y_ref = bf16[512,2048]{1,0:T(8,128)(2,1)} custom-call(bf16[512,2560]{1,0:T(8,128)(2,1)} %project_conv.2.x_ref.b_ref.c_ref, bf16[512,2560]{1,0:T(8,128)(2,1)} %project_conv.2.x_ref.b_ref.c_ref, bf16[512,2560]{1,0:T(8,128)(2,1)} %project_conv.2.x_ref.b_ref.c_ref, f32[8,8,512]{2,1,0:T(8,128)} %pad_maximum_fusion.decay_ref, ...), custom_call_target="tpu_custom_call" | custom-call | flops 536870912 | bytes 7340032 | tf_op jit(solution)/shard_map/mix_blocks/pallas_call | solution.py:296
  164.3 2.8 %all-gather.8.cloned.1.call-done = bf16[576,2048]{1,0:T(8,128)(2,1)} async-done(((bf16[144,2048]{1,0:T(8,128)(2,1)}), bf16[576,2048]{1,0:T(8,128)(2,1)}) %all-gather.8.cloned.1.call-update) | async-done | bytes 2359312 | tf_op jit(solution)/shard_map/all_gather | solution.py:517
  167.1 7.5 %read_states.2 = (bf16[512,2048]{1,0:T(8,128)(2,1)}, f32[1,512]{1,0:T(1,128)}) custom-call(bf16[512,2048]{1,0:T(8,128)(2,1)} %mix_blocks.2.y_ref, bf16[512,2560]{1,0:T(8,128)(2,1)} %project_conv.2.x_ref.b_ref.c_ref, bf16[512,2560]{1,0:T(8,128)(2,1)} %project_conv.2.x_ref.b_ref.c_ref, f32[128,2048]{1,0:T(8,128)} %get-tuple-element.46.gained_ref, ...), custom_call_target="tpu_custom_call" | custom-call | flops 268435456 | bytes 14680064 | tf_op jit(solution)/shard_map/read_states/pallas_call | solution.py:362
  174.6 0.9 collective-permute-start.3
  175.5 0.9 collective-permute-done.3
  177.0 3.6 %multiply_convert_fusion.1 = bf16[512,2048]{1,0:T(8,128)(2,1)} fusion(bf16[512,2048]{1,0:T(8,128)(2,1)} %get-tuple-element.49, f32[2048]{0:T(1024)S(1)} %dynamic-slice.15, f32[512]{0:T(512)S(1)} %bitcast.174), kind=kLoop, calls=%fused_computation.1 | loop fusion | flops 4194304 | bytes 4204544 | tf_op jit(solution)/shard_map/convert_element_type | solution.py:531
  180.6 7.4 %all-to-all-start.1 = ((bf16[32,16,2048]{2,1,0:T(8,128)(2,1)}), bf16[32,16,2048]{2,1,0:T(8,128)(2,1)}, u32[]{:S(2)}, u32[]{:S(2)}) async-start(bf16[32,16,2048]{2,1,0:T(8,128)(2,1)} %bitcast.33), calls=%async_computation.1 | async-start | bytes 4194304 | tf_op jit(solution)/shard_map/all_to_all | solution.py:534
  188.0 9.4 %mix_blocks.3.y_ref = bf16[512,2048]{1,0:T(8,128)(2,1)} custom-call(bf16[512,2560]{1,0:T(8,128)(2,1)} %project_conv.3.x_ref.b_ref.c_ref, bf16[512,2560]{1,0:T(8,128)(2,1)} %project_conv.3.x_ref.b_ref.c_ref, bf16[512,2560]{1,0:T(8,128)(2,1)} %project_conv.3.x_ref.b_ref.c_ref, f32[8,8,512]{2,1,0:T(8,128)} %pad_maximum_fusion.3.decay_ref, ...), custom_call_target="tpu_custom_call" | custom-call | flops 536870912 | bytes 7340032 | tf_op jit(solution)/shard_map/mix_blocks/pallas_call | solution.py:296
  197.4 4.4 %all-gather.10.cloned.1.call-done = bf16[576,2048]{1,0:T(8,128)(2,1)} async-done(((bf16[144,2048]{1,0:T(8,128)(2,1)}), bf16[576,2048]{1,0:T(8,128)(2,1)}) %all-gather.10.cloned.1.call-update) | async-done | bytes 2359312 | tf_op jit(solution)/shard_map/all_gather | solution.py:517
  201.8 7.5 %read_states.3 = (bf16[512,2048]{1,0:T(8,128)(2,1)}, f32[1,512]{1,0:T(1,128)}) custom-call(bf16[512,2048]{1,0:T(8,128)(2,1)} %mix_blocks.3.y_ref, bf16[512,2560]{1,0:T(8,128)(2,1)} %project_conv.3.x_ref.b_ref.c_ref, bf16[512,2560]{1,0:T(8,128)(2,1)} %project_conv.3.x_ref.b_ref.c_ref, f32[128,2048]{1,0:T(8,128)} %get-tuple-element.60.gained_ref, ...), custom_call_target="tpu_custom_call" | custom-call | flops 268435456 | bytes 14680064 | tf_op jit(solution)/shard_map/read_states/pallas_call | solution.py:362
  209.3 0.9 collective-permute-start.4
  210.1 1.0 collective-permute-done.4
  211.8 2.1 multiply_convert_fusion
  213.9 2.8 %all-to-all-done.1.even_ref = bf16[32,16,2048]{2,1,0:T(8,128)(2,1)} async-done(((bf16[32,16,2048]{2,1,0:T(8,128)(2,1)}), bf16[32,16,2048]{2,1,0:T(8,128)(2,1)}, u32[]{:S(2)}, u32[]{:S(2)}) %all-to-all-start.1) | async-done | bytes 2097184 | tf_op jit(solution)/shard_map/all_to_all | solution.py:534
  216.8 33.3 %all_to_all.15.odd_ref = bf16[32,16,2048]{2,1,0:T(8,128)(2,1)} all-to-all(bf16[32,16,2048]{2,1,0:T(8,128)(2,1)S(1)} %bitcast.157), channel_id=1, replica_groups=mesh['seq'=4,'chip'=16,'core'=2] {'chip','core'}, dimensions={0} | all-to-all | bytes 4194304 | tf_op jit(solution)/shard_map/all_to_all | solution.py:534
  250.1 5.7 %join_pages.1 = bf16[32,16,4096]{2,1,0:T(8,128)(2,1)} custom-call(s32[32]{0:T(128)} %bitcast.178, bf16[32,16,2048]{2,1,0:T(8,128)(2,1)} %all-to-all-done.1.even_ref, bf16[32,16,2048]{2,1,0:T(8,128)(2,1)} %all_to_all.15.odd_ref), custom_call_target="tpu_custom_call" | custom-call | tf_op jit(solution)/shard_map/join_pages/pallas_call | solution.py:84
  (129 shorter events, 20.7 us)
Async XLA Ops:
  6.5 63.3 %copy-start = (bf16[2048,64]{0,1:T(8,128)(2,1)S(1)}, bf16[2048,64]{0,1:T(8,128)(2,1)}, u32[]{:S(2)}) copy-start(bf16[2048,64]{0,1:T(8,128)(2,1)} %param.13) | copy-start | bytes 786436
  6.5 107.9 %all-gather.6.cloned.1.call-start = ((), (), s32[]{:S(2)}) async-start(), calls=%async_computation.3 | async-start | bytes 21135360 | tf_op jit(solution)/shard_map/all_gather | solution.py:468
  11.1 9.9 %copy-start.7 = (f32[5120]{0:T(1024)S(1)}, f32[5120]{0:T(1024)}, u32[]{:S(2)}) copy-start(f32[5120]{0:T(1024)} %param.15) | copy-start | bytes 61444
  11.1 10.0 %copy-start.5 = (f32[4,5120]{1,0:T(4,128)S(1)}, f32[4,5120]{1,0:T(4,128)}, u32[]{:S(2)}) copy-start(f32[4,5120]{1,0:T(4,128)} %param.14) | copy-start | bytes 245764
  11.1 39.2 %copy-start.6 = (s32[1,2048]{1,0:T(1,128)S(1)}, s32[1,2048]{1,0:T(1,128)}, u32[]{:S(2)}) copy-start(s32[1,2048]{1,0:T(1,128)} %param.20) | copy-start | bytes 24580
  11.1 41.5 %copy-start.9 = (f32[64]{0:T(128)S(1)}, f32[64]{0:T(128)}, u32[]{:S(2)}) copy-start(f32[64]{0:T(128)} %param.16) | copy-start | bytes 772
  11.1 41.6 %copy-start.10 = (f32[64]{0:T(128)S(1)}, f32[64]{0:T(128)}, u32[]{:S(2)}) copy-start(f32[64]{0:T(128)} %param.17) | copy-start | bytes 772
  11.2 41.7 %copy-start.11 = (f32[64]{0:T(128)S(1)}, f32[64]{0:T(128)}, u32[]{:S(2)}) copy-start(f32[64]{0:T(128)} %param.18) | copy-start | bytes 772
  11.2 42.0 %copy-start.8 = (f32[4096]{0:T(1024)S(1)}, f32[4096]{0:T(1024)}, u32[]{:S(2)}) copy-start(f32[4096]{0:T(1024)} %param.19) | copy-start | bytes 49156
  11.2 39.2 %all-to-all-start = ((bf16[32,16,2048]{2,1,0:T(8,128)(2,1)}), bf16[32,16,2048]{2,1,0:T(8,128)(2,1)S(1)}, u32[]{:S(2)}, u32[]{:S(2)}) async-start(bf16[32,16,2048]{2,1,0:T(8,128)(2,1)} %scatter_pages.1), calls=%async_computation | async-start | bytes 4194304 | tf_op jit(solution)/shard_map/all_to_all | solution.py:456
  20.9 146.2 %all-gather.8.cloned.1.call-start = ((), (), s32[]{:S(2)}) async-start(), calls=%async_computation.4 | async-start | bytes 2949120 | tf_op jit(solution)/shard_map/all_gather | solution.py:517
  50.4 13.7 %copy-start.4 = (bf16[32,16,2048]{2,1,0:T(8,128)(2,1)}, bf16[32,16,2048]{2,1,0:T(8,128)(2,1)S(1)}, u32[]{:S(2)}) copy-start(bf16[32,16,2048]{2,1,0:T(8,128)(2,1)S(1)} %all-to-all-done) | copy-start | bytes 6291460
  50.4 3.1 %collective-permute-start.1 = (s32[1,2048]{1,0:T(1,128)S(1)}, s32[1,2048]{1,0:T(1,128)S(1)}, u32[]{:S(2)}, u32[]{:S(2)}) collective-permute-start(s32[1,2048]{1,0:T(1,128)S(1)} %copy-done.6), channel_id=1, source_target_pairs={{0,1},{1,0},{2,3},{3,2},{4,5},{5,4},{6,7},{7,6},{8,9},{9,8},{10,11... | collective-permute-start | bytes 24584 | tf_op jit(solution)/shard_map/ppermute | solution.py:459
  53.2 10.9 %collective-permute-start = (bf16[32,16,2048]{2,1,0:T(8,128)(2,1)S(1)}, bf16[32,16,2048]{2,1,0:T(8,128)(2,1)}, u32[]{:S(2)}, u32[]{:S(2)}) collective-permute-start(bf16[32,16,2048]{2,1,0:T(8,128)(2,1)S(1)} %all-to-all-done), channel_id=1, source_target_pairs={{0,1},{1,0},{2,3},{3,2},{4,5},{5,4},{6,7},{7,6},{8,9},{9,8},{10,11... | collective-permute-start | bytes 6291464 | tf_op jit(solution)/shard_map/ppermute | solution.py:458
  66.6 3.2 %copy-start.3 = (bf16[32,16,2048]{2,1,0:T(8,128)(2,1)}, bf16[32,16,2048]{2,1,0:T(8,128)(2,1)S(1)}, u32[]{:S(2)}) copy-start(bf16[32,16,2048]{2,1,0:T(8,128)(2,1)S(1)} %get-tuple-element.66) | copy-start | bytes 6291460
  66.6 5.9 %copy-start.2 = (bf16[32,16,2048]{2,1,0:T(8,128)(2,1)}, bf16[32,16,2048]{2,1,0:T(8,128)(2,1)S(1)}, u32[]{:S(2)}) copy-start(bf16[32,16,2048]{2,1,0:T(8,128)(2,1)S(1)} %get-tuple-element.65) | copy-start | bytes 6291460
  66.7 14.8 %collective-permute-start.2 = (bf16[2,16,2048]{2,1,0:T(8,128)(2,1)S(1)}, bf16[2,16,2048]{2,1,0:T(8,128)(2,1)S(1)}, u32[]{:S(2)}, u32[]{:S(2)}) collective-permute-start(bf16[2,16,2048]{2,1,0:T(8,128)(2,1)S(1)} %pad_maximum_fusion.6), channel_id=1, source_target_pairs={{0,32},{32,64},{64,96},{1,33},{33,65},{65,97},{2,34},{34,66},{66,9... | collective-permute-start | bytes 393224 | tf_op jit(solution)/shard_map/ppermute | solution.py:466
  135.2 66.6 %all-gather.10.cloned.1.call-start = ((), (), s32[]{:S(2)}) async-start(), calls=%async_computation.5 | async-start | bytes 2949120 | tf_op jit(solution)/shard_map/all_gather | solution.py:517
  174.6 1.7 collective-permute-start.3
  180.6 36.2 %all-to-all-start.1 = ((bf16[32,16,2048]{2,1,0:T(8,128)(2,1)}), bf16[32,16,2048]{2,1,0:T(8,128)(2,1)}, u32[]{:S(2)}, u32[]{:S(2)}) async-start(bf16[32,16,2048]{2,1,0:T(8,128)(2,1)} %bitcast.33), calls=%async_computation.1 | async-start | bytes 4194304 | tf_op jit(solution)/shard_map/all_to_all | solution.py:534
  209.3 1.9 collective-permute-start.4
  250.1 5.7 %copy-start.1 = (bf16[2048,64]{0,1:T(8,128)(2,1)S(1)}, bf16[2048,64]{0,1:T(8,128)(2,1)}, u32[]{:S(2)}) copy-start(bf16[2048,64]{0,1:T(8,128)(2,1)} %param.13) | copy-start | bytes 786436
Sparse Core Ops, SparseCore 0:
  10.2 104.2 all-gather.5
  135.3 31.7 all-gather.7
  168.8 32.9 all-gather.9

commit v6 on v5

--- a/solution.py
+++ b/solution.py
@@ -48,12 +48,13 @@
     )(targets, pages)
 
 
-def join_kernel(target_ref, even_ref, odd_ref, out_ref, held_ref, read_sems, write_sems):
-    count = even_ref.shape[0]
-
-    def read(pages, page, k, half):
+def join_kernel(target_ref, pages_ref, *rest, which):
+    out_ref, held_ref, read_sems, write_sems = rest[-4:]
+    count = pages_ref.shape[0]
+
+    def read(page, k, half):
         return pltpu.make_async_copy(
-            pages.at[page],
+            pages_ref.at[page],
             held_ref.at[k, :, pl.ds(half * HALF, HALF)],
             read_sems.at[CORES * k + half],
         )
@@ -61,38 +62,44 @@
     def write(k):
         return pltpu.make_async_copy(held_ref.at[k], out_ref.at[k], write_sems.at[k])
 
-    for k in range(count):
-        group = target_ref[k]
-        odd = group % CORES
-        for which, pages in enumerate((even_ref, odd_ref)):
-
-            @pl.when(odd == which)
-            def _():
-                for half in range(CORES):
-                    read(pages, group - odd + half, k, half).start()
-
-    for k in range(count):
+    def for_mine(act):
+        for k in range(count):
+            pl.when(target_ref[k] % CORES == which)(partial(act, k))
+
+    def start_reads(k):
         for half in range(CORES):
-            read(even_ref, 0, k, half).wait()
+            read(target_ref[k] - which + half, k, half).start()
+
+    def pass_on(k):
+        for half in range(CORES):
+            read(0, k, half).wait()
         write(k).start()
-    for k in range(count):
+
+    def finish(k):
         write(k).wait()
 
-
-def join_pages(even, odd, targets):
-    count, rows, width = even.shape
+    for_mine(start_reads)
+    for_mine(pass_on)
+    for_mine(finish)
+
+
+def join_pages(which, pages, targets, behind=()):
+    count, rows, width = pages.shape
     return pl.pallas_call(
-        join_kernel,
-        out_shape=jax.ShapeDtypeStruct((count, rows, 2 * width), even.dtype),
-        in_specs=[pl.BlockSpec(memory_space=pltpu.SMEM)] + [pl.BlockSpec(memory_space=pl.ANY)] * 2,
+        partial(join_kernel, which=which),
+        out_shape=jax.ShapeDtypeStruct((count, rows, CORES * width), pages.dtype),
+        in_specs=[pl.BlockSpec(memory_space=pltpu.SMEM)]
+        + [pl.BlockSpec(memory_space=pl.ANY)] * (1 + len(behind)),
         out_specs=pl.BlockSpec(memory_space=pl.ANY),
+        input_output_aliases={2: 0} if behind else {},
         scratch_shapes=[
-            pltpu.VMEM((count, rows, 2 * width), even.dtype),
+            pltpu.VMEM((count, rows, CORES * width), pages.dtype),
             pltpu.SemaphoreType.DMA((CORES * count,)),
             pltpu.SemaphoreType.DMA((count,)),
         ],
+        cost_estimate=pl.CostEstimate(flops=0, transcendentals=0, bytes_accessed=4 << 20),
         name="join_pages",
-    )(targets, even, odd)
+    )(targets, pages, *behind)
 
 
 INTERPRET = False
@@ -540,7 +547,8 @@
         )
         for rows_out in returned
     ]
-    return join_pages(even, odd, targets).reshape(tok_rows, INNER)
+    joined = join_pages(0, even, targets)
+    return join_pages(1, odd, targets, (joined,)).reshape(tok_rows, INNER)
 
 
 def solution(mesh):

time: 264 us -> 264 us (level)
  blocking collectives: 33.3 us -> 0 us
  waiting for transfers between devices: 73.1 us -> 94.3 us
  starting transfers between devices: 24.7 us -> 30.7 us
  local copies, waits for them, and re-layouts: 7.41 us -> 10.1 us
    all_to_all x1 -> x0, blocking collectives: 33.3 us -> none  [per_device(): lax.all_to_all(rows_out.reshape(request_groups, page_rows, HALF), REQ, sp...]
    all_to_all x1 -> x2, waiting for transfers between devices: 2.83 us -> 26.1 us  [per_device(): lax.all_to_all(rows_out.reshape(request_groups, page_rows, HALF), REQ, sp...]
    all_to_all x1 -> x2, starting transfers between devices: 7.42 us -> 13.5 us  [per_device(): lax.all_to_all(rows_out.reshape(request_groups, page_rows, HALF), REQ, sp...]
    pallas_call x1 -> x2, Pallas kernels: 5.67 us -> 7.69 us  [join_pages(): pl.pallas_call(partial(join_kernel, which=which), out_shape=jax.ShapeDtyp...]
  transfers between devices with their start and end apart: 10 -> 11, of which waited for: 8 -> 9; matrix products, arithmetic and copies ran while one was open for 13% -> 14% of each run, Pallas kernels for 22% -> 23%
where the time goes in v6:
time: 264 us; the launch traced here: 262 us
  waiting for transfers between devices  94.3 us (36%)
  Pallas kernels  84.3 us (32%)
  starting transfers between devices  30.7 us (12%)
  other arithmetic  27.9 us (11%)
  between operations  13.6 us (5%)
  local copies, waits for them, and re-layouts  10.1 us (4%)
    pallas_call x2, Pallas kernels, project_conv(): pl.pallas_call(conv_kernel, grid_spec=pltpu.PrefetchScalarGridSpec(num_sc...  32.2 us
    all_gather x1, waiting for transfers between devices, per_device(): weight = lax.all_gather(xbc_weight.T, ALL, axis=0, tiled=True)  30 us
    all_to_all x1, waiting for transfers between devices, per_device(): own = lax.all_to_all(pages, REQ, split_axis=0, concat_axis=0, tiled=True)  28 us
    all_to_all x2, waiting for transfers between devices, per_device(): lax.all_to_all(rows_out.reshape(request_groups, page_rows, HALF), REQ, sp...  26.1 us
    pallas_call x2, Pallas kernels, mix_blocks(): pl.pallas_call(mixing_kernel, grid=(GROUPS, steps), out_shape=jax.ShapeDt...  18.7 us
    pallas_call x2, Pallas kernels, read_states(): pl.pallas_call(readout_kernel, grid=(GROUPS, steps), out_shape=[jax.Shape...  15 us
    all_to_all x2, starting transfers between devices, per_device(): lax.all_to_all(rows_out.reshape(request_groups, page_rows, HALF), REQ, sp...  13.5 us
    all_to_all x1, starting transfers between devices, per_device(): own = lax.all_to_all(pages, REQ, split_axis=0, concat_axis=0, tiled=True)  9.73 us
  transfers between devices with their start and end apart: 11, of which 9 were waited for; matrix products, arithmetic and copies ran while one was open for 14% of the time, Pallas kernels for 23%

profile of v6, /device:TPU:1, one launch (start us, length us, event | category | flops | bytes accessed | tf_op | source)
XLA Modules:
  0.0 262.4 jit_solution(2823301082978470157)
XLA Ops:
  7.3 3.8 %scatter_pages.1 = bf16[32,16,2048]{2,1,0:T(8,128)(2,1)} custom-call(s32[32]{0:T(128)} %bitcast.176, bf16[32,16,2048]{2,1,0:T(8,128)(2,1)} %bitcast.161), custom_call_target="tpu_custom_call" | custom-call | tf_op jit(solution)/shard_map/scatter_pages/pallas_call | solution.py:41
  11.2 9.7 %all-to-all-start = ((bf16[32,16,2048]{2,1,0:T(8,128)(2,1)}), bf16[32,16,2048]{2,1,0:T(8,128)(2,1)S(1)}, u32[]{:S(2)}, u32[]{:S(2)}) async-start(bf16[32,16,2048]{2,1,0:T(8,128)(2,1)} %scatter_pages.1), calls=%async_computation | async-start | bytes 4194304 | tf_op jit(solution)/shard_map/all_to_all | solution.py:463
  22.3 28.0 %all-to-all-done = bf16[32,16,2048]{2,1,0:T(8,128)(2,1)S(1)} async-done(((bf16[32,16,2048]{2,1,0:T(8,128)(2,1)}), bf16[32,16,2048]{2,1,0:T(8,128)(2,1)S(1)}, u32[]{:S(2)}, u32[]{:S(2)}) %all-to-all-start) | async-done | bytes 2097184 | tf_op jit(solution)/shard_map/all_to_all | solution.py:463
  50.4 2.3 collective-permute-start.1
  58.4 2.5 pad_add_fusion.2
  61.1 1.3 compare_reduce_fusion
  62.5 1.5 compare_reduce_fusion.1
  64.1 2.6 broadcast_select_fusion
  66.7 1.3 copy-done.3
  68.8 1.2 reduce-window.14
  71.7 1.2 reduce-window.16
  74.4 3.1 %collective-permute-start.2 = (bf16[2,16,2048]{2,1,0:T(8,128)(2,1)S(1)}, bf16[2,16,2048]{2,1,0:T(8,128)(2,1)S(1)}, u32[]{:S(2)}, u32[]{:S(2)}) collective-permute-start(bf16[2,16,2048]{2,1,0:T(8,128)(2,1)S(1)} %pad_maximum_fusion.6), channel_id=1, source_target_pairs={{0,32},{32,64},{64,96},{1,33},{33,65},{65,97},{2,34},{34,66},{66,9... | collective-permute-start | bytes 393224 | tf_op jit(solution)/shard_map/ppermute | solution.py:473
  83.5 30.0 %all-gather.6.cloned.1.call-done.left_ref.right_ref = bf16[5120,2048]{1,0:T(8,128)(2,1)} async-done(((bf16[40,2048]{1,0:T(8,128)(2,1)}), bf16[5120,2048]{1,0:T(8,128)(2,1)}) %all-gather.6.cloned.1.call-update) | async-done | bytes 20971536 | tf_op jit(solution)/shard_map/all_gather | solution.py:475
  114.7 16.1 %project_conv.3.x_ref.b_ref.c_ref = bf16[512,2560]{1,0:T(8,128)(2,1)} custom-call(s32[1]{0:T(128)} %bitcast.1.core_ref, bf16[16,2048]{1,0:T(8,128)(2,1)} %get-tuple-element.42.halo_ref, bf16[512,2048]{1,0:T(8,128)(2,1)} %bitcast.156, bf16[5120,2048]{1,0:T(8,128)(2,1)} %all-gather.6.cloned.1.call-done.left_ref.right_ref, ...), custom_call_target="tpu_custom_call" | custom-call | flops 5536481280 | bytes 15728640 | tf_op jit(solution)/shard_map/project_conv/pallas_call | solution.py:163
  130.9 3.4 %block_states.2 = (f32[128,2048]{1,0:T(8,128)}, bf16[144,2048]{1,0:T(8,128)(2,1)}) custom-call(bf16[512,2560]{1,0:T(8,128)(2,1)} %project_conv.3.x_ref.b_ref.c_ref, bf16[512,2560]{1,0:T(8,128)(2,1)} %project_conv.3.x_ref.b_ref.c_ref, bf16[512,64]{1,0:T(8,128)(2,1)} %pad_maximum_fusion.2.tail_ref, f32[8,2048]{1,0:T(8,128)} %get-tuple-element.47.row_ref), custom_call_target="tpu_custom_call" | custom-call | flops 268435456 | bytes 4194304 | tf_op jit(solution)/shard_map/block_states/pallas_call | solution.py:226
  134.5 16.1 %project_conv.2.x_ref.b_ref.c_ref = bf16[512,2560]{1,0:T(8,128)(2,1)} custom-call(s32[1]{0:T(128)} %bitcast.1.core_ref, bf16[16,2048]{1,0:T(8,128)(2,1)} %get-tuple-element.37.halo_ref, bf16[512,2048]{1,0:T(8,128)(2,1)} %bitcast.154, bf16[5120,2048]{1,0:T(8,128)(2,1)} %all-gather.6.cloned.1.call-done.left_ref.right_ref, ...), custom_call_target="tpu_custom_call" | custom-call | flops 5536481280 | bytes 15728640 | tf_op jit(solution)/shard_map/project_conv/pallas_call | solution.py:163
  150.6 3.4 %block_states.3 = (f32[128,2048]{1,0:T(8,128)}, bf16[144,2048]{1,0:T(8,128)(2,1)}) custom-call(bf16[512,2560]{1,0:T(8,128)(2,1)} %project_conv.2.x_ref.b_ref.c_ref, bf16[512,2560]{1,0:T(8,128)(2,1)} %project_conv.2.x_ref.b_ref.c_ref, bf16[512,64]{1,0:T(8,128)(2,1)} %pad_maximum_fusion.5.tail_ref, f32[8,2048]{1,0:T(8,128)} %get-tuple-element.58.row_ref), custom_call_target="tpu_custom_call" | custom-call | flops 268435456 | bytes 4194304 | tf_op jit(solution)/shard_map/block_states/pallas_call | solution.py:226
  154.0 9.4 %mix_blocks.2.y_ref = bf16[512,2048]{1,0:T(8,128)(2,1)} custom-call(bf16[512,2560]{1,0:T(8,128)(2,1)} %project_conv.3.x_ref.b_ref.c_ref, bf16[512,2560]{1,0:T(8,128)(2,1)} %project_conv.3.x_ref.b_ref.c_ref, bf16[512,2560]{1,0:T(8,128)(2,1)} %project_conv.3.x_ref.b_ref.c_ref, f32[8,8,512]{2,1,0:T(8,128)} %pad_maximum_fusion.decay_ref, ...), custom_call_target="tpu_custom_call" | custom-call | flops 536870912 | bytes 7340032 | tf_op jit(solution)/shard_map/mix_blocks/pallas_call | solution.py:303
  163.4 2.8 %all-gather.8.cloned.1.call-done = bf16[576,2048]{1,0:T(8,128)(2,1)} async-done(((bf16[144,2048]{1,0:T(8,128)(2,1)}), bf16[576,2048]{1,0:T(8,128)(2,1)}) %all-gather.8.cloned.1.call-update) | async-done | bytes 2359312 | tf_op jit(solution)/shard_map/all_gather | solution.py:524
  166.2 7.5 %read_states.2 = (bf16[512,2048]{1,0:T(8,128)(2,1)}, f32[1,512]{1,0:T(1,128)}) custom-call(bf16[512,2048]{1,0:T(8,128)(2,1)} %mix_blocks.2.y_ref, bf16[512,2560]{1,0:T(8,128)(2,1)} %project_conv.3.x_ref.b_ref.c_ref, bf16[512,2560]{1,0:T(8,128)(2,1)} %project_conv.3.x_ref.b_ref.c_ref, f32[128,2048]{1,0:T(8,128)} %get-tuple-element.48.gained_ref, ...), custom_call_target="tpu_custom_call" | custom-call | flops 268435456 | bytes 14680064 | tf_op jit(solution)/shard_map/read_states/pallas_call | solution.py:369
  176.2 3.6 %multiply_convert_fusion.1 = bf16[512,2048]{1,0:T(8,128)(2,1)} fusion(bf16[512,2048]{1,0:T(8,128)(2,1)} %get-tuple-element.51, f32[2048]{0:T(1024)S(1)} %dynamic-slice.15, f32[512]{0:T(512)S(1)} %bitcast.175), kind=kLoop, calls=%fused_computation.1 | loop fusion | flops 4194304 | bytes 4204544 | tf_op jit(solution)/shard_map/convert_element_type | solution.py:538
  179.8 7.4 %all-to-all-start.2 = ((bf16[32,16,2048]{2,1,0:T(8,128)(2,1)}), bf16[32,16,2048]{2,1,0:T(8,128)(2,1)S(1)}, u32[]{:S(2)}, u32[]{:S(2)}) async-start(bf16[32,16,2048]{2,1,0:T(8,128)(2,1)} %bitcast.157), calls=%async_computation.2 | async-start | bytes 4194304 | tf_op jit(solution)/shard_map/all_to_all | solution.py:541
  187.2 9.4 %mix_blocks.3.y_ref = bf16[512,2048]{1,0:T(8,128)(2,1)} custom-call(bf16[512,2560]{1,0:T(8,128)(2,1)} %project_conv.2.x_ref.b_ref.c_ref, bf16[512,2560]{1,0:T(8,128)(2,1)} %project_conv.2.x_ref.b_ref.c_ref, bf16[512,2560]{1,0:T(8,128)(2,1)} %project_conv.2.x_ref.b_ref.c_ref, f32[8,8,512]{2,1,0:T(8,128)} %pad_maximum_fusion.3.decay_ref, ...), custom_call_target="tpu_custom_call" | custom-call | flops 536870912 | bytes 7340032 | tf_op jit(solution)/shard_map/mix_blocks/pallas_call | solution.py:303
  196.6 4.3 %all-gather.10.cloned.1.call-done = bf16[576,2048]{1,0:T(8,128)(2,1)} async-done(((bf16[144,2048]{1,0:T(8,128)(2,1)}), bf16[576,2048]{1,0:T(8,128)(2,1)}) %all-gather.10.cloned.1.call-update) | async-done | bytes 2359312 | tf_op jit(solution)/shard_map/all_gather | solution.py:524
  200.9 7.5 %read_states.3 = (bf16[512,2048]{1,0:T(8,128)(2,1)}, f32[1,512]{1,0:T(1,128)}) custom-call(bf16[512,2048]{1,0:T(8,128)(2,1)} %mix_blocks.3.y_ref, bf16[512,2560]{1,0:T(8,128)(2,1)} %project_conv.2.x_ref.b_ref.c_ref, bf16[512,2560]{1,0:T(8,128)(2,1)} %project_conv.2.x_ref.b_ref.c_ref, f32[128,2048]{1,0:T(8,128)} %get-tuple-element.59.gained_ref, ...), custom_call_target="tpu_custom_call" | custom-call | flops 268435456 | bytes 14680064 | tf_op jit(solution)/shard_map/read_states/pallas_call | solution.py:369
  211.0 3.5 %multiply_convert_fusion = bf16[512,2048]{1,0:T(8,128)(2,1)} fusion(bf16[512,2048]{1,0:T(8,128)(2,1)} %get-tuple-element.62, f32[512]{0:T(512)S(1)} %bitcast.174, f32[2048]{0:T(1024)S(1)} %dynamic-slice.15), kind=kLoop, calls=%fused_computation | loop fusion | flops 4194304 | bytes 4204544 | tf_op jit(solution)/shard_map/convert_element_type | solution.py:538
  214.5 1.3 all-to-all-done.2.pages_ref
  215.8 1.3 copy-done.4
  217.1 6.1 %all-to-all-start.1 = ((bf16[32,16,2048]{2,1,0:T(8,128)(2,1)}), bf16[32,16,2048]{2,1,0:T(8,128)(2,1)}, u32[]{:S(2)}, u32[]{:S(2)}) async-start(bf16[32,16,2048]{2,1,0:T(8,128)(2,1)} %bitcast.158), calls=%async_computation.1 | async-start | bytes 4194304 | tf_op jit(solution)/shard_map/all_to_all | solution.py:541
  223.3 3.8 %join_pages.2.rest_0_ = bf16[32,16,4096]{2,1,0:T(8,128)(2,1)} custom-call(s32[32]{0:T(128)} %bitcast.177, bf16[32,16,2048]{2,1,0:T(8,128)(2,1)} %copy-done.4), custom_call_target="tpu_custom_call" | custom-call | bytes 4194304 | tf_op jit(solution)/shard_map/join_pages/pallas_call | solution.py:88
  227.1 24.8 %all-to-all-done.1.pages_ref = bf16[32,16,2048]{2,1,0:T(8,128)(2,1)} async-done(((bf16[32,16,2048]{2,1,0:T(8,128)(2,1)}), bf16[32,16,2048]{2,1,0:T(8,128)(2,1)}, u32[]{:S(2)}, u32[]{:S(2)}) %all-to-all-start.1) | async-done | bytes 2097184 | tf_op jit(solution)/shard_map/all_to_all | solution.py:541
  251.9 3.9 %join_pages.3 = bf16[32,16,4096]{2,1,0:T(8,128)(2,1)} custom-call(s32[32]{0:T(128)} %bitcast.178, bf16[32,16,2048]{2,1,0:T(8,128)(2,1)} %all-to-all-done.1.pages_ref, bf16[32,16,4096]{2,1,0:T(8,128)(2,1)} %join_pages.2.rest_0_), custom_call_target="tpu_custom_call", output_to_operand_aliasing={{}: (2, {})} | custom-call | bytes 4194304 | tf_op jit(solution)/shard_map/join_pages/pallas_call | solution.py:88
  (133 shorter events, 24.6 us)
Async XLA Ops:
  6.5 61.5 %copy-start = (bf16[2048,64]{0,1:T(8,128)(2,1)S(1)}, bf16[2048,64]{0,1:T(8,128)(2,1)}, u32[]{:S(2)}) copy-start(bf16[2048,64]{0,1:T(8,128)(2,1)} %param.13) | copy-start | bytes 786436
  6.5 107.0 %all-gather.6.cloned.1.call-start = ((), (), s32[]{:S(2)}) async-start(), calls=%async_computation.3 | async-start | bytes 21135360 | tf_op jit(solution)/shard_map/all_gather | solution.py:475
  11.1 9.9 %copy-start.8 = (f32[5120]{0:T(1024)S(1)}, f32[5120]{0:T(1024)}, u32[]{:S(2)}) copy-start(f32[5120]{0:T(1024)} %param.15) | copy-start | bytes 61444
  11.1 10.0 %copy-start.6 = (f32[4,5120]{1,0:T(4,128)S(1)}, f32[4,5120]{1,0:T(4,128)}, u32[]{:S(2)}) copy-start(f32[4,5120]{1,0:T(4,128)} %param.14) | copy-start | bytes 245764
  11.1 39.2 %copy-start.7 = (s32[1,2048]{1,0:T(1,128)S(1)}, s32[1,2048]{1,0:T(1,128)}, u32[]{:S(2)}) copy-start(s32[1,2048]{1,0:T(1,128)} %param.20) | copy-start | bytes 24580
  11.1 41.5 %copy-start.10 = (f32[64]{0:T(128)S(1)}, f32[64]{0:T(128)}, u32[]{:S(2)}) copy-start(f32[64]{0:T(128)} %param.17) | copy-start | bytes 772
  11.1 41.6 %copy-start.11 = (f32[64]{0:T(128)S(1)}, f32[64]{0:T(128)}, u32[]{:S(2)}) copy-start(f32[64]{0:T(128)} %param.16) | copy-start | bytes 772
  11.2 41.7 %copy-start.12 = (f32[64]{0:T(128)S(1)}, f32[64]{0:T(128)}, u32[]{:S(2)}) copy-start(f32[64]{0:T(128)} %param.18) | copy-start | bytes 772
  11.2 42.0 %copy-start.9 = (f32[4096]{0:T(1024)S(1)}, f32[4096]{0:T(1024)}, u32[]{:S(2)}) copy-start(f32[4096]{0:T(1024)} %param.19) | copy-start | bytes 49156
  11.2 39.2 %all-to-all-start = ((bf16[32,16,2048]{2,1,0:T(8,128)(2,1)}), bf16[32,16,2048]{2,1,0:T(8,128)(2,1)S(1)}, u32[]{:S(2)}, u32[]{:S(2)}) async-start(bf16[32,16,2048]{2,1,0:T(8,128)(2,1)} %scatter_pages.1), calls=%async_computation | async-start | bytes 4194304 | tf_op jit(solution)/shard_map/all_to_all | solution.py:463
  20.9 145.3 %all-gather.8.cloned.1.call-start = ((), (), s32[]{:S(2)}) async-start(), calls=%async_computation.4 | async-start | bytes 2949120 | tf_op jit(solution)/shard_map/all_gather | solution.py:524
  50.4 13.8 %copy-start.5 = (bf16[32,16,2048]{2,1,0:T(8,128)(2,1)}, bf16[32,16,2048]{2,1,0:T(8,128)(2,1)S(1)}, u32[]{:S(2)}) copy-start(bf16[32,16,2048]{2,1,0:T(8,128)(2,1)S(1)} %all-to-all-done) | copy-start | bytes 6291460
  50.4 3.1 %collective-permute-start.1 = (s32[1,2048]{1,0:T(1,128)S(1)}, s32[1,2048]{1,0:T(1,128)S(1)}, u32[]{:S(2)}, u32[]{:S(2)}) collective-permute-start(s32[1,2048]{1,0:T(1,128)S(1)} %copy-done.7), channel_id=1, source_target_pairs={{0,1},{1,0},{2,3},{3,2},{4,5},{5,4},{6,7},{7,6},{8,9},{9,8},{10,11... | collective-permute-start | bytes 24584 | tf_op jit(solution)/shard_map/ppermute | solution.py:466
  53.2 10.9 %collective-permute-start = (bf16[32,16,2048]{2,1,0:T(8,128)(2,1)S(1)}, bf16[32,16,2048]{2,1,0:T(8,128)(2,1)}, u32[]{:S(2)}, u32[]{:S(2)}) collective-permute-start(bf16[32,16,2048]{2,1,0:T(8,128)(2,1)S(1)} %all-to-all-done), channel_id=1, source_target_pairs={{0,1},{1,0},{2,3},{3,2},{4,5},{5,4},{6,7},{7,6},{8,9},{9,8},{10,11... | collective-permute-start | bytes 6291464 | tf_op jit(solution)/shard_map/ppermute | solution.py:465
  66.7 1.3 copy-start.3
  66.7 4.2 %copy-start.2 = (bf16[32,16,2048]{2,1,0:T(8,128)(2,1)}, bf16[32,16,2048]{2,1,0:T(8,128)(2,1)S(1)}, u32[]{:S(2)}) copy-start(bf16[32,16,2048]{2,1,0:T(8,128)(2,1)S(1)} %get-tuple-element.65) | copy-start | bytes 6291460
  74.4 8.4 %collective-permute-start.2 = (bf16[2,16,2048]{2,1,0:T(8,128)(2,1)S(1)}, bf16[2,16,2048]{2,1,0:T(8,128)(2,1)S(1)}, u32[]{:S(2)}, u32[]{:S(2)}) collective-permute-start(bf16[2,16,2048]{2,1,0:T(8,128)(2,1)S(1)} %pad_maximum_fusion.6), channel_id=1, source_target_pairs={{0,32},{32,64},{64,96},{1,33},{33,65},{65,97},{2,34},{34,66},{66,9... | collective-permute-start | bytes 393224 | tf_op jit(solution)/shard_map/ppermute | solution.py:473
  134.3 66.6 %all-gather.10.cloned.1.call-start = ((), (), s32[]{:S(2)}) async-start(), calls=%async_computation.5 | async-start | bytes 2949120 | tf_op jit(solution)/shard_map/all_gather | solution.py:524
  173.7 1.9 collective-permute-start.3
  179.8 36.0 %all-to-all-start.2 = ((bf16[32,16,2048]{2,1,0:T(8,128)(2,1)}), bf16[32,16,2048]{2,1,0:T(8,128)(2,1)S(1)}, u32[]{:S(2)}, u32[]{:S(2)}) async-start(bf16[32,16,2048]{2,1,0:T(8,128)(2,1)} %bitcast.157), calls=%async_computation.2 | async-start | bytes 4194304 | tf_op jit(solution)/shard_map/all_to_all | solution.py:541
  208.4 1.9 collective-permute-start.4
  215.8 1.3 copy-start.4
  217.1 34.8 %all-to-all-start.1 = ((bf16[32,16,2048]{2,1,0:T(8,128)(2,1)}), bf16[32,16,2048]{2,1,0:T(8,128)(2,1)}, u32[]{:S(2)}, u32[]{:S(2)}) async-start(bf16[32,16,2048]{2,1,0:T(8,128)(2,1)} %bitcast.158), calls=%async_computation.1 | async-start | bytes 4194304 | tf_op jit(solution)/shard_map/all_to_all | solution.py:541
  251.9 3.9 %copy-start.1 = (bf16[2048,64]{0,1:T(8,128)(2,1)S(1)}, bf16[2048,64]{0,1:T(8,128)(2,1)}, u32[]{:S(2)}) copy-start(bf16[2048,64]{0,1:T(8,128)(2,1)} %param.13) | copy-start | bytes 786436
Sparse Core Ops, SparseCore 0:
  10.2 103.2 all-gather.5
  134.4 31.7 all-gather.7
  167.9 32.9 all-gather.9
